TPU v7x, 32 devices: a whole 2x2x4 slice. The times are simulated.
32 devices in a mesh: prow: 4 (over y, x), pcol: 8 (over z, core).
Axes of the slice: x: 2, y: 2, z: 4, core: 2. Of those that a mesh axis runs over, the one named last changes fastest.
Arguments:
- l_panel: bfloat16 [8192, 1024], P('prow', 'pcol'), may hold values from -0.29882812 to 0.29882812
- inverse_tile: bfloat16 [8192, 8192], P('prow', 'pcol'), may hold values from -0.5 to 0.5
- unit_inverse: bfloat16 [8, 128, 128], P('pcol'), may hold values from -0.5 to 0.5
- pivot_inverse: float32 [8, 128, 128], P('pcol'), may hold values from -6 to 6
- listed: int32 [8, 64], replicated, may hold values 0 or 1
Outputs:
- offdiag: float32 [1024, 8192], P('pcol', 'prow')
- diag: float32 [8, 128, 128], P('pcol')
All inputs are finite; a program needn't handle non-finite values.
Results may differ from a plain program's by a relative error of at most 0.015.
Values may be sent and summed in bfloat16 or wider, within the bound.
No kernel may reach another device: no remote copies, remote signals or barrier semaphores. Data moves between devices by JAX's collectives and lax.ppermute only.
A program may use at most 64 MiB of HBM per device.

v0:
```python
import functools

import jax
import jax.numpy as jnp
from jax import lax
from jax.experimental import pallas as pl
from jax.experimental.pallas import tpu as pltpu
from jax.sharding import PartitionSpec as P


BLOCK = 128
AXES = ("prow", "pcol")
VMEM = pltpu.VMEM
SMEM = pltpu.SMEM
LIMIT = 24 << 20


def whole(space):
    return pl.BlockSpec(memory_space=space)


def normalize_kernel(n, listed, panel, unit, *refs):
    outs, rows, right, keeps, came = refs[: n + 1], refs[n + 1], refs[n + 2], refs[n + 3], refs[n + 4]
    p = lax.axis_index("prow")
    c = lax.axis_index("pcol")
    part = panel.shape[0] // n
    per = part // BLOCK
    order = list(range(1, n)) + [0]
    first = [
        pltpu.make_async_copy(unit.at[0], right, came.at[n]),
        pltpu.make_async_copy(listed.at[pl.ds(c, 1), :], keeps, came.at[n + 1]),
    ]
    take = [
        pltpu.make_async_copy(panel.at[pl.ds(pl.multiple_of((p ^ a) * part, part), part), :], rows.at[a], came.at[a])
        for a in order
    ]
    for x in first + take:
        x.start()
    for x in first:
        x.wait()
    for a, x in zip(order, take):
        x.wait()
        g = p ^ a
        t = jnp.dot(rows[a], right[...], preferred_element_type=jnp.float32)
        for b in range(per):
            keep = keeps[0, (p * n + g) * per + b].astype(jnp.float32)
            v = (t[b * BLOCK : (b + 1) * BLOCK] * keep).astype(jnp.bfloat16)
            outs[a][b * BLOCK : (b + 1) * BLOCK, :] = v
            outs[n][pl.ds(pl.multiple_of(g * part + b * BLOCK, BLOCK), BLOCK), :] = v


def normalize(n, listed, panel, unit):
    rows, width = panel.shape
    part = rows // n
    shapes = [jax.ShapeDtypeStruct((part, width), jnp.bfloat16)] * n + [jax.ShapeDtypeStruct((rows, width), jnp.bfloat16)]
    return pl.pallas_call(
        functools.partial(normalize_kernel, n),
        out_shape=shapes,
        in_specs=[whole(pltpu.HBM)] * 3,
        out_specs=[whole(VMEM)] * (n + 1),
        scratch_shapes=[
            pltpu.VMEM((n, part, width), jnp.bfloat16),
            pltpu.VMEM((width, width), jnp.bfloat16),
            pltpu.SMEM((1, listed.shape[1]), jnp.int32),
            pltpu.SemaphoreType.DMA((n + 2,)),
        ],
        compiler_params=pltpu.CompilerParams(vmem_limit_bytes=LIMIT),
        cost_estimate=pl.CostEstimate(flops=2 * rows * width * width, bytes_accessed=6 * rows * width, transcendentals=0),
        name="normalize",
    )(listed, panel, unit)


def load_kernel(tile, out, came):
    x = pltpu.make_async_copy(tile, out, came)
    x.start()
    x.wait()


def load(tile):
    return pl.pallas_call(
        load_kernel,
        out_shape=jax.ShapeDtypeStruct(tile.shape, tile.dtype),
        in_specs=[whole(pltpu.HBM)],
        out_specs=whole(VMEM),
        scratch_shapes=[pltpu.SemaphoreType.DMA],
        compiler_params=pltpu.CompilerParams(vmem_limit_bytes=LIMIT),
        cost_estimate=pl.CostEstimate(flops=0, bytes_accessed=4 * tile.shape[0] * tile.shape[1], transcendentals=0),
        name="load",
    )(tile)


def pick_kernel(n, q, *refs):
    ins, outs, held, came, left = refs[:n], refs[n : 2 * n], refs[2 * n], refs[2 * n + 1], refs[2 * n + 2]
    p = lax.axis_index("prow")
    z = lax.axis_index("pcol") // q
    take = [pltpu.make_async_copy(ins[a], held.at[a], came.at[a]) for a in range(n)]
    for x in take:
        x.start()
    for x in take:
        x.wait()
    give = [pltpu.make_async_copy(held.at[p ^ z ^ m], outs[m], left.at[m]) for m in reversed(range(n))]
    for x in give:
        x.start()
    for x in give:
        x.wait()


def pick(n, q, pieces):
    shape = pieces[0].shape
    return pl.pallas_call(
        functools.partial(pick_kernel, n, q),
        out_shape=[jax.ShapeDtypeStruct(shape, jnp.bfloat16)] * n,
        in_specs=[whole(pl.ANY)] * n,
        out_specs=[whole(pl.ANY)] * n,
        scratch_shapes=[
            pltpu.VMEM((n,) + shape, jnp.bfloat16),
            pltpu.SemaphoreType.DMA((n,)),
            pltpu.SemaphoreType.DMA((n,)),
        ],
        cost_estimate=pl.CostEstimate(flops=0, bytes_accessed=4 * n * shape[0] * shape[1], transcendentals=0),
        compiler_params=pltpu.CompilerParams(vmem_limit_bytes=LIMIT),
        name="pick",
    )(*pieces)


def partial_kernel(n, q, step, *refs):
    ins, tiles, out, held, came = refs[:n], refs[n : n + q], refs[n + q], refs[n + q + 1], refs[n + q + 2]
    p = lax.axis_index("prow")
    core = lax.axis_index("pcol") % q
    part = ins[0].shape[0]
    take = [
        pltpu.make_async_copy(ins[a], held.at[pl.ds(pl.multiple_of((a ^ p) * part, part), part), :], came.at[a])
        for a in range(n)
    ]
    for x in take:
        x.start()
    for x in take:
        x.wait()
    rows, depth = tiles[0].shape
    for i in range(rows // step):
        total = None
        for e in range(q):
            right = held[pl.ds(pl.multiple_of((core ^ e) * depth, depth), depth), :]
            term = jnp.dot(tiles[e][i * step : (i + 1) * step, :], right, preferred_element_type=jnp.float32)
            total = term if total is None else total + term
        out[i * step : (i + 1) * step, :] = total.astype(out.dtype)


def partial_product(n, q, pieces, tiles, dtype):
    part, width = pieces[0].shape
    rows, depth = tiles[0].shape
    return pl.pallas_call(
        functools.partial(partial_kernel, n, q, min(rows, 512)),
        out_shape=jax.ShapeDtypeStruct((rows, width), dtype),
        in_specs=[whole(pl.ANY)] * n + [whole(VMEM)] * q,
        out_specs=whole(VMEM),
        scratch_shapes=[pltpu.VMEM((n * part, width), jnp.bfloat16), pltpu.SemaphoreType.DMA((n,))],
        compiler_params=pltpu.CompilerParams(vmem_limit_bytes=LIMIT),
        cost_estimate=pl.CostEstimate(
            flops=2 * rows * width * depth * q, bytes_accessed=2 * q * rows * depth, transcendentals=0
        ),
        name="partial_product",
    )(*pieces, *tiles)


def diagonal_kernel(count, lhat, *refs):
    parts, product, diag, sent = refs[:count], refs[count], refs[count + 1], refs[count + 2]
    rows, _ = lhat.shape
    step = min(rows, 512)
    total = None
    for i in range(rows // step):
        here = slice(i * step, (i + 1) * step)
        x = parts[0][here, :].astype(jnp.float32)
        for r in parts[1:]:
            x = x + r[here, :].astype(jnp.float32)
        x = x.T
        product[:, here] = x
        high = x.astype(jnp.bfloat16)
        low = (x - high.astype(jnp.float32)).astype(jnp.bfloat16)
        for y in (high, low):
            term = jnp.dot(y, lhat[here, :], preferred_element_type=jnp.float32)
            total = term if total is None else total + term
    diag[...] = total
    sent[...] = total.astype(jnp.bfloat16)


def diagonal(lhat, parts):
    rows, width = lhat.shape
    return pl.pallas_call(
        functools.partial(diagonal_kernel, len(parts)),
        out_shape=[
            jax.ShapeDtypeStruct((width, rows), jnp.float32),
            jax.ShapeDtypeStruct((width, width), jnp.float32),
            jax.ShapeDtypeStruct((width, width), jnp.bfloat16),
        ],
        in_specs=[whole(VMEM)] * (1 + len(parts)),
        out_specs=[whole(VMEM)] * 3,
        compiler_params=pltpu.CompilerParams(vmem_limit_bytes=LIMIT),
        cost_estimate=pl.CostEstimate(flops=4 * rows * width * width, bytes_accessed=10 * rows * width, transcendentals=0),
        name="diagonal",
    )(lhat, *parts)


def masked_kernel(listed, product, off):
    p = lax.axis_index("prow")
    c = lax.axis_index("pcol")
    i = pl.program_id(0)
    per = off.shape[1] // BLOCK
    base = (p * pl.num_programs(0) + i) * per
    for b in range(per):
        keep = listed[c, base + b].astype(jnp.float32)
        off[:, b * BLOCK : (b + 1) * BLOCK] = -(product[:, b * BLOCK : (b + 1) * BLOCK] * keep)


def masked(listed, product):
    width, rows = product.shape
    step = min(rows, 1024)
    block = pl.BlockSpec((width, step), lambda i: (0, i))
    return pl.pallas_call(
        masked_kernel,
        grid=(rows // step,),
        out_shape=jax.ShapeDtypeStruct((width, rows), jnp.float32),
        in_specs=[whole(SMEM), block],
        out_specs=block,
        compiler_params=pltpu.CompilerParams(vmem_limit_bytes=LIMIT),
        cost_estimate=pl.CostEstimate(flops=2 * rows * width, bytes_accessed=8 * rows * width, transcendentals=0),
        name="masked",
    )(listed, product)


def per_device(n, ncol, l_panel, inverse_tile, unit_inverse, pivot_inverse, listed):
    return level(n, ncol, l_panel, inverse_tile, unit_inverse, pivot_inverse, listed)


def level(n, ncol, l_panel, inverse_tile, unit_inverse, pivot_inverse, listed):
    q = ncol // n
    devices = [(p, z, k) for p in range(n) for z in range(n) for k in range(q)]

    def at(p, z, k):
        return p * ncol + z * q + k

    def swap(x, move):
        pairs = []
        for d in devices:
            to = move(*d)
            if to is not None:
                pairs.append((at(*d), at(*to)))
        return lax.ppermute(x, AXES, pairs)

    def over_rows(x, a):
        return swap(x, lambda p, z, k: (p ^ a, z, k))

    *pieces, lhat = normalize(n, listed, l_panel, unit_inverse)
    tiles = [load(inverse_tile)]
    tiles += [swap(inverse_tile, lambda p, z, k: (p, z, k ^ e)) for e in range(1, q)]
    tiles = [pltpu.with_memory_space_constraint(t, pltpu.VMEM) for t in tiles]

    scattered = [pieces[0]] + [over_rows(pieces[a], a) for a in range(1, n)]
    chosen = pick(n, q, scattered)
    chunk = [None] * n
    for m in reversed(range(n)):
        mine = chosen[m] if m == 0 else swap(chosen[m], lambda p, z, k: (p, z ^ m, k))
        quarters = [mine] + [over_rows(mine, a) for a in range(1, n)]
        chunk[m] = partial_product(n, q, quarters, tiles, jnp.float32 if m == 0 else jnp.bfloat16)

    z_here = lax.axis_index("pcol") // q

    def own(odd, d):
        at_mask = {}
        for z in range(n):
            to = z + d if (z % 2) == odd else z - d
            if 0 <= to < n:
                at_mask.setdefault(z ^ to, []).append(z)
        masks = sorted(at_mask)
        x = chunk[masks[0]]
        for m in masks[1:]:
            here = functools.reduce(jnp.logical_or, [z_here == z for z in at_mask[m]])
            x = jnp.where(here, chunk[m], x)
        return x

    def add(x, y):
        if y is None:
            return x
        return (x.astype(jnp.float32) + y.astype(jnp.float32)).astype(jnp.bfloat16)

    came = [None, None]
    for d in range(n - 1, 0, -1):
        sent = [None, None]
        for odd in (0, 1):
            pairs = line_pairs(n, d, odd)
            if not pairs:
                continue
            to = {}
            for z in pairs:
                to[z], to[z + 1] = z + 1, z
            load_ = add(own(odd, d), came[1 - odd])
            sent[odd] = swap(load_, lambda p, z, k: (p, to[z], k) if z in to else None)
        came = sent

    product, part, travel = diagonal(lhat, [chunk[0]] + [x for x in came if x is not None])
    off = masked(listed, product)
    total = part
    for a in range(1, n):
        total = total + over_rows(travel, a).astype(jnp.float32)
    return off, pivot_inverse + total[None]


def line_pairs(n, d, odd):
    return [z for z in range(odd, n - 1, 2) if z + d < n or z + 1 - d >= 0]


def solution(mesh):
    n, ncol = mesh.shape["prow"], mesh.shape["pcol"]
    return jax.shard_map(
        functools.partial(per_device, n, ncol),
        mesh=mesh,
        in_specs=(
            P("prow", "pcol"),
            P("prow", "pcol"),
            P("pcol", None, None),
            P("pcol", None, None),
            P(),
        ),
        out_specs=(P("pcol", "prow"), P("pcol", None, None)),
        check_vma=False,
    )
```

profile of v0, /device:TPU:0, one launch (start us, length us, event | category | flops | bytes accessed | tf_op | source)
XLA Modules:
  0.0 104.0 jit_solution(3390086081390451357)
XLA Ops:
  0.6 0.6 collective-permute-start.6
  1.2 1.0 copy-done.1
  2.2 0.8 copy-done.2
  3.0 0.7 copy-done.3
  3.7 1.6 %normalize.1 = (bf16[512,128]{1,0:T(8,128)(2,1)S(1)}, bf16[512,128]{1,0:T(8,128)(2,1)S(1)}, bf16[512,128]{1,0:T(8,128)(2,1)S(1)}, bf16[512,128]{1,0:T(8,128)(2,1)S(1)}, bf16[2048,128]{1,0:T(8,128)(2,1)S(1)}) custom-call(s32[8,64]{1,0:T(8,128)S(1)} %copy-done.3, bf16[2048,128]{1,0:T(8,128)(2,1)S(1)} %copy-done.1, bf16[1,128,128]{2,1,0:T(8,128)(2,1)S(1)} %copy-done.2), custom_call_target="tpu_custom_call" | custom-call | flops 67108864 | bytes 1572864 | tf_op jit(solution)/shard_map/normalize/pallas_call | solution.py:56
  5.2 2.6 %collective-permute-start = (bf16[512,128]{1,0:T(8,128)(2,1)S(1)}, bf16[512,128]{1,0:T(8,128)(2,1)S(1)}, u32[]{:S(2)}, u32[]{:S(2)}) collective-permute-start(bf16[512,128]{1,0:T(8,128)(2,1)S(1)} %get-tuple-element.16), channel_id=1, source_target_pairs={{0,8},{1,9},{2,10},{3,11},{4,12},{5,13},{6,14},{7,15},{8,0},{9,1},... | collective-permute-start | bytes 393224 | tf_op jit(solution)/shard_map/ppermute | solution.py:248
  7.8 1.5 %collective-permute-start.1 = (bf16[512,128]{1,0:T(8,128)(2,1)S(1)}, bf16[512,128]{1,0:T(8,128)(2,1)S(1)}, u32[]{:S(2)}, u32[]{:S(2)}) collective-permute-start(bf16[512,128]{1,0:T(8,128)(2,1)S(1)} %get-tuple-element.17), channel_id=1, source_target_pairs={{0,16},{1,17},{2,18},{3,19},{4,20},{5,21},{6,22},{7,23},{8,24},{9,... | collective-permute-start | bytes 393224 | tf_op jit(solution)/shard_map/ppermute | solution.py:248
  9.3 0.0 collective-permute-start.2
  9.3 2.8 %collective-permute-done.refs_1_ = bf16[512,128]{1,0:T(8,128)(2,1)S(1)} collective-permute-done((bf16[512,128]{1,0:T(8,128)(2,1)S(1)}, bf16[512,128]{1,0:T(8,128)(2,1)S(1)}, u32[]{:S(2)}, u32[]{:S(2)}) %collective-permute-start) | collective-permute-done | bytes 131104 | tf_op jit(solution)/shard_map/ppermute | solution.py:248
  12.1 4.1 %collective-permute-done.1.refs_2_ = bf16[512,128]{1,0:T(8,128)(2,1)S(1)} collective-permute-done((bf16[512,128]{1,0:T(8,128)(2,1)S(1)}, bf16[512,128]{1,0:T(8,128)(2,1)S(1)}, u32[]{:S(2)}, u32[]{:S(2)}) %collective-permute-start.1) | collective-permute-done | bytes 131104 | tf_op jit(solution)/shard_map/ppermute | solution.py:248
  16.2 1.4 %pick.1 = (bf16[512,128]{1,0:T(8,128)(2,1)S(1)}, bf16[512,128]{1,0:T(8,128)(2,1)S(1)}, bf16[512,128]{1,0:T(8,128)(2,1)S(1)}, bf16[512,128]{1,0:T(8,128)(2,1)S(1)}) custom-call(bf16[512,128]{1,0:T(8,128)(2,1)S(1)} %get-tuple-element.15.refs_0_, bf16[512,128]{1,0:T(8,128)(2,1)S(1)} %collective-permute-done.refs_1_, ...), custom_call_target="tpu_custom_call" | custom-call | bytes 1048576 | tf_op jit(solution)/shard_map/pick/pallas_call | solution.py:110
  17.6 3.7 %collective-permute-start.15 = (bf16[512,128]{1,0:T(8,128)(2,1)S(1)}, bf16[512,128]{1,0:T(8,128)(2,1)S(1)}, u32[]{:S(2)}, u32[]{:S(2)}) collective-permute-start(bf16[512,128]{1,0:T(8,128)(2,1)S(1)} %get-tuple-element.22), channel_id=1, source_target_pairs={{0,6},{1,7},{2,4},{3,5},{4,2},{5,3},{6,0},{7,1},{8,14},{9,15},{10,... | collective-permute-start | bytes 393224 | tf_op jit(solution)/shard_map/ppermute | solution.py:248
  21.3 3.2 %collective-permute-done.15.refs_0_ = bf16[512,128]{1,0:T(8,128)(2,1)S(1)} collective-permute-done((bf16[512,128]{1,0:T(8,128)(2,1)S(1)}, bf16[512,128]{1,0:T(8,128)(2,1)S(1)}, u32[]{:S(2)}, u32[]{:S(2)}) %collective-permute-start.15) | collective-permute-done | bytes 131104 | tf_op jit(solution)/shard_map/ppermute | solution.py:248
  24.5 1.5 %collective-permute-start.16 = (bf16[512,128]{1,0:T(8,128)(2,1)S(1)}, bf16[512,128]{1,0:T(8,128)(2,1)S(1)}, u32[]{:S(2)}, u32[]{:S(2)}) collective-permute-start(bf16[512,128]{1,0:T(8,128)(2,1)S(1)} %collective-permute-done.15.refs_0_), channel_id=1, source_target_pairs={{0,8},{1,9},{2,10},{3,11},{4,12},{5,13},{6,14},{7,15},{8,0},{9,1},... | collective-permute-start | bytes 393224 | tf_op jit(solution)/shard_map/ppermute | solution.py:248
  25.9 0.6 collective-permute-start.17
  26.5 1.4 %collective-permute-start.18 = (bf16[512,128]{1,0:T(8,128)(2,1)S(1)}, bf16[512,128]{1,0:T(8,128)(2,1)S(1)}, u32[]{:S(2)}, u32[]{:S(2)}) collective-permute-start(bf16[512,128]{1,0:T(8,128)(2,1)S(1)} %collective-permute-done.15.refs_0_), channel_id=1, source_target_pairs={{0,24},{1,25},{2,26},{3,27},{4,28},{5,29},{6,30},{7,31},{8,16},{9,... | collective-permute-start | bytes 393224 | tf_op jit(solution)/shard_map/ppermute | solution.py:248
  28.0 2.2 %copy-done = bf16[2048,1024]{1,0:T(8,128)(2,1)S(1)} copy-done((bf16[2048,1024]{1,0:T(8,128)(2,1)S(1)}, bf16[2048,1024]{1,0:T(8,128)(2,1)}, u32[]{:S(2)}) %copy-start) | copy-done | bytes 4194328
  30.2 0.3 load.1.refs_4_
  30.4 0.2 collective-permute-done.16.refs_1_
  30.6 2.1 %collective-permute-done.17.refs_2_ = bf16[512,128]{1,0:T(8,128)(2,1)S(1)} collective-permute-done((bf16[512,128]{1,0:T(8,128)(2,1)S(1)}, bf16[512,128]{1,0:T(8,128)(2,1)S(1)}, u32[]{:S(2)}, u32[]{:S(2)}) %collective-permute-start.17) | collective-permute-done | bytes 131104 | tf_op jit(solution)/shard_map/ppermute | solution.py:248
  32.7 3.0 %partial_product.7 = bf16[2048,128]{1,0:T(8,128)(2,1)S(1)} custom-call(bf16[512,128]{1,0:T(8,128)(2,1)S(1)} %collective-permute-done.15.refs_0_, bf16[512,128]{1,0:T(8,128)(2,1)S(1)} %collective-permute-done.16.refs_1_, bf16[512,128]{1,0:T(8,128)(2,1)S(1)} %collective-permute-done.17.refs_2_, bf16[512,128]{1,0:T(8,128)(2,1)S(1)} %collective-permute-done.18.refs_3_, ...), custom_call_target="tpu_custom_call" | custom-call | flops 1073741824 | bytes 8388608 | tf_op jit(solution)/shard_map/partial_product/pallas_call | solution.py:152
  35.8 2.9 %collective-permute-start.19 = (bf16[2048,128]{1,0:T(8,128)(2,1)S(1)}, bf16[2048,128]{1,0:T(8,128)(2,1)S(1)}, u32[]{:S(2)}, u32[]{:S(2)}) collective-permute-start(bf16[2048,128]{1,0:T(8,128)(2,1)S(1)} %partial_product.7), channel_id=1, source_target_pairs={{0,2},{1,3},{2,0},{3,1},{4,6},{5,7},{6,4},{7,5},{8,10},{9,11},{10,... | collective-permute-start | bytes 1572872 | tf_op jit(solution)/shard_map/ppermute | solution.py:248
  38.6 1.2 %collective-permute-start.11 = (bf16[512,128]{1,0:T(8,128)(2,1)S(1)}, bf16[512,128]{1,0:T(8,128)(2,1)S(1)}, u32[]{:S(2)}, u32[]{:S(2)}) collective-permute-start(bf16[512,128]{1,0:T(8,128)(2,1)S(1)} %get-tuple-element.21), channel_id=1, source_target_pairs={{0,4},{1,5},{2,6},{3,7},{4,0},{5,1},{6,2},{7,3},{8,12},{9,13},{10,... | collective-permute-start | bytes 393224 | tf_op jit(solution)/shard_map/ppermute | solution.py:248
  39.9 1.3 %collective-permute-start.7 = (bf16[512,128]{1,0:T(8,128)(2,1)S(1)}, bf16[512,128]{1,0:T(8,128)(2,1)S(1)}, u32[]{:S(2)}, u32[]{:S(2)}) collective-permute-start(bf16[512,128]{1,0:T(8,128)(2,1)S(1)} %get-tuple-element.20), channel_id=1, source_target_pairs={{0,2},{1,3},{2,0},{3,1},{4,6},{5,7},{6,4},{7,5},{8,10},{9,11},{10,... | collective-permute-start | bytes 393224 | tf_op jit(solution)/shard_map/ppermute | solution.py:248
  41.1 10.8 %collective-permute-done.11.refs_0_ = bf16[512,128]{1,0:T(8,128)(2,1)S(1)} collective-permute-done((bf16[512,128]{1,0:T(8,128)(2,1)S(1)}, bf16[512,128]{1,0:T(8,128)(2,1)S(1)}, u32[]{:S(2)}, u32[]{:S(2)}) %collective-permute-start.11) | collective-permute-done | bytes 131104 | tf_op jit(solution)/shard_map/ppermute | solution.py:248
  51.9 1.4 %collective-permute-start.12 = (bf16[512,128]{1,0:T(8,128)(2,1)S(1)}, bf16[512,128]{1,0:T(8,128)(2,1)S(1)}, u32[]{:S(2)}, u32[]{:S(2)}) collective-permute-start(bf16[512,128]{1,0:T(8,128)(2,1)S(1)} %collective-permute-done.11.refs_0_), channel_id=1, source_target_pairs={{0,8},{1,9},{2,10},{3,11},{4,12},{5,13},{6,14},{7,15},{8,0},{9,1},... | collective-permute-start | bytes 393224 | tf_op jit(solution)/shard_map/ppermute | solution.py:248
  53.3 0.6 collective-permute-start.13
  53.9 1.6 %collective-permute-start.14 = (bf16[512,128]{1,0:T(8,128)(2,1)S(1)}, bf16[512,128]{1,0:T(8,128)(2,1)S(1)}, u32[]{:S(2)}, u32[]{:S(2)}) collective-permute-start(bf16[512,128]{1,0:T(8,128)(2,1)S(1)} %collective-permute-done.11.refs_0_), channel_id=1, source_target_pairs={{0,24},{1,25},{2,26},{3,27},{4,28},{5,29},{6,30},{7,31},{8,16},{9,... | collective-permute-start | bytes 393224 | tf_op jit(solution)/shard_map/ppermute | solution.py:248
  55.4 1.4 %collective-permute-start.10 = (bf16[512,128]{1,0:T(8,128)(2,1)S(1)}, bf16[512,128]{1,0:T(8,128)(2,1)S(1)}, u32[]{:S(2)}, u32[]{:S(2)}) collective-permute-start(bf16[512,128]{1,0:T(8,128)(2,1)S(1)} %collective-permute-done.7.refs_0_), channel_id=1, source_target_pairs={{0,24},{1,25},{2,26},{3,27},{4,28},{5,29},{6,30},{7,31},{8,16},{9,... | collective-permute-start | bytes 393224 | tf_op jit(solution)/shard_map/ppermute | solution.py:248
  56.8 1.5 %collective-permute-done.12.refs_1_ = bf16[512,128]{1,0:T(8,128)(2,1)S(1)} collective-permute-done((bf16[512,128]{1,0:T(8,128)(2,1)S(1)}, bf16[512,128]{1,0:T(8,128)(2,1)S(1)}, u32[]{:S(2)}, u32[]{:S(2)}) %collective-permute-start.12) | collective-permute-done | bytes 131104 | tf_op jit(solution)/shard_map/ppermute | solution.py:248
  58.3 1.4 %collective-permute-start.8 = (bf16[512,128]{1,0:T(8,128)(2,1)S(1)}, bf16[512,128]{1,0:T(8,128)(2,1)S(1)}, u32[]{:S(2)}, u32[]{:S(2)}) collective-permute-start(bf16[512,128]{1,0:T(8,128)(2,1)S(1)} %collective-permute-done.7.refs_0_), channel_id=1, source_target_pairs={{0,8},{1,9},{2,10},{3,11},{4,12},{5,13},{6,14},{7,15},{8,0},{9,1},... | collective-permute-start | bytes 393224 | tf_op jit(solution)/shard_map/ppermute | solution.py:248
  59.7 2.9 %collective-permute-done.13.refs_2_ = bf16[512,128]{1,0:T(8,128)(2,1)S(1)} collective-permute-done((bf16[512,128]{1,0:T(8,128)(2,1)S(1)}, bf16[512,128]{1,0:T(8,128)(2,1)S(1)}, u32[]{:S(2)}, u32[]{:S(2)}) %collective-permute-start.13) | collective-permute-done | bytes 131104 | tf_op jit(solution)/shard_map/ppermute | solution.py:248
  62.6 1.1 %collective-permute-start.9 = (bf16[512,128]{1,0:T(8,128)(2,1)S(1)}, bf16[512,128]{1,0:T(8,128)(2,1)S(1)}, u32[]{:S(2)}, u32[]{:S(2)}) collective-permute-start(bf16[512,128]{1,0:T(8,128)(2,1)S(1)} %collective-permute-done.7.refs_0_), channel_id=1, source_target_pairs={{0,16},{1,17},{2,18},{3,19},{4,20},{5,21},{6,22},{7,23},{8,24},{9,... | collective-permute-start | bytes 393224 | tf_op jit(solution)/shard_map/ppermute | solution.py:248
  63.7 0.0 collective-permute-done.14.refs_3_
  63.7 3.0 %partial_product.6 = bf16[2048,128]{1,0:T(8,128)(2,1)S(1)} custom-call(bf16[512,128]{1,0:T(8,128)(2,1)S(1)} %collective-permute-done.11.refs_0_, bf16[512,128]{1,0:T(8,128)(2,1)S(1)} %collective-permute-done.12.refs_1_, bf16[512,128]{1,0:T(8,128)(2,1)S(1)} %collective-permute-done.13.refs_2_, bf16[512,128]{1,0:T(8,128)(2,1)S(1)} %collective-permute-done.14.refs_3_, ...), custom_call_target="tpu_custom_call" | custom-call | flops 1073741824 | bytes 8388608 | tf_op jit(solution)/shard_map/partial_product/pallas_call | solution.py:152
  66.7 0.1 collective-permute-start.22
  66.8 0.1 add_convert_fusion.2
  66.9 0.7 collective-permute-start.20
  67.6 0.0 collective-permute-done.8.refs_1_
  67.7 3.1 %partial_product.5 = bf16[2048,128]{1,0:T(8,128)(2,1)S(1)} custom-call(bf16[512,128]{1,0:T(8,128)(2,1)S(1)} %collective-permute-done.7.refs_0_, bf16[512,128]{1,0:T(8,128)(2,1)S(1)} %collective-permute-done.8.refs_1_, bf16[512,128]{1,0:T(8,128)(2,1)S(1)} %collective-permute-done.9.refs_2_, bf16[512,128]{1,0:T(8,128)(2,1)S(1)} %collective-permute-done.10.refs_3_, ...), custom_call_target="tpu_custom_call" | custom-call | flops 1073741824 | bytes 8388608 | tf_op jit(solution)/shard_map/partial_product/pallas_call | solution.py:152
  70.7 7.7 %collective-permute-done.22 = bf16[2048,128]{1,0:T(8,128)(2,1)S(1)} collective-permute-done((bf16[2048,128]{1,0:T(8,128)(2,1)S(1)}, bf16[2048,128]{1,0:T(8,128)(2,1)S(1)}, u32[]{:S(2)}, u32[]{:S(2)}) %collective-permute-start.22) | collective-permute-done | bytes 524320 | tf_op jit(solution)/shard_map/ppermute | solution.py:248
  78.5 0.1 add_convert_fusion
  78.6 0.7 collective-permute-start.23
  79.3 0.0 collective-permute-done.20
  79.3 0.1 add_convert_fusion.1
  79.5 5.4 %collective-permute-start.21 = (bf16[2048,128]{1,0:T(8,128)(2,1)S(1)}, bf16[2048,128]{1,0:T(8,128)(2,1)S(1)}, u32[]{:S(2)}, u32[]{:S(2)}) collective-permute-start(bf16[2048,128]{1,0:T(8,128)(2,1)S(1)} %add_convert_fusion.1), channel_id=1, source_target_pairs={{0,2},{1,3},{2,0},{3,1},{4,6},{5,7},{6,4},{7,5},{8,10},{9,11},{10,... | collective-permute-start | bytes 1572872 | tf_op jit(solution)/shard_map/ppermute | solution.py:248
  84.9 0.2 collective-permute-start.3
  85.1 1.2 %collective-permute-start.4 = (bf16[512,128]{1,0:T(8,128)(2,1)S(1)}, bf16[512,128]{1,0:T(8,128)(2,1)S(1)}, u32[]{:S(2)}, u32[]{:S(2)}) collective-permute-start(bf16[512,128]{1,0:T(8,128)(2,1)S(1)} %get-tuple-element.19.refs_0_), channel_id=1, source_target_pairs={{0,16},{1,17},{2,18},{3,19},{4,20},{5,21},{6,22},{7,23},{8,24},{9,... | collective-permute-start | bytes 393224 | tf_op jit(solution)/shard_map/ppermute | solution.py:248
  86.3 2.1 %collective-permute-start.5 = (bf16[512,128]{1,0:T(8,128)(2,1)S(1)}, bf16[512,128]{1,0:T(8,128)(2,1)S(1)}, u32[]{:S(2)}, u32[]{:S(2)}) collective-permute-start(bf16[512,128]{1,0:T(8,128)(2,1)S(1)} %get-tuple-element.19.refs_0_), channel_id=1, source_target_pairs={{0,24},{1,25},{2,26},{3,27},{4,28},{5,29},{6,30},{7,31},{8,16},{9,... | collective-permute-start | bytes 393224 | tf_op jit(solution)/shard_map/ppermute | solution.py:248
  88.4 1.5 %collective-permute-done.3.refs_1_ = bf16[512,128]{1,0:T(8,128)(2,1)S(1)} collective-permute-done((bf16[512,128]{1,0:T(8,128)(2,1)S(1)}, bf16[512,128]{1,0:T(8,128)(2,1)S(1)}, u32[]{:S(2)}, u32[]{:S(2)}) %collective-permute-start.3) | collective-permute-done | bytes 131104 | tf_op jit(solution)/shard_map/ppermute | solution.py:248
  89.9 0.2 collective-permute-done.4.refs_2_
  90.1 2.1 %collective-permute-done.5.refs_3_ = bf16[512,128]{1,0:T(8,128)(2,1)S(1)} collective-permute-done((bf16[512,128]{1,0:T(8,128)(2,1)S(1)}, bf16[512,128]{1,0:T(8,128)(2,1)S(1)}, u32[]{:S(2)}, u32[]{:S(2)}) %collective-permute-start.5) | collective-permute-done | bytes 131104 | tf_op jit(solution)/shard_map/ppermute | solution.py:248
  92.2 3.0 %partial_product.4.refs_0_ = f32[2048,128]{1,0:T(8,128)S(1)} custom-call(bf16[512,128]{1,0:T(8,128)(2,1)S(1)} %get-tuple-element.19.refs_0_, bf16[512,128]{1,0:T(8,128)(2,1)S(1)} %collective-permute-done.3.refs_1_, bf16[512,128]{1,0:T(8,128)(2,1)S(1)} %collective-permute-done.4.refs_2_, bf16[512,128]{1,0:T(8,128)(2,1)S(1)} %collective-permute-done.5.refs_3_, ...), custom_call_target="tpu_custom_call" | custom-call | flops 1073741824 | bytes 8388608 | tf_op jit(solution)/shard_map/partial_product/pallas_call | solution.py:152
  95.2 0.0 copy-start.5
  95.2 0.0 collective-permute-done.23.refs_2_
  95.2 0.0 collective-permute-done.21.refs_1_
  95.3 0.5 diagonal.1
  95.8 2.1 %collective-permute-start.24 = (bf16[128,128]{1,0:T(8,128)(2,1)S(1)}, bf16[128,128]{1,0:T(8,128)(2,1)S(1)}, u32[]{:S(2)}, u32[]{:S(2)}) collective-permute-start(bf16[128,128]{1,0:T(8,128)(2,1)S(1)} %get-tuple-element.25), channel_id=1, source_target_pairs={{0,8},{1,9},{2,10},{3,11},{4,12},{5,13},{6,14},{7,15},{8,0},{9,1},... | collective-permute-start | bytes 98312 | tf_op jit(solution)/shard_map/ppermute | solution.py:248
  97.9 0.6 collective-permute-start.25
  98.5 1.0 collective-permute-start.26
  99.4 1.7 %masked.1 = f32[128,2048]{1,0:T(8,128)} custom-call(s32[8,64]{1,0:T(8,128)S(1)} %copy-done.4, f32[128,2048]{1,0:T(8,128)S(1)} %get-tuple-element.23.product), custom_call_target="tpu_custom_call" | custom-call | flops 524288 | bytes 2097152 | tf_op jit(solution)/shard_map/masked/pallas_call | solution.py:219
  101.1 0.7 collective-permute-done.25
  101.8 1.5 %collective-permute-done.26 = bf16[128,128]{1,0:T(8,128)(2,1)S(1)} collective-permute-done((bf16[128,128]{1,0:T(8,128)(2,1)S(1)}, bf16[128,128]{1,0:T(8,128)(2,1)S(1)}, u32[]{:S(2)}, u32[]{:S(2)}) %collective-permute-start.26) | collective-permute-done | bytes 32800 | tf_op jit(solution)/shard_map/ppermute | solution.py:248
  103.3 0.7 bitcast_add_fusion
  (15 shorter events, 0.0 us)
Async XLA Ops:
  0.6 32.1 %collective-permute-start.6 = (bf16[2048,1024]{1,0:T(8,128)(2,1)}, bf16[2048,1024]{1,0:T(8,128)(2,1)S(1)}, u32[]{:S(2)}, u32[]{:S(2)}) collective-permute-start(bf16[2048,1024]{1,0:T(8,128)(2,1)} %tile.1), channel_id=1, source_target_pairs={{0,1},{1,0},{2,3},{3,2},{4,5},{5,4},{6,7},{7,6},{8,9},{9,8},{10,11... | collective-permute-start | bytes 12582920 | tf_op jit(solution)/shard_map/ppermute | solution.py:248
  1.2 1.0 %copy-start.1 = (bf16[2048,128]{1,0:T(8,128)(2,1)S(1)}, bf16[2048,128]{1,0:T(8,128)(2,1)}, u32[]{:S(2)}) copy-start(bf16[2048,128]{1,0:T(8,128)(2,1)} %panel.1) | copy-start | bytes 1572868
  2.2 0.8 copy-start.2
  3.0 0.7 copy-start.3
  5.2 6.9 %collective-permute-start = (bf16[512,128]{1,0:T(8,128)(2,1)S(1)}, bf16[512,128]{1,0:T(8,128)(2,1)S(1)}, u32[]{:S(2)}, u32[]{:S(2)}) collective-permute-start(bf16[512,128]{1,0:T(8,128)(2,1)S(1)} %get-tuple-element.16), channel_id=1, source_target_pairs={{0,8},{1,9},{2,10},{3,11},{4,12},{5,13},{6,14},{7,15},{8,0},{9,1},... | collective-permute-start | bytes 393224 | tf_op jit(solution)/shard_map/ppermute | solution.py:248
  7.8 8.4 %collective-permute-start.1 = (bf16[512,128]{1,0:T(8,128)(2,1)S(1)}, bf16[512,128]{1,0:T(8,128)(2,1)S(1)}, u32[]{:S(2)}, u32[]{:S(2)}) collective-permute-start(bf16[512,128]{1,0:T(8,128)(2,1)S(1)} %get-tuple-element.17), channel_id=1, source_target_pairs={{0,16},{1,17},{2,18},{3,19},{4,20},{5,21},{6,22},{7,23},{8,24},{9,... | collective-permute-start | bytes 393224 | tf_op jit(solution)/shard_map/ppermute | solution.py:248
  9.3 6.9 %collective-permute-start.2 = (bf16[512,128]{1,0:T(8,128)(2,1)S(1)}, bf16[512,128]{1,0:T(8,128)(2,1)S(1)}, u32[]{:S(2)}, u32[]{:S(2)}) collective-permute-start(bf16[512,128]{1,0:T(8,128)(2,1)S(1)} %get-tuple-element.18), channel_id=1, source_target_pairs={{0,24},{1,25},{2,26},{3,27},{4,28},{5,29},{6,30},{7,31},{8,16},{9,... | collective-permute-start | bytes 393224 | tf_op jit(solution)/shard_map/ppermute | solution.py:248
  17.6 6.8 %collective-permute-start.15 = (bf16[512,128]{1,0:T(8,128)(2,1)S(1)}, bf16[512,128]{1,0:T(8,128)(2,1)S(1)}, u32[]{:S(2)}, u32[]{:S(2)}) collective-permute-start(bf16[512,128]{1,0:T(8,128)(2,1)S(1)} %get-tuple-element.22), channel_id=1, source_target_pairs={{0,6},{1,7},{2,4},{3,5},{4,2},{5,3},{6,0},{7,1},{8,14},{9,15},{10,... | collective-permute-start | bytes 393224 | tf_op jit(solution)/shard_map/ppermute | solution.py:248
  24.5 6.1 %collective-permute-start.16 = (bf16[512,128]{1,0:T(8,128)(2,1)S(1)}, bf16[512,128]{1,0:T(8,128)(2,1)S(1)}, u32[]{:S(2)}, u32[]{:S(2)}) collective-permute-start(bf16[512,128]{1,0:T(8,128)(2,1)S(1)} %collective-permute-done.15.refs_0_), channel_id=1, source_target_pairs={{0,8},{1,9},{2,10},{3,11},{4,12},{5,13},{6,14},{7,15},{8,0},{9,1},... | collective-permute-start | bytes 393224 | tf_op jit(solution)/shard_map/ppermute | solution.py:248
  25.9 6.8 %collective-permute-start.17 = (bf16[512,128]{1,0:T(8,128)(2,1)S(1)}, bf16[512,128]{1,0:T(8,128)(2,1)S(1)}, u32[]{:S(2)}, u32[]{:S(2)}) collective-permute-start(bf16[512,128]{1,0:T(8,128)(2,1)S(1)} %collective-permute-done.15.refs_0_), channel_id=1, source_target_pairs={{0,16},{1,17},{2,18},{3,19},{4,20},{5,21},{6,22},{7,23},{8,24},{9,... | collective-permute-start | bytes 393224 | tf_op jit(solution)/shard_map/ppermute | solution.py:248
  26.5 6.2 %collective-permute-start.18 = (bf16[512,128]{1,0:T(8,128)(2,1)S(1)}, bf16[512,128]{1,0:T(8,128)(2,1)S(1)}, u32[]{:S(2)}, u32[]{:S(2)}) collective-permute-start(bf16[512,128]{1,0:T(8,128)(2,1)S(1)} %collective-permute-done.15.refs_0_), channel_id=1, source_target_pairs={{0,24},{1,25},{2,26},{3,27},{4,28},{5,29},{6,30},{7,31},{8,16},{9,... | collective-permute-start | bytes 393224 | tf_op jit(solution)/shard_map/ppermute | solution.py:248
  28.0 2.2 %copy-start = (bf16[2048,1024]{1,0:T(8,128)(2,1)S(1)}, bf16[2048,1024]{1,0:T(8,128)(2,1)}, u32[]{:S(2)}) copy-start(bf16[2048,1024]{1,0:T(8,128)(2,1)} %tile.1) | copy-start | bytes 12582916
  35.8 31.0 %collective-permute-start.19 = (bf16[2048,128]{1,0:T(8,128)(2,1)S(1)}, bf16[2048,128]{1,0:T(8,128)(2,1)S(1)}, u32[]{:S(2)}, u32[]{:S(2)}) collective-permute-start(bf16[2048,128]{1,0:T(8,128)(2,1)S(1)} %partial_product.7), channel_id=1, source_target_pairs={{0,2},{1,3},{2,0},{3,1},{4,6},{5,7},{6,4},{7,5},{8,10},{9,11},{10,... | collective-permute-start | bytes 1572872 | tf_op jit(solution)/shard_map/ppermute | solution.py:248
  38.6 13.3 %collective-permute-start.11 = (bf16[512,128]{1,0:T(8,128)(2,1)S(1)}, bf16[512,128]{1,0:T(8,128)(2,1)S(1)}, u32[]{:S(2)}, u32[]{:S(2)}) collective-permute-start(bf16[512,128]{1,0:T(8,128)(2,1)S(1)} %get-tuple-element.21), channel_id=1, source_target_pairs={{0,4},{1,5},{2,6},{3,7},{4,0},{5,1},{6,2},{7,3},{8,12},{9,13},{10,... | collective-permute-start | bytes 393224 | tf_op jit(solution)/shard_map/ppermute | solution.py:248
  39.9 15.6 %collective-permute-start.7 = (bf16[512,128]{1,0:T(8,128)(2,1)S(1)}, bf16[512,128]{1,0:T(8,128)(2,1)S(1)}, u32[]{:S(2)}, u32[]{:S(2)}) collective-permute-start(bf16[512,128]{1,0:T(8,128)(2,1)S(1)} %get-tuple-element.20), channel_id=1, source_target_pairs={{0,2},{1,3},{2,0},{3,1},{4,6},{5,7},{6,4},{7,5},{8,10},{9,11},{10,... | collective-permute-start | bytes 393224 | tf_op jit(solution)/shard_map/ppermute | solution.py:248
  51.9 6.4 %collective-permute-start.12 = (bf16[512,128]{1,0:T(8,128)(2,1)S(1)}, bf16[512,128]{1,0:T(8,128)(2,1)S(1)}, u32[]{:S(2)}, u32[]{:S(2)}) collective-permute-start(bf16[512,128]{1,0:T(8,128)(2,1)S(1)} %collective-permute-done.11.refs_0_), channel_id=1, source_target_pairs={{0,8},{1,9},{2,10},{3,11},{4,12},{5,13},{6,14},{7,15},{8,0},{9,1},... | collective-permute-start | bytes 393224 | tf_op jit(solution)/shard_map/ppermute | solution.py:248
  53.3 9.3 %collective-permute-start.13 = (bf16[512,128]{1,0:T(8,128)(2,1)S(1)}, bf16[512,128]{1,0:T(8,128)(2,1)S(1)}, u32[]{:S(2)}, u32[]{:S(2)}) collective-permute-start(bf16[512,128]{1,0:T(8,128)(2,1)S(1)} %collective-permute-done.11.refs_0_), channel_id=1, source_target_pairs={{0,16},{1,17},{2,18},{3,19},{4,20},{5,21},{6,22},{7,23},{8,24},{9,... | collective-permute-start | bytes 393224 | tf_op jit(solution)/shard_map/ppermute | solution.py:248
  53.9 9.8 %collective-permute-start.14 = (bf16[512,128]{1,0:T(8,128)(2,1)S(1)}, bf16[512,128]{1,0:T(8,128)(2,1)S(1)}, u32[]{:S(2)}, u32[]{:S(2)}) collective-permute-start(bf16[512,128]{1,0:T(8,128)(2,1)S(1)} %collective-permute-done.11.refs_0_), channel_id=1, source_target_pairs={{0,24},{1,25},{2,26},{3,27},{4,28},{5,29},{6,30},{7,31},{8,16},{9,... | collective-permute-start | bytes 393224 | tf_op jit(solution)/shard_map/ppermute | solution.py:248
  55.4 12.2 %collective-permute-start.10 = (bf16[512,128]{1,0:T(8,128)(2,1)S(1)}, bf16[512,128]{1,0:T(8,128)(2,1)S(1)}, u32[]{:S(2)}, u32[]{:S(2)}) collective-permute-start(bf16[512,128]{1,0:T(8,128)(2,1)S(1)} %collective-permute-done.7.refs_0_), channel_id=1, source_target_pairs={{0,24},{1,25},{2,26},{3,27},{4,28},{5,29},{6,30},{7,31},{8,16},{9,... | collective-permute-start | bytes 393224 | tf_op jit(solution)/shard_map/ppermute | solution.py:248
  58.3 9.3 %collective-permute-start.8 = (bf16[512,128]{1,0:T(8,128)(2,1)S(1)}, bf16[512,128]{1,0:T(8,128)(2,1)S(1)}, u32[]{:S(2)}, u32[]{:S(2)}) collective-permute-start(bf16[512,128]{1,0:T(8,128)(2,1)S(1)} %collective-permute-done.7.refs_0_), channel_id=1, source_target_pairs={{0,8},{1,9},{2,10},{3,11},{4,12},{5,13},{6,14},{7,15},{8,0},{9,1},... | collective-permute-start | bytes 393224 | tf_op jit(solution)/shard_map/ppermute | solution.py:248
  62.6 5.1 %collective-permute-start.9 = (bf16[512,128]{1,0:T(8,128)(2,1)S(1)}, bf16[512,128]{1,0:T(8,128)(2,1)S(1)}, u32[]{:S(2)}, u32[]{:S(2)}) collective-permute-start(bf16[512,128]{1,0:T(8,128)(2,1)S(1)} %collective-permute-done.7.refs_0_), channel_id=1, source_target_pairs={{0,16},{1,17},{2,18},{3,19},{4,20},{5,21},{6,22},{7,23},{8,24},{9,... | collective-permute-start | bytes 393224 | tf_op jit(solution)/shard_map/ppermute | solution.py:248
  66.7 11.8 %collective-permute-start.22 = (bf16[2048,128]{1,0:T(8,128)(2,1)S(1)}, bf16[2048,128]{1,0:T(8,128)(2,1)S(1)}, u32[]{:S(2)}, u32[]{:S(2)}) collective-permute-start(bf16[2048,128]{1,0:T(8,128)(2,1)S(1)} %partial_product.6), channel_id=1, source_target_pairs={{0,2},{1,3},{2,0},{3,1},{4,6},{5,7},{6,4},{7,5},{8,10},{9,11},{10,... | collective-permute-start | bytes 1572872 | tf_op jit(solution)/shard_map/ppermute | solution.py:248
  66.9 12.4 %collective-permute-start.20 = (bf16[2048,128]{1,0:T(8,128)(2,1)S(1)}, bf16[2048,128]{1,0:T(8,128)(2,1)S(1)}, u32[]{:S(2)}, u32[]{:S(2)}) collective-permute-start(bf16[2048,128]{1,0:T(8,128)(2,1)S(1)} %add_convert_fusion.2), channel_id=1, source_target_pairs={{2,4},{3,5},{4,2},{5,3},{10,12},{11,13},{12,10},{13,11},{18,20},{1... | collective-permute-start | bytes 1572872 | tf_op jit(solution)/shard_map/ppermute | solution.py:248
  78.6 16.6 %collective-permute-start.23 = (bf16[2048,128]{1,0:T(8,128)(2,1)S(1)}, bf16[2048,128]{1,0:T(8,128)(2,1)S(1)}, u32[]{:S(2)}, u32[]{:S(2)}) collective-permute-start(bf16[2048,128]{1,0:T(8,128)(2,1)S(1)} %add_convert_fusion), channel_id=1, source_target_pairs={{2,4},{3,5},{4,2},{5,3},{10,12},{11,13},{12,10},{13,11},{18,20},{1... | collective-permute-start | bytes 1572872 | tf_op jit(solution)/shard_map/ppermute | solution.py:248
  79.5 15.8 %collective-permute-start.21 = (bf16[2048,128]{1,0:T(8,128)(2,1)S(1)}, bf16[2048,128]{1,0:T(8,128)(2,1)S(1)}, u32[]{:S(2)}, u32[]{:S(2)}) collective-permute-start(bf16[2048,128]{1,0:T(8,128)(2,1)S(1)} %add_convert_fusion.1), channel_id=1, source_target_pairs={{0,2},{1,3},{2,0},{3,1},{4,6},{5,7},{6,4},{7,5},{8,10},{9,11},{10,... | collective-permute-start | bytes 1572872 | tf_op jit(solution)/shard_map/ppermute | solution.py:248
  84.9 14.5 %copy-start.4 = (s32[8,64]{1,0:T(8,128)S(1)}, s32[8,64]{1,0:T(8,128)}, u32[]{:S(2)}) copy-start(s32[8,64]{1,0:T(8,128)} %listed.3) | copy-start | bytes 6148
  84.9 5.0 %collective-permute-start.3 = (bf16[512,128]{1,0:T(8,128)(2,1)S(1)}, bf16[512,128]{1,0:T(8,128)(2,1)S(1)}, u32[]{:S(2)}, u32[]{:S(2)}) collective-permute-start(bf16[512,128]{1,0:T(8,128)(2,1)S(1)} %get-tuple-element.19.refs_0_), channel_id=1, source_target_pairs={{0,8},{1,9},{2,10},{3,11},{4,12},{5,13},{6,14},{7,15},{8,0},{9,1},... | collective-permute-start | bytes 393224 | tf_op jit(solution)/shard_map/ppermute | solution.py:248
  85.1 5.0 %collective-permute-start.4 = (bf16[512,128]{1,0:T(8,128)(2,1)S(1)}, bf16[512,128]{1,0:T(8,128)(2,1)S(1)}, u32[]{:S(2)}, u32[]{:S(2)}) collective-permute-start(bf16[512,128]{1,0:T(8,128)(2,1)S(1)} %get-tuple-element.19.refs_0_), channel_id=1, source_target_pairs={{0,16},{1,17},{2,18},{3,19},{4,20},{5,21},{6,22},{7,23},{8,24},{9,... | collective-permute-start | bytes 393224 | tf_op jit(solution)/shard_map/ppermute | solution.py:248
  86.3 5.9 %collective-permute-start.5 = (bf16[512,128]{1,0:T(8,128)(2,1)S(1)}, bf16[512,128]{1,0:T(8,128)(2,1)S(1)}, u32[]{:S(2)}, u32[]{:S(2)}) collective-permute-start(bf16[512,128]{1,0:T(8,128)(2,1)S(1)} %get-tuple-element.19.refs_0_), channel_id=1, source_target_pairs={{0,24},{1,25},{2,26},{3,27},{4,28},{5,29},{6,30},{7,31},{8,16},{9,... | collective-permute-start | bytes 393224 | tf_op jit(solution)/shard_map/ppermute | solution.py:248
  95.2 8.1 %copy-start.5 = (f32[1,128,128]{2,1,0:T(8,128)S(1)}, f32[1,128,128]{2,1,0:T(8,128)}, u32[]{:S(2)}) copy-start(f32[1,128,128]{2,1,0:T(8,128)} %param.8) | copy-start | bytes 196612
  95.8 5.3 %collective-permute-start.24 = (bf16[128,128]{1,0:T(8,128)(2,1)S(1)}, bf16[128,128]{1,0:T(8,128)(2,1)S(1)}, u32[]{:S(2)}, u32[]{:S(2)}) collective-permute-start(bf16[128,128]{1,0:T(8,128)(2,1)S(1)} %get-tuple-element.25), channel_id=1, source_target_pairs={{0,8},{1,9},{2,10},{3,11},{4,12},{5,13},{6,14},{7,15},{8,0},{9,1},... | collective-permute-start | bytes 98312 | tf_op jit(solution)/shard_map/ppermute | solution.py:248
  97.9 3.9 %collective-permute-start.25 = (bf16[128,128]{1,0:T(8,128)(2,1)S(1)}, bf16[128,128]{1,0:T(8,128)(2,1)S(1)}, u32[]{:S(2)}, u32[]{:S(2)}) collective-permute-start(bf16[128,128]{1,0:T(8,128)(2,1)S(1)} %get-tuple-element.25), channel_id=1, source_target_pairs={{0,16},{1,17},{2,18},{3,19},{4,20},{5,21},{6,22},{7,23},{8,24},{9,... | collective-permute-start | bytes 98312 | tf_op jit(solution)/shard_map/ppermute | solution.py:248
  98.5 4.8 %collective-permute-start.26 = (bf16[128,128]{1,0:T(8,128)(2,1)S(1)}, bf16[128,128]{1,0:T(8,128)(2,1)S(1)}, u32[]{:S(2)}, u32[]{:S(2)}) collective-permute-start(bf16[128,128]{1,0:T(8,128)(2,1)S(1)} %get-tuple-element.25), channel_id=1, source_target_pairs={{0,24},{1,25},{2,26},{3,27},{4,28},{5,29},{6,30},{7,31},{8,16},{9,... | collective-permute-start | bytes 98312 | tf_op jit(solution)/shard_map/ppermute | solution.py:248
where the time goes:
time: 104 us
  waiting for transfers between devices  41.2 us (40%)
  starting transfers between devices  38.5 us (37%)
  Pallas kernels  17.6 us (17%)
  local copies, waits for them, and re-layouts  4.68 us (4%)
  other arithmetic  1.07 us (1%)
    ppermute x27, waiting for transfers between devices, swap(): return lax.ppermute(x, AXES, pairs)  41.2 us
    ppermute x27, starting transfers between devices, swap(): return lax.ppermute(x, AXES, pairs)  38.5 us
    pallas_call x4, Pallas kernels, partial_product(): pl.pallas_call(functools.partial(partial_kernel, n, q, min(rows, 512)), o...  12.2 us
    unnamed x12, local copies, waits for them, and re-layouts  4.68 us
  transfers between devices with their start and end apart: 27, of which 14 were waited for; matrix products, arithmetic and copies ran while one was open for 0% of the time, Pallas kernels for 14%

commit v1 on v0

--- a/solution.py
+++ b/solution.py
@@ -13,6 +13,7 @@
 VMEM = pltpu.VMEM
 SMEM = pltpu.SMEM
 LIMIT = 24 << 20
+HALVES = 2
 
 
 def whole(space):
@@ -117,88 +118,112 @@
             pltpu.SemaphoreType.DMA((n,)),
             pltpu.SemaphoreType.DMA((n,)),
         ],
+        compiler_params=pltpu.CompilerParams(vmem_limit_bytes=LIMIT),
         cost_estimate=pl.CostEstimate(flops=0, bytes_accessed=4 * n * shape[0] * shape[1], transcendentals=0),
-        compiler_params=pltpu.CompilerParams(vmem_limit_bytes=LIMIT),
         name="pick",
     )(*pieces)
 
 
-def partial_kernel(n, q, step, *refs):
-    ins, tiles, out, held, came = refs[:n], refs[n : n + q], refs[n + q], refs[n + q + 1], refs[n + q + 2]
+def partial_kernel(n, q, halves, step, *refs):
+    ins, tiles = refs[:n], refs[n : n + q]
+    outs, held, came = refs[n + q : -2], refs[-2], refs[-1]
     p = lax.axis_index("prow")
     core = lax.axis_index("pcol") % q
-    part = ins[0].shape[0]
+    chunks, part, width = ins[0].shape
     take = [
-        pltpu.make_async_copy(ins[a], held.at[pl.ds(pl.multiple_of((a ^ p) * part, part), part), :], came.at[a])
+        pltpu.make_async_copy(
+            ins[a].at[k],
+            held.at[pl.ds(pl.multiple_of((a ^ p) * part, part), part), k * width : (k + 1) * width],
+            came.at[a * chunks + k],
+        )
         for a in range(n)
+        for k in range(chunks)
     ]
     for x in take:
         x.start()
     for x in take:
         x.wait()
     rows, depth = tiles[0].shape
-    for i in range(rows // step):
-        total = None
-        for e in range(q):
-            right = held[pl.ds(pl.multiple_of((core ^ e) * depth, depth), depth), :]
-            term = jnp.dot(tiles[e][i * step : (i + 1) * step, :], right, preferred_element_type=jnp.float32)
-            total = term if total is None else total + term
-        out[i * step : (i + 1) * step, :] = total.astype(out.dtype)
-
-
-def partial_product(n, q, pieces, tiles, dtype):
-    part, width = pieces[0].shape
+    tall = rows // HALVES
+    for i, h in enumerate(halves):
+        for r in range(tall // step):
+            base = h * tall + r * step
+            total = None
+            for e in range(q):
+                right = held[pl.ds(pl.multiple_of((core ^ e) * depth, depth), depth), :]
+                term = jnp.dot(tiles[e][base : base + step, :], right, preferred_element_type=jnp.float32)
+                total = term if total is None else total + term
+            for k in range(chunks):
+                outs[k * len(halves) + i][r * step : (r + 1) * step, :] = total[:, k * width : (k + 1) * width].astype(
+                    jnp.bfloat16
+                )
+
+
+def partial_product(n, q, halves, pieces, tiles):
+    chunks, part, width = pieces[0].shape
     rows, depth = tiles[0].shape
-    return pl.pallas_call(
-        functools.partial(partial_kernel, n, q, min(rows, 512)),
-        out_shape=jax.ShapeDtypeStruct((rows, width), dtype),
+    tall = rows // HALVES
+    outs = pl.pallas_call(
+        functools.partial(partial_kernel, n, q, halves, min(tall, 512)),
+        out_shape=[jax.ShapeDtypeStruct((tall, width), jnp.bfloat16)] * (chunks * len(halves)),
         in_specs=[whole(pl.ANY)] * n + [whole(VMEM)] * q,
-        out_specs=whole(VMEM),
-        scratch_shapes=[pltpu.VMEM((n * part, width), jnp.bfloat16), pltpu.SemaphoreType.DMA((n,))],
+        out_specs=[whole(VMEM)] * (chunks * len(halves)),
+        scratch_shapes=[
+            pltpu.VMEM((n * part, chunks * width), jnp.bfloat16),
+            pltpu.SemaphoreType.DMA((n * chunks,)),
+        ],
         compiler_params=pltpu.CompilerParams(vmem_limit_bytes=LIMIT),
         cost_estimate=pl.CostEstimate(
-            flops=2 * rows * width * depth * q, bytes_accessed=2 * q * rows * depth, transcendentals=0
+            flops=2 * tall * len(halves) * width * chunks * depth * q,
+            bytes_accessed=2 * q * tall * len(halves) * depth,
+            transcendentals=0,
         ),
         name="partial_product",
     )(*pieces, *tiles)
-
-
-def diagonal_kernel(count, lhat, *refs):
-    parts, product, diag, sent = refs[:count], refs[count], refs[count + 1], refs[count + 2]
-    rows, _ = lhat.shape
-    step = min(rows, 512)
+    return [list(outs[k * len(halves) : (k + 1) * len(halves)]) for k in range(chunks)]
+
+
+def diagonal_kernel(lhat, *refs):
+    ins, product, diag, sent = refs[:-3], refs[-3], refs[-2], refs[-1]
+    count = len(ins) // HALVES
+    tall = ins[0].shape[0]
+    step = min(tall, 512)
     total = None
-    for i in range(rows // step):
-        here = slice(i * step, (i + 1) * step)
-        x = parts[0][here, :].astype(jnp.float32)
-        for r in parts[1:]:
-            x = x + r[here, :].astype(jnp.float32)
-        x = x.T
-        product[:, here] = x
-        high = x.astype(jnp.bfloat16)
-        low = (x - high.astype(jnp.float32)).astype(jnp.bfloat16)
-        for y in (high, low):
-            term = jnp.dot(y, lhat[here, :], preferred_element_type=jnp.float32)
-            total = term if total is None else total + term
+    for h in range(HALVES):
+        first, *came = ins[h * count : (h + 1) * count]
+        for r in range(tall // step):
+            here = slice(r * step, (r + 1) * step)
+            there = slice(h * tall + r * step, h * tall + (r + 1) * step)
+            x = first[here, :].astype(jnp.float32)
+            for y in came:
+                x = x + y[here, :].astype(jnp.float32)
+            x = x.T
+            product[:, there] = x
+            high = x.astype(jnp.bfloat16)
+            low = (x - high.astype(jnp.float32)).astype(jnp.bfloat16)
+            for y in (high, low):
+                term = jnp.dot(y, lhat[there, :], preferred_element_type=jnp.float32)
+                total = term if total is None else total + term
     diag[...] = total
     sent[...] = total.astype(jnp.bfloat16)
 
 
 def diagonal(lhat, parts):
     rows, width = lhat.shape
-    return pl.pallas_call(
-        functools.partial(diagonal_kernel, len(parts)),
+    ins = [x for half in parts for x in half]
+    return pl.pallas_call(
+        diagonal_kernel,
         out_shape=[
             jax.ShapeDtypeStruct((width, rows), jnp.float32),
             jax.ShapeDtypeStruct((width, width), jnp.float32),
             jax.ShapeDtypeStruct((width, width), jnp.bfloat16),
         ],
-        in_specs=[whole(VMEM)] * (1 + len(parts)),
+        in_specs=[whole(VMEM)] * (1 + len(ins)),
         out_specs=[whole(VMEM)] * 3,
         compiler_params=pltpu.CompilerParams(vmem_limit_bytes=LIMIT),
         cost_estimate=pl.CostEstimate(flops=4 * rows * width * width, bytes_accessed=10 * rows * width, transcendentals=0),
         name="diagonal",
-    )(lhat, *parts)
+    )(lhat, *ins)
 
 
 def masked_kernel(listed, product, off):
@@ -257,25 +282,34 @@
 
     scattered = [pieces[0]] + [over_rows(pieces[a], a) for a in range(1, n)]
     chosen = pick(n, q, scattered)
+
+    mine = [chosen[0]] + [swap(chosen[m], lambda p, z, k: (p, z ^ m, k)) for m in range(1, n)]
     chunk = [None] * n
-    for m in reversed(range(n)):
-        mine = chosen[m] if m == 0 else swap(chosen[m], lambda p, z, k: (p, z ^ m, k))
-        quarters = [mine] + [over_rows(mine, a) for a in range(1, n)]
-        chunk[m] = partial_product(n, q, quarters, tiles, jnp.float32 if m == 0 else jnp.bfloat16)
+    for i, group in enumerate(groups(n)):
+        load_ = jnp.stack([mine[m] for m in group])
+        quarters = [load_] + [over_rows(load_, a) for a in range(1, n)]
+        if i == 1:
+            chunk[group[0]] = []
+            for h in range(HALVES):
+                chunk[group[0]] += partial_product(n, q, (h,), quarters, tiles)[0]
+        else:
+            done = partial_product(n, q, tuple(range(HALVES)), quarters, tiles)
+            for m, x in zip(group, done):
+                chunk[m] = x
 
     z_here = lax.axis_index("pcol") // q
 
-    def own(odd, d):
+    def own(odd, d, h):
         at_mask = {}
         for z in range(n):
             to = z + d if (z % 2) == odd else z - d
             if 0 <= to < n:
                 at_mask.setdefault(z ^ to, []).append(z)
         masks = sorted(at_mask)
-        x = chunk[masks[0]]
+        x = chunk[masks[0]][h]
         for m in masks[1:]:
             here = functools.reduce(jnp.logical_or, [z_here == z for z in at_mask[m]])
-            x = jnp.where(here, chunk[m], x)
+            x = jnp.where(here, chunk[m][h], x)
         return x
 
     def add(x, y):
@@ -283,26 +317,32 @@
             return x
         return (x.astype(jnp.float32) + y.astype(jnp.float32)).astype(jnp.bfloat16)
 
-    came = [None, None]
+    came = [[None, None] for _ in range(HALVES)]
     for d in range(n - 1, 0, -1):
-        sent = [None, None]
-        for odd in (0, 1):
-            pairs = line_pairs(n, d, odd)
-            if not pairs:
-                continue
-            to = {}
-            for z in pairs:
-                to[z], to[z + 1] = z + 1, z
-            load_ = add(own(odd, d), came[1 - odd])
-            sent[odd] = swap(load_, lambda p, z, k: (p, to[z], k) if z in to else None)
-        came = sent
-
-    product, part, travel = diagonal(lhat, [chunk[0]] + [x for x in came if x is not None])
+        for h in range(HALVES):
+            sent = [None, None]
+            for odd in (0, 1):
+                pairs = line_pairs(n, d, odd)
+                if not pairs:
+                    continue
+                to = {}
+                for z in pairs:
+                    to[z], to[z + 1] = z + 1, z
+                load_ = add(own(odd, d, h), came[h][1 - odd])
+                sent[odd] = swap(load_, lambda p, z, k: (p, to[z], k) if z in to else None)
+            came[h] = sent
+
+    parts = [[chunk[0][h]] + [x for x in came[h] if x is not None] for h in range(HALVES)]
+    product, part, travel = diagonal(lhat, parts)
     off = masked(listed, product)
     total = part
     for a in range(1, n):
         total = total + over_rows(travel, a).astype(jnp.float32)
     return off, pivot_inverse + total[None]
+
+
+def groups(n):
+    return [[0], [n - 1]] + [[m for m in (b, b - 1) if m > 0] for b in range(n - 2, 0, -2)]
 
 
 def line_pairs(n, d, odd):

time: 104 us -> 108 us (1.038)
  starting transfers between devices: 38.5 us -> 51.5 us
  waiting for transfers between devices: 41.2 us -> 34 us
  Pallas kernels: 17.6 us -> 15 us
    ppermute x27 -> x29, starting transfers between devices: 38.5 us -> 51.5 us  [swap(): return lax.ppermute(x, AXES, pairs)]
    ppermute x27 -> x29, waiting for transfers between devices: 41.2 us -> 34 us  [swap(): return lax.ppermute(x, AXES, pairs)]
    pallas_call x5, Pallas kernels: 12.7 us -> 10 us  [the longest x4 9.51 us: partial_product(): pl.pallas_call(functools.partial(partial_kernel, n, q, halves, min(tall,...]
  transfers between devices with their start and end apart: 27 -> 29, of which waited for: 14 -> 13; matrix products, arithmetic and copies ran while one was open for 0% -> 0% of each run, Pallas kernels for 14% -> 13%
where the time goes in v1:
time: 108 us; the launch traced here: 107 us
  starting transfers between devices  51.5 us (48%)
  waiting for transfers between devices  34 us (31%)
  Pallas kernels  15 us (14%)
  local copies, waits for them, and re-layouts  4.68 us (4%)
  other arithmetic  1.11 us (1%)
    ppermute x29, starting transfers between devices, swap(): return lax.ppermute(x, AXES, pairs)  51.5 us
    ppermute x29, waiting for transfers between devices, swap(): return lax.ppermute(x, AXES, pairs)  34 us
    pallas_call x4, Pallas kernels, partial_product(): pl.pallas_call(functools.partial(partial_kernel, n, q, halves, min(tall,...  9.51 us
    unnamed x12, local copies, waits for them, and re-layouts  4.68 us
  transfers between devices with their start and end apart: 29, of which 13 were waited for; matrix products, arithmetic and copies ran while one was open for 0% of the time, Pallas kernels for 13%

profile of v1, /device:TPU:0, one launch (start us, length us, event | category | flops | bytes accessed | tf_op | source)
XLA Modules:
  0.0 107.2 jit_solution(11198126148887610036)
XLA Ops:
  0.6 0.6 collective-permute-start.6
  1.2 1.0 copy-done.1
  2.2 0.8 copy-done.2
  3.0 0.7 copy-done.3
  3.7 1.6 %normalize.1 = (bf16[512,128]{1,0:T(8,128)(2,1)S(1)}, bf16[512,128]{1,0:T(8,128)(2,1)S(1)}, bf16[512,128]{1,0:T(8,128)(2,1)S(1)}, bf16[512,128]{1,0:T(8,128)(2,1)S(1)}, bf16[2048,128]{1,0:T(8,128)(2,1)S(1)}) custom-call(s32[8,64]{1,0:T(8,128)S(1)} %copy-done.3, bf16[2048,128]{1,0:T(8,128)(2,1)S(1)} %copy-done.1, bf16[1,128,128]{2,1,0:T(8,128)(2,1)S(1)} %copy-done.2), custom_call_target="tpu_custom_call" | custom-call | flops 67108864 | bytes 1572864 | tf_op jit(solution)/shard_map/normalize/pallas_call | solution.py:57
  5.2 2.6 %collective-permute-start = (bf16[512,128]{1,0:T(8,128)(2,1)S(1)}, bf16[512,128]{1,0:T(8,128)(2,1)S(1)}, u32[]{:S(2)}, u32[]{:S(2)}) collective-permute-start(bf16[512,128]{1,0:T(8,128)(2,1)S(1)} %get-tuple-element.22), channel_id=1, source_target_pairs={{0,8},{1,9},{2,10},{3,11},{4,12},{5,13},{6,14},{7,15},{8,0},{9,1},... | collective-permute-start | bytes 393224 | tf_op jit(solution)/shard_map/ppermute | solution.py:273
  7.8 1.5 %collective-permute-start.1 = (bf16[512,128]{1,0:T(8,128)(2,1)S(1)}, bf16[512,128]{1,0:T(8,128)(2,1)S(1)}, u32[]{:S(2)}, u32[]{:S(2)}) collective-permute-start(bf16[512,128]{1,0:T(8,128)(2,1)S(1)} %get-tuple-element.23), channel_id=1, source_target_pairs={{0,16},{1,17},{2,18},{3,19},{4,20},{5,21},{6,22},{7,23},{8,24},{9,... | collective-permute-start | bytes 393224 | tf_op jit(solution)/shard_map/ppermute | solution.py:273
  9.3 0.0 collective-permute-start.2
  9.3 2.8 %collective-permute-done.refs_1_ = bf16[512,128]{1,0:T(8,128)(2,1)S(1)} collective-permute-done((bf16[512,128]{1,0:T(8,128)(2,1)S(1)}, bf16[512,128]{1,0:T(8,128)(2,1)S(1)}, u32[]{:S(2)}, u32[]{:S(2)}) %collective-permute-start) | collective-permute-done | bytes 131104 | tf_op jit(solution)/shard_map/ppermute | solution.py:273
  12.1 4.1 %collective-permute-done.1.refs_2_ = bf16[512,128]{1,0:T(8,128)(2,1)S(1)} collective-permute-done((bf16[512,128]{1,0:T(8,128)(2,1)S(1)}, bf16[512,128]{1,0:T(8,128)(2,1)S(1)}, u32[]{:S(2)}, u32[]{:S(2)}) %collective-permute-start.1) | collective-permute-done | bytes 131104 | tf_op jit(solution)/shard_map/ppermute | solution.py:273
  16.2 1.4 %pick.1 = (bf16[512,128]{1,0:T(8,128)(2,1)S(1)}, bf16[512,128]{1,0:T(8,128)(2,1)S(1)}, bf16[512,128]{1,0:T(8,128)(2,1)S(1)}, bf16[512,128]{1,0:T(8,128)(2,1)S(1)}) custom-call(bf16[512,128]{1,0:T(8,128)(2,1)S(1)} %get-tuple-element.21.refs_0_, bf16[512,128]{1,0:T(8,128)(2,1)S(1)} %collective-permute-done.refs_1_, ...), custom_call_target="tpu_custom_call" | custom-call | bytes 1048576 | tf_op jit(solution)/shard_map/pick/pallas_call | solution.py:111
  17.6 2.7 %collective-permute-start.7 = (bf16[512,128]{1,0:T(8,128)(2,1)S(1)}, bf16[512,128]{1,0:T(8,128)(2,1)S(1)}, u32[]{:S(2)}, u32[]{:S(2)}) collective-permute-start(bf16[512,128]{1,0:T(8,128)(2,1)S(1)} %get-tuple-element.27), channel_id=1, source_target_pairs={{0,4},{1,5},{2,6},{3,7},{4,0},{5,1},{6,2},{7,3},{8,12},{9,13},{10,... | collective-permute-start | bytes 393224 | tf_op jit(solution)/shard_map/ppermute | solution.py:273
  20.3 1.6 %collective-permute-start.8 = (bf16[512,128]{1,0:T(8,128)(2,1)S(1)}, bf16[512,128]{1,0:T(8,128)(2,1)S(1)}, u32[]{:S(2)}, u32[]{:S(2)}) collective-permute-start(bf16[512,128]{1,0:T(8,128)(2,1)S(1)} %get-tuple-element.28), channel_id=1, source_target_pairs={{0,2},{1,3},{2,0},{3,1},{4,6},{5,7},{6,4},{7,5},{8,10},{9,11},{10,... | collective-permute-start | bytes 393224 | tf_op jit(solution)/shard_map/ppermute | solution.py:273
  21.9 4.2 %collective-permute-done.7 = bf16[512,128]{1,0:T(8,128)(2,1)S(1)} collective-permute-done((bf16[512,128]{1,0:T(8,128)(2,1)S(1)}, bf16[512,128]{1,0:T(8,128)(2,1)S(1)}, u32[]{:S(2)}, u32[]{:S(2)}) %collective-permute-start.7) | collective-permute-done | bytes 131104 | tf_op jit(solution)/shard_map/ppermute | solution.py:273
  26.1 0.3 collective-permute-done.8
  26.5 1.7 %collective-permute-start.10 = (bf16[2,512,128]{2,1,0:T(8,128)(2,1)S(1)}, bf16[2,512,128]{2,1,0:T(8,128)(2,1)S(1)}, u32[]{:S(2)}, u32[]{:S(2)}) collective-permute-start(bf16[2,512,128]{2,1,0:T(8,128)(2,1)S(1)} %pad_maximum_fusion.refs_0_), channel_id=1, source_target_pairs={{0,16},{1,17},{2,18},{3,19},{4,20},{5,21},{6,22},{7,23},{8,24},{9,... | collective-permute-start | bytes 786440 | tf_op jit(solution)/shard_map/ppermute | solution.py:273
  28.1 1.4 %collective-permute-start.11 = (bf16[2,512,128]{2,1,0:T(8,128)(2,1)S(1)}, bf16[2,512,128]{2,1,0:T(8,128)(2,1)S(1)}, u32[]{:S(2)}, u32[]{:S(2)}) collective-permute-start(bf16[2,512,128]{2,1,0:T(8,128)(2,1)S(1)} %pad_maximum_fusion.refs_0_), channel_id=1, source_target_pairs={{0,24},{1,25},{2,26},{3,27},{4,28},{5,29},{6,30},{7,31},{8,16},{9,... | collective-permute-start | bytes 786440 | tf_op jit(solution)/shard_map/ppermute | solution.py:273
  29.6 0.4 collective-permute-start.9
  30.0 2.2 %copy-done = bf16[2048,1024]{1,0:T(8,128)(2,1)S(1)} copy-done((bf16[2048,1024]{1,0:T(8,128)(2,1)S(1)}, bf16[2048,1024]{1,0:T(8,128)(2,1)}, u32[]{:S(2)}) %copy-start) | copy-done | bytes 4194328
  32.2 0.3 load.1.refs_4_
  32.5 3.2 %collective-permute-start.12 = (bf16[512,128]{1,0:T(8,128)(2,1)S(1)}, bf16[512,128]{1,0:T(8,128)(2,1)S(1)}, u32[]{:S(2)}, u32[]{:S(2)}) collective-permute-start(bf16[512,128]{1,0:T(8,128)(2,1)S(1)} %get-tuple-element.31), channel_id=1, source_target_pairs={{0,6},{1,7},{2,4},{3,5},{4,2},{5,3},{6,0},{7,1},{8,14},{9,15},{10,... | collective-permute-start | bytes 393224 | tf_op jit(solution)/shard_map/ppermute | solution.py:273
  35.7 2.3 %collective-permute-done.10.refs_2_ = bf16[2,512,128]{2,1,0:T(8,128)(2,1)S(1)} collective-permute-done((bf16[2,512,128]{2,1,0:T(8,128)(2,1)S(1)}, bf16[2,512,128]{2,1,0:T(8,128)(2,1)S(1)}, u32[]{:S(2)}, u32[]{:S(2)}) %collective-permute-start.10) | collective-permute-done | bytes 262176 | tf_op jit(solution)/shard_map/ppermute | solution.py:273
  38.0 1.3 %collective-permute-done.9.refs_1_ = bf16[2,512,128]{2,1,0:T(8,128)(2,1)S(1)} collective-permute-done((bf16[2,512,128]{2,1,0:T(8,128)(2,1)S(1)}, bf16[2,512,128]{2,1,0:T(8,128)(2,1)S(1)}, u32[]{:S(2)}, u32[]{:S(2)}) %collective-permute-start.9) | collective-permute-done | bytes 262176 | tf_op jit(solution)/shard_map/ppermute | solution.py:273
  39.3 2.6 %partial_product.5 = (bf16[1024,128]{1,0:T(8,128)(2,1)S(1)}, bf16[1024,128]{1,0:T(8,128)(2,1)S(1)}, bf16[1024,128]{1,0:T(8,128)(2,1)S(1)}, bf16[1024,128]{1,0:T(8,128)(2,1)S(1)}) custom-call(bf16[2,512,128]{2,1,0:T(8,128)(2,1)S(1)} %pad_maximum_fusion.refs_0_, bf16[2,512,128]{2,1,0:T(8,128)(2,1)S(1)} %collective-permute-done.9.refs_1_, ...), custom_call_target="tpu_custom_call" | custom-call | flops 2147483648 | bytes 8388608 | tf_op jit(solution)/shard_map/partial_product/pallas_call | solution.py:166
  41.9 2.5 %collective-permute-start.24 = (bf16[1024,128]{1,0:T(8,128)(2,1)S(1)}, bf16[1024,128]{1,0:T(8,128)(2,1)S(1)}, u32[]{:S(2)}, u32[]{:S(2)}) collective-permute-start(bf16[1024,128]{1,0:T(8,128)(2,1)S(1)} %get-tuple-element.34), channel_id=1, source_target_pairs={{0,2},{1,3},{2,0},{3,1},{4,6},{5,7},{6,4},{7,5},{8,10},{9,11},{10,... | collective-permute-start | bytes 786440 | tf_op jit(solution)/shard_map/ppermute | solution.py:273
  44.4 1.8 %collective-permute-start.13 = (bf16[1,512,128]{2,1,0:T(8,128)(2,1)S(1)}, bf16[1,512,128]{2,1,0:T(8,128)(2,1)S(1)}, u32[]{:S(2)}, u32[]{:S(2)}) collective-permute-start(bf16[1,512,128]{2,1,0:T(8,128)(2,1)S(1)} %bitcast.6), channel_id=1, source_target_pairs={{0,8},{1,9},{2,10},{3,11},{4,12},{5,13},{6,14},{7,15},{8,0},{9,1},... | collective-permute-start | bytes 393224 | tf_op jit(solution)/shard_map/ppermute | solution.py:273
  46.2 0.4 collective-permute-start.14
  46.6 1.3 %collective-permute-start.15 = (bf16[1,512,128]{2,1,0:T(8,128)(2,1)S(1)}, bf16[1,512,128]{2,1,0:T(8,128)(2,1)S(1)}, u32[]{:S(2)}, u32[]{:S(2)}) collective-permute-start(bf16[1,512,128]{2,1,0:T(8,128)(2,1)S(1)} %bitcast.8), channel_id=1, source_target_pairs={{0,24},{1,25},{2,26},{3,27},{4,28},{5,29},{6,30},{7,31},{8,16},{9,... | collective-permute-start | bytes 393224 | tf_op jit(solution)/shard_map/ppermute | solution.py:273
  47.9 1.8 %collective-permute-start.3 = (bf16[1,512,128]{2,1,0:T(8,128)(2,1)S(1)}, bf16[1,512,128]{2,1,0:T(8,128)(2,1)S(1)}, u32[]{:S(2)}, u32[]{:S(2)}) collective-permute-start(bf16[1,512,128]{2,1,0:T(8,128)(2,1)S(1)} %bitcast.11), channel_id=1, source_target_pairs={{0,8},{1,9},{2,10},{3,11},{4,12},{5,13},{6,14},{7,15},{8,0},{9,1},... | collective-permute-start | bytes 393224 | tf_op jit(solution)/shard_map/ppermute | solution.py:273
  49.7 1.1 collective-permute-done.13.refs_1_
  50.8 1.1 %collective-permute-start.4 = (bf16[1,512,128]{2,1,0:T(8,128)(2,1)S(1)}, bf16[1,512,128]{2,1,0:T(8,128)(2,1)S(1)}, u32[]{:S(2)}, u32[]{:S(2)}) collective-permute-start(bf16[1,512,128]{2,1,0:T(8,128)(2,1)S(1)} %bitcast.12), channel_id=1, source_target_pairs={{0,16},{1,17},{2,18},{3,19},{4,20},{5,21},{6,22},{7,23},{8,24},{9,... | collective-permute-start | bytes 393224 | tf_op jit(solution)/shard_map/ppermute | solution.py:273
  51.9 1.3 %collective-permute-done.14.refs_2_ = bf16[1,512,128]{2,1,0:T(8,128)(2,1)S(1)} collective-permute-done((bf16[1,512,128]{2,1,0:T(8,128)(2,1)S(1)}, bf16[1,512,128]{2,1,0:T(8,128)(2,1)S(1)}, u32[]{:S(2)}, u32[]{:S(2)}) %collective-permute-start.14) | collective-permute-done | bytes 131104 | tf_op jit(solution)/shard_map/ppermute | solution.py:273
  53.2 1.9 %partial_product.7 = bf16[1024,128]{1,0:T(8,128)(2,1)S(1)} custom-call(bf16[1,512,128]{2,1,0:T(8,128)(2,1)S(1)} %bitcast.9, bf16[1,512,128]{2,1,0:T(8,128)(2,1)S(1)} %collective-permute-done.13.refs_1_, bf16[1,512,128]{2,1,0:T(8,128)(2,1)S(1)} %collective-permute-done.14.refs_2_, bf16[1,512,128]{2,1,0:T(8,128)(2,1)S(1)} %collective-permute-done.15.refs_3_, ...), custom_call_target="tpu_custom_call" | custom-call | flops 536870912 | bytes 4194304 | tf_op jit(solution)/shard_map/partial_product/pallas_call | solution.py:166
  55.1 0.4 collective-permute-start.21
  55.6 1.7 %collective-permute-start.19 = (bf16[1024,128]{1,0:T(8,128)(2,1)S(1)}, bf16[1024,128]{1,0:T(8,128)(2,1)S(1)}, u32[]{:S(2)}, u32[]{:S(2)}) collective-permute-start(bf16[1024,128]{1,0:T(8,128)(2,1)S(1)} %get-tuple-element.30), channel_id=1, source_target_pairs={{0,2},{1,3},{2,0},{3,1},{4,6},{5,7},{6,4},{7,5},{8,10},{9,11},{10,... | collective-permute-start | bytes 786440 | tf_op jit(solution)/shard_map/ppermute | solution.py:273
  57.2 1.9 %partial_product.6 = bf16[1024,128]{1,0:T(8,128)(2,1)S(1)} custom-call(bf16[1,512,128]{2,1,0:T(8,128)(2,1)S(1)} %bitcast.10, bf16[1,512,128]{2,1,0:T(8,128)(2,1)S(1)} %collective-permute-done.13.refs_1_, bf16[1,512,128]{2,1,0:T(8,128)(2,1)S(1)} %collective-permute-done.14.refs_2_, bf16[1,512,128]{2,1,0:T(8,128)(2,1)S(1)} %collective-permute-done.15.refs_3_, ...), custom_call_target="tpu_custom_call" | custom-call | flops 536870912 | bytes 4194304 | tf_op jit(solution)/shard_map/partial_product/pallas_call | solution.py:166
  59.2 0.4 collective-permute-start.16
  59.6 0.1 add_convert_fusion
  59.7 4.7 %collective-permute-done.21 = bf16[1024,128]{1,0:T(8,128)(2,1)S(1)} collective-permute-done((bf16[1024,128]{1,0:T(8,128)(2,1)S(1)}, bf16[1024,128]{1,0:T(8,128)(2,1)S(1)}, u32[]{:S(2)}, u32[]{:S(2)}) %collective-permute-start.21) | collective-permute-done | bytes 262176 | tf_op jit(solution)/shard_map/ppermute | solution.py:273
  64.4 0.7 collective-permute-start.25
  65.1 0.1 add_convert_fusion.2
  65.1 5.4 %collective-permute-done.16 = bf16[1024,128]{1,0:T(8,128)(2,1)S(1)} collective-permute-done((bf16[1024,128]{1,0:T(8,128)(2,1)S(1)}, bf16[1024,128]{1,0:T(8,128)(2,1)S(1)}, u32[]{:S(2)}, u32[]{:S(2)}) %collective-permute-start.16) | collective-permute-done | bytes 262176 | tf_op jit(solution)/shard_map/ppermute | solution.py:273
  70.6 0.7 collective-permute-start.22
  71.2 0.1 add_convert_fusion.5
  71.3 0.7 collective-permute-start.17
  72.0 0.1 add_convert_fusion.3
  72.1 0.7 collective-permute-start.20
  72.8 0.1 add_convert_fusion.1
  72.9 16.6 %collective-permute-start.23 = (bf16[1024,128]{1,0:T(8,128)(2,1)S(1)}, bf16[1024,128]{1,0:T(8,128)(2,1)S(1)}, u32[]{:S(2)}, u32[]{:S(2)}) collective-permute-start(bf16[1024,128]{1,0:T(8,128)(2,1)S(1)} %add_convert_fusion.1), channel_id=1, source_target_pairs={{0,2},{1,3},{2,0},{3,1},{4,6},{5,7},{6,4},{7,5},{8,10},{9,11},{10,... | collective-permute-start | bytes 786440 | tf_op jit(solution)/shard_map/ppermute | solution.py:273
  89.5 0.1 add_convert_fusion.4
  89.6 0.0 copy-start.4
  89.6 0.1 collective-permute-start.18
  89.7 1.5 %collective-permute-start.5 = (bf16[1,512,128]{2,1,0:T(8,128)(2,1)S(1)}, bf16[1,512,128]{2,1,0:T(8,128)(2,1)S(1)}, u32[]{:S(2)}, u32[]{:S(2)}) collective-permute-start(bf16[1,512,128]{2,1,0:T(8,128)(2,1)S(1)} %bitcast.13), channel_id=1, source_target_pairs={{0,24},{1,25},{2,26},{3,27},{4,28},{5,29},{6,30},{7,31},{8,16},{9,... | collective-permute-start | bytes 393224 | tf_op jit(solution)/shard_map/ppermute | solution.py:273
  91.2 4.8 %collective-permute-done.5.refs_3_ = bf16[1,512,128]{2,1,0:T(8,128)(2,1)S(1)} collective-permute-done((bf16[1,512,128]{2,1,0:T(8,128)(2,1)S(1)}, bf16[1,512,128]{2,1,0:T(8,128)(2,1)S(1)}, u32[]{:S(2)}, u32[]{:S(2)}) %collective-permute-start.5) | collective-permute-done | bytes 131104 | tf_op jit(solution)/shard_map/ppermute | solution.py:273
  96.0 3.0 %partial_product.4 = (bf16[1024,128]{1,0:T(8,128)(2,1)S(1)}, bf16[1024,128]{1,0:T(8,128)(2,1)S(1)}) custom-call(bf16[1,512,128]{2,1,0:T(8,128)(2,1)S(1)} %bitcast.14, bf16[1,512,128]{2,1,0:T(8,128)(2,1)S(1)} %collective-permute-done.3.refs_1_, bf16[1,512,128]{2,1,0:T(8,128)(2,1)S(1)} %collective-permute-done.4.refs_2_, ...), custom_call_target="tpu_custom_call" | custom-call | flops 1073741824 | bytes 8388608 | tf_op jit(solution)/shard_map/partial_product/pallas_call | solution.py:166
  99.0 0.0 copy-start.5
  99.1 0.5 diagonal.1
  99.6 1.5 %collective-permute-start.26 = (bf16[128,128]{1,0:T(8,128)(2,1)S(1)}, bf16[128,128]{1,0:T(8,128)(2,1)S(1)}, u32[]{:S(2)}, u32[]{:S(2)}) collective-permute-start(bf16[128,128]{1,0:T(8,128)(2,1)S(1)} %get-tuple-element.37), channel_id=1, source_target_pairs={{0,8},{1,9},{2,10},{3,11},{4,12},{5,13},{6,14},{7,15},{8,0},{9,1},... | collective-permute-start | bytes 98312 | tf_op jit(solution)/shard_map/ppermute | solution.py:273
  101.1 0.6 collective-permute-start.27
  101.7 1.5 %collective-permute-start.28 = (bf16[128,128]{1,0:T(8,128)(2,1)S(1)}, bf16[128,128]{1,0:T(8,128)(2,1)S(1)}, u32[]{:S(2)}, u32[]{:S(2)}) collective-permute-start(bf16[128,128]{1,0:T(8,128)(2,1)S(1)} %get-tuple-element.37), channel_id=1, source_target_pairs={{0,24},{1,25},{2,26},{3,27},{4,28},{5,29},{6,30},{7,31},{8,16},{9,... | collective-permute-start | bytes 98312 | tf_op jit(solution)/shard_map/ppermute | solution.py:273
  103.2 1.7 %masked.1 = f32[128,2048]{1,0:T(8,128)} custom-call(s32[8,64]{1,0:T(8,128)S(1)} %copy-done.4, f32[128,2048]{1,0:T(8,128)S(1)} %get-tuple-element.35.product), custom_call_target="tpu_custom_call" | custom-call | flops 524288 | bytes 2097152 | tf_op jit(solution)/shard_map/masked/pallas_call | solution.py:244
  104.8 0.1 collective-permute-done.27
  105.0 1.5 %collective-permute-done.28 = bf16[128,128]{1,0:T(8,128)(2,1)S(1)} collective-permute-done((bf16[128,128]{1,0:T(8,128)(2,1)S(1)}, bf16[128,128]{1,0:T(8,128)(2,1)S(1)}, u32[]{:S(2)}, u32[]{:S(2)}) %collective-permute-start.28) | collective-permute-done | bytes 32800 | tf_op jit(solution)/shard_map/ppermute | solution.py:273
  106.5 0.7 bitcast_add_fusion
  (23 shorter events, 0.1 us)
Async XLA Ops:
  0.6 38.6 %collective-permute-start.6 = (bf16[2048,1024]{1,0:T(8,128)(2,1)}, bf16[2048,1024]{1,0:T(8,128)(2,1)S(1)}, u32[]{:S(2)}, u32[]{:S(2)}) collective-permute-start(bf16[2048,1024]{1,0:T(8,128)(2,1)} %tile.1), channel_id=1, source_target_pairs={{0,1},{1,0},{2,3},{3,2},{4,5},{5,4},{6,7},{7,6},{8,9},{9,8},{10,11... | collective-permute-start | bytes 12582920 | tf_op jit(solution)/shard_map/ppermute | solution.py:273
  1.2 1.0 copy-start.1
  2.2 0.8 copy-start.2
  3.0 0.7 copy-start.3
  5.2 6.9 %collective-permute-start = (bf16[512,128]{1,0:T(8,128)(2,1)S(1)}, bf16[512,128]{1,0:T(8,128)(2,1)S(1)}, u32[]{:S(2)}, u32[]{:S(2)}) collective-permute-start(bf16[512,128]{1,0:T(8,128)(2,1)S(1)} %get-tuple-element.22), channel_id=1, source_target_pairs={{0,8},{1,9},{2,10},{3,11},{4,12},{5,13},{6,14},{7,15},{8,0},{9,1},... | collective-permute-start | bytes 393224 | tf_op jit(solution)/shard_map/ppermute | solution.py:273
  7.8 8.4 %collective-permute-start.1 = (bf16[512,128]{1,0:T(8,128)(2,1)S(1)}, bf16[512,128]{1,0:T(8,128)(2,1)S(1)}, u32[]{:S(2)}, u32[]{:S(2)}) collective-permute-start(bf16[512,128]{1,0:T(8,128)(2,1)S(1)} %get-tuple-element.23), channel_id=1, source_target_pairs={{0,16},{1,17},{2,18},{3,19},{4,20},{5,21},{6,22},{7,23},{8,24},{9,... | collective-permute-start | bytes 393224 | tf_op jit(solution)/shard_map/ppermute | solution.py:273
  9.3 6.9 %collective-permute-start.2 = (bf16[512,128]{1,0:T(8,128)(2,1)S(1)}, bf16[512,128]{1,0:T(8,128)(2,1)S(1)}, u32[]{:S(2)}, u32[]{:S(2)}) collective-permute-start(bf16[512,128]{1,0:T(8,128)(2,1)S(1)} %get-tuple-element.24), channel_id=1, source_target_pairs={{0,24},{1,25},{2,26},{3,27},{4,28},{5,29},{6,30},{7,31},{8,16},{9,... | collective-permute-start | bytes 393224 | tf_op jit(solution)/shard_map/ppermute | solution.py:273
  17.6 8.4 %collective-permute-start.7 = (bf16[512,128]{1,0:T(8,128)(2,1)S(1)}, bf16[512,128]{1,0:T(8,128)(2,1)S(1)}, u32[]{:S(2)}, u32[]{:S(2)}) collective-permute-start(bf16[512,128]{1,0:T(8,128)(2,1)S(1)} %get-tuple-element.27), channel_id=1, source_target_pairs={{0,4},{1,5},{2,6},{3,7},{4,0},{5,1},{6,2},{7,3},{8,12},{9,13},{10,... | collective-permute-start | bytes 393224 | tf_op jit(solution)/shard_map/ppermute | solution.py:273
  20.3 6.1 %collective-permute-start.8 = (bf16[512,128]{1,0:T(8,128)(2,1)S(1)}, bf16[512,128]{1,0:T(8,128)(2,1)S(1)}, u32[]{:S(2)}, u32[]{:S(2)}) collective-permute-start(bf16[512,128]{1,0:T(8,128)(2,1)S(1)} %get-tuple-element.28), channel_id=1, source_target_pairs={{0,2},{1,3},{2,0},{3,1},{4,6},{5,7},{6,4},{7,5},{8,10},{9,11},{10,... | collective-permute-start | bytes 393224 | tf_op jit(solution)/shard_map/ppermute | solution.py:273
  26.5 11.5 %collective-permute-start.10 = (bf16[2,512,128]{2,1,0:T(8,128)(2,1)S(1)}, bf16[2,512,128]{2,1,0:T(8,128)(2,1)S(1)}, u32[]{:S(2)}, u32[]{:S(2)}) collective-permute-start(bf16[2,512,128]{2,1,0:T(8,128)(2,1)S(1)} %pad_maximum_fusion.refs_0_), channel_id=1, source_target_pairs={{0,16},{1,17},{2,18},{3,19},{4,20},{5,21},{6,22},{7,23},{8,24},{9,... | collective-permute-start | bytes 786440 | tf_op jit(solution)/shard_map/ppermute | solution.py:273
  28.1 9.9 %collective-permute-start.11 = (bf16[2,512,128]{2,1,0:T(8,128)(2,1)S(1)}, bf16[2,512,128]{2,1,0:T(8,128)(2,1)S(1)}, u32[]{:S(2)}, u32[]{:S(2)}) collective-permute-start(bf16[2,512,128]{2,1,0:T(8,128)(2,1)S(1)} %pad_maximum_fusion.refs_0_), channel_id=1, source_target_pairs={{0,24},{1,25},{2,26},{3,27},{4,28},{5,29},{6,30},{7,31},{8,16},{9,... | collective-permute-start | bytes 786440 | tf_op jit(solution)/shard_map/ppermute | solution.py:273
  29.6 9.7 %collective-permute-start.9 = (bf16[2,512,128]{2,1,0:T(8,128)(2,1)S(1)}, bf16[2,512,128]{2,1,0:T(8,128)(2,1)S(1)}, u32[]{:S(2)}, u32[]{:S(2)}) collective-permute-start(bf16[2,512,128]{2,1,0:T(8,128)(2,1)S(1)} %pad_maximum_fusion.refs_0_), channel_id=1, source_target_pairs={{0,8},{1,9},{2,10},{3,11},{4,12},{5,13},{6,14},{7,15},{8,0},{9,1},... | collective-permute-start | bytes 786440 | tf_op jit(solution)/shard_map/ppermute | solution.py:273
  30.0 2.2 %copy-start = (bf16[2048,1024]{1,0:T(8,128)(2,1)S(1)}, bf16[2048,1024]{1,0:T(8,128)(2,1)}, u32[]{:S(2)}) copy-start(bf16[2048,1024]{1,0:T(8,128)(2,1)} %tile.1) | copy-start | bytes 12582916
  32.5 11.9 %collective-permute-start.12 = (bf16[512,128]{1,0:T(8,128)(2,1)S(1)}, bf16[512,128]{1,0:T(8,128)(2,1)S(1)}, u32[]{:S(2)}, u32[]{:S(2)}) collective-permute-start(bf16[512,128]{1,0:T(8,128)(2,1)S(1)} %get-tuple-element.31), channel_id=1, source_target_pairs={{0,6},{1,7},{2,4},{3,5},{4,2},{5,3},{6,0},{7,1},{8,14},{9,15},{10,... | collective-permute-start | bytes 393224 | tf_op jit(solution)/shard_map/ppermute | solution.py:273
  41.9 17.3 %collective-permute-start.24 = (bf16[1024,128]{1,0:T(8,128)(2,1)S(1)}, bf16[1024,128]{1,0:T(8,128)(2,1)S(1)}, u32[]{:S(2)}, u32[]{:S(2)}) collective-permute-start(bf16[1024,128]{1,0:T(8,128)(2,1)S(1)} %get-tuple-element.34), channel_id=1, source_target_pairs={{0,2},{1,3},{2,0},{3,1},{4,6},{5,7},{6,4},{7,5},{8,10},{9,11},{10,... | collective-permute-start | bytes 786440 | tf_op jit(solution)/shard_map/ppermute | solution.py:273
  44.4 6.4 %collective-permute-start.13 = (bf16[1,512,128]{2,1,0:T(8,128)(2,1)S(1)}, bf16[1,512,128]{2,1,0:T(8,128)(2,1)S(1)}, u32[]{:S(2)}, u32[]{:S(2)}) collective-permute-start(bf16[1,512,128]{2,1,0:T(8,128)(2,1)S(1)} %bitcast.6), channel_id=1, source_target_pairs={{0,8},{1,9},{2,10},{3,11},{4,12},{5,13},{6,14},{7,15},{8,0},{9,1},... | collective-permute-start | bytes 393224 | tf_op jit(solution)/shard_map/ppermute | solution.py:273
  46.2 7.0 %collective-permute-start.14 = (bf16[1,512,128]{2,1,0:T(8,128)(2,1)S(1)}, bf16[1,512,128]{2,1,0:T(8,128)(2,1)S(1)}, u32[]{:S(2)}, u32[]{:S(2)}) collective-permute-start(bf16[1,512,128]{2,1,0:T(8,128)(2,1)S(1)} %bitcast.7), channel_id=1, source_target_pairs={{0,16},{1,17},{2,18},{3,19},{4,20},{5,21},{6,22},{7,23},{8,24},{9,... | collective-permute-start | bytes 393224 | tf_op jit(solution)/shard_map/ppermute | solution.py:273
  46.6 6.6 %collective-permute-start.15 = (bf16[1,512,128]{2,1,0:T(8,128)(2,1)S(1)}, bf16[1,512,128]{2,1,0:T(8,128)(2,1)S(1)}, u32[]{:S(2)}, u32[]{:S(2)}) collective-permute-start(bf16[1,512,128]{2,1,0:T(8,128)(2,1)S(1)} %bitcast.8), channel_id=1, source_target_pairs={{0,24},{1,25},{2,26},{3,27},{4,28},{5,29},{6,30},{7,31},{8,16},{9,... | collective-permute-start | bytes 393224 | tf_op jit(solution)/shard_map/ppermute | solution.py:273
  47.9 41.7 %collective-permute-start.3 = (bf16[1,512,128]{2,1,0:T(8,128)(2,1)S(1)}, bf16[1,512,128]{2,1,0:T(8,128)(2,1)S(1)}, u32[]{:S(2)}, u32[]{:S(2)}) collective-permute-start(bf16[1,512,128]{2,1,0:T(8,128)(2,1)S(1)} %bitcast.11), channel_id=1, source_target_pairs={{0,8},{1,9},{2,10},{3,11},{4,12},{5,13},{6,14},{7,15},{8,0},{9,1},... | collective-permute-start | bytes 393224 | tf_op jit(solution)/shard_map/ppermute | solution.py:273
  50.8 38.9 %collective-permute-start.4 = (bf16[1,512,128]{2,1,0:T(8,128)(2,1)S(1)}, bf16[1,512,128]{2,1,0:T(8,128)(2,1)S(1)}, u32[]{:S(2)}, u32[]{:S(2)}) collective-permute-start(bf16[1,512,128]{2,1,0:T(8,128)(2,1)S(1)} %bitcast.12), channel_id=1, source_target_pairs={{0,16},{1,17},{2,18},{3,19},{4,20},{5,21},{6,22},{7,23},{8,24},{9,... | collective-permute-start | bytes 393224 | tf_op jit(solution)/shard_map/ppermute | solution.py:273
  55.1 9.2 %collective-permute-start.21 = (bf16[1024,128]{1,0:T(8,128)(2,1)S(1)}, bf16[1024,128]{1,0:T(8,128)(2,1)S(1)}, u32[]{:S(2)}, u32[]{:S(2)}) collective-permute-start(bf16[1024,128]{1,0:T(8,128)(2,1)S(1)} %partial_product.7), channel_id=1, source_target_pairs={{0,2},{1,3},{2,0},{3,1},{4,6},{5,7},{6,4},{7,5},{8,10},{9,11},{10,... | collective-permute-start | bytes 786440 | tf_op jit(solution)/shard_map/ppermute | solution.py:273
  55.6 15.7 %collective-permute-start.19 = (bf16[1024,128]{1,0:T(8,128)(2,1)S(1)}, bf16[1024,128]{1,0:T(8,128)(2,1)S(1)}, u32[]{:S(2)}, u32[]{:S(2)}) collective-permute-start(bf16[1024,128]{1,0:T(8,128)(2,1)S(1)} %get-tuple-element.30), channel_id=1, source_target_pairs={{0,2},{1,3},{2,0},{3,1},{4,6},{5,7},{6,4},{7,5},{8,10},{9,11},{10,... | collective-permute-start | bytes 786440 | tf_op jit(solution)/shard_map/ppermute | solution.py:273
  59.2 11.4 %collective-permute-start.16 = (bf16[1024,128]{1,0:T(8,128)(2,1)S(1)}, bf16[1024,128]{1,0:T(8,128)(2,1)S(1)}, u32[]{:S(2)}, u32[]{:S(2)}) collective-permute-start(bf16[1024,128]{1,0:T(8,128)(2,1)S(1)} %partial_product.6), channel_id=1, source_target_pairs={{0,2},{1,3},{2,0},{3,1},{4,6},{5,7},{6,4},{7,5},{8,10},{9,11},{10,... | collective-permute-start | bytes 786440 | tf_op jit(solution)/shard_map/ppermute | solution.py:273
  64.4 34.6 %collective-permute-start.25 = (bf16[1024,128]{1,0:T(8,128)(2,1)S(1)}, bf16[1024,128]{1,0:T(8,128)(2,1)S(1)}, u32[]{:S(2)}, u32[]{:S(2)}) collective-permute-start(bf16[1024,128]{1,0:T(8,128)(2,1)S(1)} %add_convert_fusion), channel_id=1, source_target_pairs={{2,4},{3,5},{4,2},{5,3},{10,12},{11,13},{12,10},{13,11},{18,20},{1... | collective-permute-start | bytes 786440 | tf_op jit(solution)/shard_map/ppermute | solution.py:273
  70.6 1.5 %collective-permute-start.22 = (bf16[1024,128]{1,0:T(8,128)(2,1)S(1)}, bf16[1024,128]{1,0:T(8,128)(2,1)S(1)}, u32[]{:S(2)}, u32[]{:S(2)}) collective-permute-start(bf16[1024,128]{1,0:T(8,128)(2,1)S(1)} %add_convert_fusion.2), channel_id=1, source_target_pairs={{2,4},{3,5},{4,2},{5,3},{10,12},{11,13},{12,10},{13,11},{18,20},{1... | collective-permute-start | bytes 786440 | tf_op jit(solution)/shard_map/ppermute | solution.py:273
  71.3 1.5 %collective-permute-start.17 = (bf16[1024,128]{1,0:T(8,128)(2,1)S(1)}, bf16[1024,128]{1,0:T(8,128)(2,1)S(1)}, u32[]{:S(2)}, u32[]{:S(2)}) collective-permute-start(bf16[1024,128]{1,0:T(8,128)(2,1)S(1)} %add_convert_fusion.5), channel_id=1, source_target_pairs={{2,4},{3,5},{4,2},{5,3},{10,12},{11,13},{12,10},{13,11},{18,20},{1... | collective-permute-start | bytes 786440 | tf_op jit(solution)/shard_map/ppermute | solution.py:273
  72.1 26.9 %collective-permute-start.20 = (bf16[1024,128]{1,0:T(8,128)(2,1)S(1)}, bf16[1024,128]{1,0:T(8,128)(2,1)S(1)}, u32[]{:S(2)}, u32[]{:S(2)}) collective-permute-start(bf16[1024,128]{1,0:T(8,128)(2,1)S(1)} %add_convert_fusion.3), channel_id=1, source_target_pairs={{2,4},{3,5},{4,2},{5,3},{10,12},{11,13},{12,10},{13,11},{18,20},{1... | collective-permute-start | bytes 786440 | tf_op jit(solution)/shard_map/ppermute | solution.py:273
  72.9 26.2 %collective-permute-start.23 = (bf16[1024,128]{1,0:T(8,128)(2,1)S(1)}, bf16[1024,128]{1,0:T(8,128)(2,1)S(1)}, u32[]{:S(2)}, u32[]{:S(2)}) collective-permute-start(bf16[1024,128]{1,0:T(8,128)(2,1)S(1)} %add_convert_fusion.1), channel_id=1, source_target_pairs={{0,2},{1,3},{2,0},{3,1},{4,6},{5,7},{6,4},{7,5},{8,10},{9,11},{10,... | collective-permute-start | bytes 786440 | tf_op jit(solution)/shard_map/ppermute | solution.py:273
  89.6 13.6 %copy-start.4 = (s32[8,64]{1,0:T(8,128)S(1)}, s32[8,64]{1,0:T(8,128)}, u32[]{:S(2)}) copy-start(s32[8,64]{1,0:T(8,128)} %listed.3) | copy-start | bytes 6148
  89.6 9.4 %collective-permute-start.18 = (bf16[1024,128]{1,0:T(8,128)(2,1)S(1)}, bf16[1024,128]{1,0:T(8,128)(2,1)S(1)}, u32[]{:S(2)}, u32[]{:S(2)}) collective-permute-start(bf16[1024,128]{1,0:T(8,128)(2,1)S(1)} %add_convert_fusion.4), channel_id=1, source_target_pairs={{0,2},{1,3},{2,0},{3,1},{4,6},{5,7},{6,4},{7,5},{8,10},{9,11},{10,... | collective-permute-start | bytes 786440 | tf_op jit(solution)/shard_map/ppermute | solution.py:273
  89.7 6.3 %collective-permute-start.5 = (bf16[1,512,128]{2,1,0:T(8,128)(2,1)S(1)}, bf16[1,512,128]{2,1,0:T(8,128)(2,1)S(1)}, u32[]{:S(2)}, u32[]{:S(2)}) collective-permute-start(bf16[1,512,128]{2,1,0:T(8,128)(2,1)S(1)} %bitcast.13), channel_id=1, source_target_pairs={{0,24},{1,25},{2,26},{3,27},{4,28},{5,29},{6,30},{7,31},{8,16},{9,... | collective-permute-start | bytes 393224 | tf_op jit(solution)/shard_map/ppermute | solution.py:273
  99.0 7.5 %copy-start.5 = (f32[1,128,128]{2,1,0:T(8,128)S(1)}, f32[1,128,128]{2,1,0:T(8,128)}, u32[]{:S(2)}) copy-start(f32[1,128,128]{2,1,0:T(8,128)} %param.8) | copy-start | bytes 196612
  99.6 5.2 %collective-permute-start.26 = (bf16[128,128]{1,0:T(8,128)(2,1)S(1)}, bf16[128,128]{1,0:T(8,128)(2,1)S(1)}, u32[]{:S(2)}, u32[]{:S(2)}) collective-permute-start(bf16[128,128]{1,0:T(8,128)(2,1)S(1)} %get-tuple-element.37), channel_id=1, source_target_pairs={{0,8},{1,9},{2,10},{3,11},{4,12},{5,13},{6,14},{7,15},{8,0},{9,1},... | collective-permute-start | bytes 98312 | tf_op jit(solution)/shard_map/ppermute | solution.py:273
  101.1 3.9 %collective-permute-start.27 = (bf16[128,128]{1,0:T(8,128)(2,1)S(1)}, bf16[128,128]{1,0:T(8,128)(2,1)S(1)}, u32[]{:S(2)}, u32[]{:S(2)}) collective-permute-start(bf16[128,128]{1,0:T(8,128)(2,1)S(1)} %get-tuple-element.37), channel_id=1, source_target_pairs={{0,16},{1,17},{2,18},{3,19},{4,20},{5,21},{6,22},{7,23},{8,24},{9,... | collective-permute-start | bytes 98312 | tf_op jit(solution)/shard_map/ppermute | solution.py:273
  101.7 4.8 %collective-permute-start.28 = (bf16[128,128]{1,0:T(8,128)(2,1)S(1)}, bf16[128,128]{1,0:T(8,128)(2,1)S(1)}, u32[]{:S(2)}, u32[]{:S(2)}) collective-permute-start(bf16[128,128]{1,0:T(8,128)(2,1)S(1)} %get-tuple-element.37), channel_id=1, source_target_pairs={{0,24},{1,25},{2,26},{3,27},{4,28},{5,29},{6,30},{7,31},{8,16},{9,... | collective-permute-start | bytes 98312 | tf_op jit(solution)/shard_map/ppermute | solution.py:273

commit v2 on v1

--- a/solution.py
+++ b/solution.py
@@ -13,6 +13,7 @@
 VMEM = pltpu.VMEM
 SMEM = pltpu.SMEM
 LIMIT = 24 << 20
+FULL = 62 << 20
 HALVES = 2
 
 
@@ -65,7 +66,7 @@
             pltpu.SMEM((1, listed.shape[1]), jnp.int32),
             pltpu.SemaphoreType.DMA((n + 2,)),
         ],
-        compiler_params=pltpu.CompilerParams(vmem_limit_bytes=LIMIT),
+        compiler_params=pltpu.CompilerParams(vmem_limit_bytes=FULL),
         cost_estimate=pl.CostEstimate(flops=2 * rows * width * width, bytes_accessed=6 * rows * width, transcendentals=0),
         name="normalize",
     )(listed, panel, unit)
@@ -91,19 +92,14 @@
 
 
 def pick_kernel(n, q, *refs):
-    ins, outs, held, came, left = refs[:n], refs[n : 2 * n], refs[2 * n], refs[2 * n + 1], refs[2 * n + 2]
-    p = lax.axis_index("prow")
-    z = lax.axis_index("pcol") // q
-    take = [pltpu.make_async_copy(ins[a], held.at[a], came.at[a]) for a in range(n)]
-    for x in take:
-        x.start()
-    for x in take:
-        x.wait()
-    give = [pltpu.make_async_copy(held.at[p ^ z ^ m], outs[m], left.at[m]) for m in reversed(range(n))]
-    for x in give:
-        x.start()
-    for x in give:
-        x.wait()
+    ins, outs = refs[:n], refs[n:]
+    at = lax.axis_index("prow") ^ (lax.axis_index("pcol") // q)
+    for b in range(n):
+
+        @pl.when(at == b)
+        def _():
+            for m in range(n):
+                outs[m][...] = ins[b ^ m][...]
 
 
 def pick(n, q, pieces):
@@ -111,13 +107,8 @@
     return pl.pallas_call(
         functools.partial(pick_kernel, n, q),
         out_shape=[jax.ShapeDtypeStruct(shape, jnp.bfloat16)] * n,
-        in_specs=[whole(pl.ANY)] * n,
-        out_specs=[whole(pl.ANY)] * n,
-        scratch_shapes=[
-            pltpu.VMEM((n,) + shape, jnp.bfloat16),
-            pltpu.SemaphoreType.DMA((n,)),
-            pltpu.SemaphoreType.DMA((n,)),
-        ],
+        in_specs=[whole(VMEM)] * n,
+        out_specs=[whole(VMEM)] * n,
         compiler_params=pltpu.CompilerParams(vmem_limit_bytes=LIMIT),
         cost_estimate=pl.CostEstimate(flops=0, bytes_accessed=4 * n * shape[0] * shape[1], transcendentals=0),
         name="pick",
@@ -126,23 +117,13 @@
 
 def partial_kernel(n, q, halves, step, *refs):
     ins, tiles = refs[:n], refs[n : n + q]
-    outs, held, came = refs[n + q : -2], refs[-2], refs[-1]
+    outs, held = refs[n + q : -1], refs[-1]
     p = lax.axis_index("prow")
     core = lax.axis_index("pcol") % q
     chunks, part, width = ins[0].shape
-    take = [
-        pltpu.make_async_copy(
-            ins[a].at[k],
-            held.at[pl.ds(pl.multiple_of((a ^ p) * part, part), part), k * width : (k + 1) * width],
-            came.at[a * chunks + k],
-        )
-        for a in range(n)
-        for k in range(chunks)
-    ]
-    for x in take:
-        x.start()
-    for x in take:
-        x.wait()
+    for a in range(n):
+        for k in range(chunks):
+            held[pl.ds(pl.multiple_of((a ^ p) * part, part), part), k * width : (k + 1) * width] = ins[a][k]
     rows, depth = tiles[0].shape
     tall = rows // HALVES
     for i, h in enumerate(halves):
@@ -166,12 +147,9 @@
     outs = pl.pallas_call(
         functools.partial(partial_kernel, n, q, halves, min(tall, 512)),
         out_shape=[jax.ShapeDtypeStruct((tall, width), jnp.bfloat16)] * (chunks * len(halves)),
-        in_specs=[whole(pl.ANY)] * n + [whole(VMEM)] * q,
+        in_specs=[whole(VMEM)] * (n + q),
         out_specs=[whole(VMEM)] * (chunks * len(halves)),
-        scratch_shapes=[
-            pltpu.VMEM((n * part, chunks * width), jnp.bfloat16),
-            pltpu.SemaphoreType.DMA((n * chunks,)),
-        ],
+        scratch_shapes=[pltpu.VMEM((n * part, chunks * width), jnp.bfloat16)],
         compiler_params=pltpu.CompilerParams(vmem_limit_bytes=LIMIT),
         cost_estimate=pl.CostEstimate(
             flops=2 * tall * len(halves) * width * chunks * depth * q,
@@ -181,6 +159,43 @@
         name="partial_product",
     )(*pieces, *tiles)
     return [list(outs[k * len(halves) : (k + 1) * len(halves)]) for k in range(chunks)]
+
+
+def piece_kernel(n, q, which, base, step, *refs):
+    ins, tiles = refs[: len(which)], refs[len(which) : len(which) + q]
+    before, out = refs[len(which) + q : -1], refs[-1]
+    p = lax.axis_index("prow")
+    core = lax.axis_index("pcol") % q
+    _, part, _ = ins[0].shape
+    each = n // q
+    for r in range(out.shape[0] // step):
+        here = slice(r * step, (r + 1) * step)
+        there = slice(base + r * step, base + (r + 1) * step)
+        total = before[0][there, :] if before else None
+        for a, piece in zip(which, ins):
+            g = a ^ p
+            columns = pl.ds(pl.multiple_of((g % each) * part, part), part)
+            left = tiles[0][there, columns]
+            for e in range(1, q):
+                left = jnp.where((core ^ e) == g // each, tiles[e][there, columns], left)
+            term = jnp.dot(left, piece[0], preferred_element_type=jnp.float32)
+            total = term if total is None else total + term
+        out[here, :] = total.astype(out.dtype)
+
+
+def piece_product(n, q, which, pieces, tiles, base, tall, before, dtype):
+    _, part, width = pieces[0].shape
+    return pl.pallas_call(
+        functools.partial(piece_kernel, n, q, which, base, min(tall, 512)),
+        out_shape=jax.ShapeDtypeStruct((tall, width), dtype),
+        in_specs=[whole(VMEM)] * (len(which) + q + len(before)),
+        out_specs=whole(VMEM),
+        compiler_params=pltpu.CompilerParams(vmem_limit_bytes=LIMIT),
+        cost_estimate=pl.CostEstimate(
+            flops=2 * tall * width * part * len(which), bytes_accessed=2 * tall * part * len(which), transcendentals=0
+        ),
+        name="piece_product",
+    )(*pieces, *tiles, *before)
 
 
 def diagonal_kernel(lhat, *refs):
@@ -289,9 +304,13 @@
         load_ = jnp.stack([mine[m] for m in group])
         quarters = [load_] + [over_rows(load_, a) for a in range(1, n)]
         if i == 1:
+            rows = inverse_tile.shape[0]
+            most = piece_product(n, q, range(n - 1), quarters[:-1], tiles, 0, rows, [], jnp.float32)
             chunk[group[0]] = []
             for h in range(HALVES):
-                chunk[group[0]] += partial_product(n, q, (h,), quarters, tiles)[0]
+                tall = rows // HALVES
+                x = piece_product(n, q, [n - 1], quarters[-1:], tiles, h * tall, tall, [most], jnp.bfloat16)
+                chunk[group[0]].append(x)
         else:
             done = partial_product(n, q, tuple(range(HALVES)), quarters, tiles)
             for m, x in zip(group, done):
@@ -342,7 +361,7 @@
 
 
 def groups(n):
-    return [[0], [n - 1]] + [[m for m in (b, b - 1) if m > 0] for b in range(n - 2, 0, -2)]
+    return [[0], [n - 1]] + [[m] for m in range(n - 2, 0, -1)]
 
 
 def line_pairs(n, d, odd):

time: 108 us -> 111 us (1.028)
  Pallas kernels: 15 us -> 28.1 us
  waiting for transfers between devices: 34 us -> 28.6 us
  starting transfers between devices: 51.5 us -> 48.8 us
  local copies, waits for them, and re-layouts: 4.68 us -> 3.11 us
    pallas_call x0 -> x3, Pallas kernels: none -> 9.27 us  [piece_product(): pl.pallas_call(functools.partial(piece_kernel, n, q, which, base, min(tal...]
    ppermute x29 -> x32, waiting for transfers between devices: 34 us -> 28.6 us  [swap(): return lax.ppermute(x, AXES, pairs)]
    pallas_call x4 -> x3, Pallas kernels: 9.51 us -> 13.7 us  [partial_product(): pl.pallas_call(functools.partial(partial_kernel, n, q, halves, min(tall,...]
    ppermute x29 -> x32, starting transfers between devices: 51.5 us -> 48.8 us  [swap(): return lax.ppermute(x, AXES, pairs)]
    unnamed x12 -> x10, local copies, waits for them, and re-layouts: 4.68 us -> 3.11 us
    pallas_call x1, Pallas kernels: 1.41 us -> 0.04 us  [pick(): pl.pallas_call(functools.partial(pick_kernel, n, q), out_shape=[jax.Shape...]
  transfers between devices with their start and end apart: 29 -> 32, of which waited for: 13 -> 8; matrix products, arithmetic and copies ran while one was open for 0% -> 0% of each run, Pallas kernels for 13% -> 25%
where the time goes in v2:
time: 111 us
  starting transfers between devices  48.8 us (44%)
  waiting for transfers between devices  28.6 us (26%)
  Pallas kernels  28.1 us (25%)
  local copies, waits for them, and re-layouts  3.11 us (3%)
    ppermute x32, starting transfers between devices, swap(): return lax.ppermute(x, AXES, pairs)  48.8 us
    ppermute x32, waiting for transfers between devices, swap(): return lax.ppermute(x, AXES, pairs)  28.6 us
    pallas_call x3, Pallas kernels, partial_product(): pl.pallas_call(functools.partial(partial_kernel, n, q, halves, min(tall,...  13.7 us
    pallas_call x3, Pallas kernels, piece_product(): pl.pallas_call(functools.partial(piece_kernel, n, q, which, base, min(tal...  9.27 us
    unnamed x10, local copies, waits for them, and re-layouts  3.11 us
    pallas_call x1, Pallas kernels, normalize(): pl.pallas_call(functools.partial(normalize_kernel, n), out_shape=shapes,...  2.62 us
  transfers between devices with their start and end apart: 32, of which 8 were waited for; matrix products, arithmetic and copies ran while one was open for 0% of the time, Pallas kernels for 25%

profile of v2, /device:TPU:0, one launch (start us, length us, event | category | flops | bytes accessed | tf_op | source)
XLA Modules:
  0.0 110.7 jit_solution(17012386984154614430)
XLA Ops:
  0.6 0.6 collective-permute-start.6
  1.2 2.6 %normalize.1 = (bf16[512,128]{1,0:T(8,128)(2,1)}, bf16[512,128]{1,0:T(8,128)(2,1)}, bf16[512,128]{1,0:T(8,128)(2,1)}, bf16[512,128]{1,0:T(8,128)(2,1)}, bf16[2048,128]{1,0:T(8,128)(2,1)}) custom-call(s32[8,64]{1,0:T(8,128)} %listed.3, bf16[2048,128]{1,0:T(8,128)(2,1)} %panel.1, bf16[1,128,128]{2,1,0:T(8,128)(2,1)} %unit.1), custom_call_target="tpu_custom_call" | custom-call | flops 67108864 | bytes 1572864 | tf_op jit(solution)/shard_map/normalize/pallas_call | solution.py:58
  3.8 2.6 %collective-permute-start = (bf16[512,128]{1,0:T(8,128)(2,1)}, bf16[512,128]{1,0:T(8,128)(2,1)S(1)}, u32[]{:S(2)}, u32[]{:S(2)}) collective-permute-start(bf16[512,128]{1,0:T(8,128)(2,1)} %get-tuple-element.22), channel_id=1, source_target_pairs={{0,8},{1,9},{2,10},{3,11},{4,12},{5,13},{6,14},{7,15},{8,0},{9,1},... | collective-permute-start | bytes 393224 | tf_op jit(solution)/shard_map/ppermute | solution.py:288
  6.4 1.5 %collective-permute-start.1 = (bf16[512,128]{1,0:T(8,128)(2,1)}, bf16[512,128]{1,0:T(8,128)(2,1)S(1)}, u32[]{:S(2)}, u32[]{:S(2)}) collective-permute-start(bf16[512,128]{1,0:T(8,128)(2,1)} %get-tuple-element.23), channel_id=1, source_target_pairs={{0,16},{1,17},{2,18},{3,19},{4,20},{5,21},{6,22},{7,23},{8,24},{9,... | collective-permute-start | bytes 393224 | tf_op jit(solution)/shard_map/ppermute | solution.py:288
  7.9 0.0 collective-permute-start.2
  7.9 3.0 %collective-permute-done.refs_1_ = bf16[512,128]{1,0:T(8,128)(2,1)S(1)} collective-permute-done((bf16[512,128]{1,0:T(8,128)(2,1)}, bf16[512,128]{1,0:T(8,128)(2,1)S(1)}, u32[]{:S(2)}, u32[]{:S(2)}) %collective-permute-start) | collective-permute-done | bytes 131104 | tf_op jit(solution)/shard_map/ppermute | solution.py:288
  10.9 4.1 %collective-permute-done.1.refs_2_ = bf16[512,128]{1,0:T(8,128)(2,1)S(1)} collective-permute-done((bf16[512,128]{1,0:T(8,128)(2,1)}, bf16[512,128]{1,0:T(8,128)(2,1)S(1)}, u32[]{:S(2)}, u32[]{:S(2)}) %collective-permute-start.1) | collective-permute-done | bytes 131104 | tf_op jit(solution)/shard_map/ppermute | solution.py:288
  15.0 0.0 collective-permute-done.2.refs_3_
  15.0 0.9 copy-done.2
  16.0 2.6 %collective-permute-start.11 = (bf16[512,128]{1,0:T(8,128)(2,1)S(1)}, bf16[512,128]{1,0:T(8,128)(2,1)S(1)}, u32[]{:S(2)}, u32[]{:S(2)}) collective-permute-start(bf16[512,128]{1,0:T(8,128)(2,1)S(1)} %get-tuple-element.29), channel_id=1, source_target_pairs={{0,4},{1,5},{2,6},{3,7},{4,0},{5,1},{6,2},{7,3},{8,12},{9,13},{10,... | collective-permute-start | bytes 393224 | tf_op jit(solution)/shard_map/ppermute | solution.py:288
  18.6 1.4 %collective-permute-start.15 = (bf16[512,128]{1,0:T(8,128)(2,1)S(1)}, bf16[512,128]{1,0:T(8,128)(2,1)S(1)}, u32[]{:S(2)}, u32[]{:S(2)}) collective-permute-start(bf16[512,128]{1,0:T(8,128)(2,1)S(1)} %get-tuple-element.31), channel_id=1, source_target_pairs={{0,6},{1,7},{2,4},{3,5},{4,2},{5,3},{6,0},{7,1},{8,14},{9,15},{10,... | collective-permute-start | bytes 393224 | tf_op jit(solution)/shard_map/ppermute | solution.py:288
  20.0 8.4 %collective-permute-done.11 = bf16[512,128]{1,0:T(8,128)(2,1)S(1)} collective-permute-done((bf16[512,128]{1,0:T(8,128)(2,1)S(1)}, bf16[512,128]{1,0:T(8,128)(2,1)S(1)}, u32[]{:S(2)}, u32[]{:S(2)}) %collective-permute-start.11) | collective-permute-done | bytes 131104 | tf_op jit(solution)/shard_map/ppermute | solution.py:288
  28.3 1.6 %collective-permute-start.12 = (bf16[1,512,128]{2,1,0:T(8,128)(2,1)S(1)}, bf16[1,512,128]{2,1,0:T(8,128)(2,1)S(1)}, u32[]{:S(2)}, u32[]{:S(2)}) collective-permute-start(bf16[1,512,128]{2,1,0:T(8,128)(2,1)S(1)} %bitcast.18), channel_id=1, source_target_pairs={{0,8},{1,9},{2,10},{3,11},{4,12},{5,13},{6,14},{7,15},{8,0},{9,1},... | collective-permute-start | bytes 393224 | tf_op jit(solution)/shard_map/ppermute | solution.py:288
  29.9 0.5 collective-permute-start.13
  30.5 1.3 %collective-permute-start.14 = (bf16[1,512,128]{2,1,0:T(8,128)(2,1)S(1)}, bf16[1,512,128]{2,1,0:T(8,128)(2,1)S(1)}, u32[]{:S(2)}, u32[]{:S(2)}) collective-permute-start(bf16[1,512,128]{2,1,0:T(8,128)(2,1)S(1)} %bitcast.20), channel_id=1, source_target_pairs={{0,24},{1,25},{2,26},{3,27},{4,28},{5,29},{6,30},{7,31},{8,16},{9,... | collective-permute-start | bytes 393224 | tf_op jit(solution)/shard_map/ppermute | solution.py:288
  31.8 2.9 %collective-permute-done.12.refs_1_ = bf16[1,512,128]{2,1,0:T(8,128)(2,1)S(1)} collective-permute-done((bf16[1,512,128]{2,1,0:T(8,128)(2,1)S(1)}, bf16[1,512,128]{2,1,0:T(8,128)(2,1)S(1)}, u32[]{:S(2)}, u32[]{:S(2)}) %collective-permute-start.12) | collective-permute-done | bytes 131104 | tf_op jit(solution)/shard_map/ppermute | solution.py:288
  34.7 0.5 collective-permute-start.17
  35.2 1.7 %collective-permute-start.18 = (bf16[1,512,128]{2,1,0:T(8,128)(2,1)S(1)}, bf16[1,512,128]{2,1,0:T(8,128)(2,1)S(1)}, u32[]{:S(2)}, u32[]{:S(2)}) collective-permute-start(bf16[1,512,128]{2,1,0:T(8,128)(2,1)S(1)} %bitcast.15), channel_id=1, source_target_pairs={{0,16},{1,17},{2,18},{3,19},{4,20},{5,21},{6,22},{7,23},{8,24},{9,... | collective-permute-start | bytes 393224 | tf_op jit(solution)/shard_map/ppermute | solution.py:288
  36.8 2.2 %copy-done = bf16[2048,1024]{1,0:T(8,128)(2,1)S(1)} copy-done((bf16[2048,1024]{1,0:T(8,128)(2,1)S(1)}, bf16[2048,1024]{1,0:T(8,128)(2,1)}, u32[]{:S(2)}) %copy-start) | copy-done | bytes 4194328
  39.0 0.3 load.1.refs_4_.refs_3_.refs_1_
  39.3 0.0 collective-permute-done.14.refs_3_
  39.3 4.6 %partial_product.5 = (bf16[1024,128]{1,0:T(8,128)(2,1)S(1)}, bf16[1024,128]{1,0:T(8,128)(2,1)S(1)}) custom-call(bf16[1,512,128]{2,1,0:T(8,128)(2,1)S(1)} %bitcast.21, bf16[1,512,128]{2,1,0:T(8,128)(2,1)S(1)} %collective-permute-done.12.refs_1_, bf16[1,512,128]{2,1,0:T(8,128)(2,1)S(1)} %collective-permute-done.13.refs_2_, ...), custom_call_target="tpu_custom_call" | custom-call | flops 1073741824 | bytes 8388608 | tf_op jit(solution)/shard_map/partial_product/pallas_call | solution.py:147
  43.9 0.7 collective-permute-start.27
  44.6 1.1 collective-permute-start.16
  45.7 0.0 collective-permute-done.7
  45.7 1.8 %collective-permute-start.10 = (bf16[1,512,128]{2,1,0:T(8,128)(2,1)S(1)}, bf16[1,512,128]{2,1,0:T(8,128)(2,1)S(1)}, u32[]{:S(2)}, u32[]{:S(2)}) collective-permute-start(bf16[1,512,128]{2,1,0:T(8,128)(2,1)S(1)} %bitcast.10), channel_id=1, source_target_pairs={{0,24},{1,25},{2,26},{3,27},{4,28},{5,29},{6,30},{7,31},{8,16},{9,... | collective-permute-start | bytes 393224 | tf_op jit(solution)/shard_map/ppermute | solution.py:288
  47.5 1.7 %collective-permute-start.8 = (bf16[1,512,128]{2,1,0:T(8,128)(2,1)S(1)}, bf16[1,512,128]{2,1,0:T(8,128)(2,1)S(1)}, u32[]{:S(2)}, u32[]{:S(2)}) collective-permute-start(bf16[1,512,128]{2,1,0:T(8,128)(2,1)S(1)} %bitcast.11), channel_id=1, source_target_pairs={{0,8},{1,9},{2,10},{3,11},{4,12},{5,13},{6,14},{7,15},{8,0},{9,1},... | collective-permute-start | bytes 393224 | tf_op jit(solution)/shard_map/ppermute | solution.py:288
  49.2 0.0 collective-permute-done.18.refs_2_
  49.2 0.0 collective-permute-start.9
  49.2 4.0 %piece_product.3.refs_3_ = f32[2048,128]{1,0:T(8,128)S(1)} custom-call(bf16[1,512,128]{2,1,0:T(8,128)(2,1)S(1)} %bitcast.17, bf16[1,512,128]{2,1,0:T(8,128)(2,1)S(1)} %collective-permute-done.17.refs_1_, bf16[1,512,128]{2,1,0:T(8,128)(2,1)S(1)} %collective-permute-done.18.refs_2_, bf16[2048,1024]{1,0:T(8,128)(2,1)S(1)} %load.1.refs_4_.refs_3_.refs_1_, ...), custom_call_target="tpu_custom_call" | custom-call | flops 805306368 | bytes 6291456 | tf_op jit(solution)/shard_map/piece_product/pallas_call | solution.py:188
  53.2 1.9 %collective-permute-start.3 = (bf16[1,512,128]{2,1,0:T(8,128)(2,1)S(1)}, bf16[1,512,128]{2,1,0:T(8,128)(2,1)S(1)}, u32[]{:S(2)}, u32[]{:S(2)}) collective-permute-start(bf16[1,512,128]{2,1,0:T(8,128)(2,1)S(1)} %bitcast.6), channel_id=1, source_target_pairs={{0,8},{1,9},{2,10},{3,11},{4,12},{5,13},{6,14},{7,15},{8,0},{9,1},... | collective-permute-start | bytes 393224 | tf_op jit(solution)/shard_map/ppermute | solution.py:288
  55.1 2.6 %piece_product.5 = bf16[1024,128]{1,0:T(8,128)(2,1)S(1)} custom-call(bf16[1,512,128]{2,1,0:T(8,128)(2,1)S(1)} %collective-permute-done.16.refs_0_, bf16[2048,1024]{1,0:T(8,128)(2,1)S(1)} %load.1.refs_4_.refs_3_.refs_1_, bf16[2048,1024]{1,0:T(8,128)(2,1)} %collective-permute-done.6.refs_5_.refs_4_.refs_2_, f32[2048,128]{1,0:T(8,128)S(1)} %piece_product.3.refs_3_), custom_call_target="tpu_custom_call" | custom-call | flops 134217728 | bytes 1048576 | tf_op jit(solution)/shard_map/piece_product/pallas_call | solution.py:188
  57.8 0.6 collective-permute-start.4
  58.4 1.4 %collective-permute-start.24 = (bf16[1024,128]{1,0:T(8,128)(2,1)S(1)}, bf16[1024,128]{1,0:T(8,128)(2,1)S(1)}, u32[]{:S(2)}, u32[]{:S(2)}) collective-permute-start(bf16[1024,128]{1,0:T(8,128)(2,1)S(1)} %piece_product.5), channel_id=1, source_target_pairs={{0,2},{1,3},{2,0},{3,1},{4,6},{5,7},{6,4},{7,5},{8,10},{9,11},{10,... | collective-permute-start | bytes 786440 | tf_op jit(solution)/shard_map/ppermute | solution.py:288
  59.8 0.6 collective-permute-start.22
  60.4 4.6 %partial_product.4 = (bf16[1024,128]{1,0:T(8,128)(2,1)S(1)}, bf16[1024,128]{1,0:T(8,128)(2,1)S(1)}) custom-call(bf16[1,512,128]{2,1,0:T(8,128)(2,1)S(1)} %bitcast.13, bf16[1,512,128]{2,1,0:T(8,128)(2,1)S(1)} %collective-permute-done.8.refs_1_, bf16[1,512,128]{2,1,0:T(8,128)(2,1)S(1)} %collective-permute-done.9.refs_2_, ...), custom_call_target="tpu_custom_call" | custom-call | flops 1073741824 | bytes 8388608 | tf_op jit(solution)/shard_map/partial_product/pallas_call | solution.py:147
  65.0 2.6 %piece_product.4 = bf16[1024,128]{1,0:T(8,128)(2,1)S(1)} custom-call(bf16[1,512,128]{2,1,0:T(8,128)(2,1)S(1)} %collective-permute-done.16.refs_0_, bf16[2048,1024]{1,0:T(8,128)(2,1)S(1)} %load.1.refs_4_.refs_3_.refs_1_, bf16[2048,1024]{1,0:T(8,128)(2,1)} %collective-permute-done.6.refs_5_.refs_4_.refs_2_, f32[2048,128]{1,0:T(8,128)S(1)} %piece_product.3.refs_3_), custom_call_target="tpu_custom_call" | custom-call | flops 134217728 | bytes 1048576 | tf_op jit(solution)/shard_map/piece_product/pallas_call | solution.py:188
  67.6 1.5 %collective-permute-start.19 = (bf16[1024,128]{1,0:T(8,128)(2,1)S(1)}, bf16[1024,128]{1,0:T(8,128)(2,1)S(1)}, u32[]{:S(2)}, u32[]{:S(2)}) collective-permute-start(bf16[1024,128]{1,0:T(8,128)(2,1)S(1)} %piece_product.4), channel_id=1, source_target_pairs={{0,2},{1,3},{2,0},{3,1},{4,6},{5,7},{6,4},{7,5},{8,10},{9,11},{10,... | collective-permute-start | bytes 786440 | tf_op jit(solution)/shard_map/ppermute | solution.py:288
  69.1 0.1 add_convert_fusion
  69.2 0.7 collective-permute-start.28
  69.9 0.1 add_convert_fusion.2
  69.9 4.1 %collective-permute-done.19 = bf16[1024,128]{1,0:T(8,128)(2,1)S(1)} collective-permute-done((bf16[1024,128]{1,0:T(8,128)(2,1)S(1)}, bf16[1024,128]{1,0:T(8,128)(2,1)S(1)}, u32[]{:S(2)}, u32[]{:S(2)}) %collective-permute-start.19) | collective-permute-done | bytes 262176 | tf_op jit(solution)/shard_map/ppermute | solution.py:288
  74.1 0.7 collective-permute-start.25
  74.7 0.1 add_convert_fusion.5
  74.8 0.7 collective-permute-start.20
  75.5 0.1 add_convert_fusion.3
  75.6 0.7 collective-permute-start.23
  76.3 0.1 add_convert_fusion.1
  76.4 15.7 %collective-permute-start.26 = (bf16[1024,128]{1,0:T(8,128)(2,1)S(1)}, bf16[1024,128]{1,0:T(8,128)(2,1)S(1)}, u32[]{:S(2)}, u32[]{:S(2)}) collective-permute-start(bf16[1024,128]{1,0:T(8,128)(2,1)S(1)} %add_convert_fusion.1), channel_id=1, source_target_pairs={{0,2},{1,3},{2,0},{3,1},{4,6},{5,7},{6,4},{7,5},{8,10},{9,11},{10,... | collective-permute-start | bytes 786440 | tf_op jit(solution)/shard_map/ppermute | solution.py:288
  92.1 0.1 add_convert_fusion.4
  92.2 0.0 copy-start.1
  92.2 0.0 copy-start.3
  92.2 0.1 collective-permute-start.21
  92.3 1.2 %collective-permute-start.5 = (bf16[1,512,128]{2,1,0:T(8,128)(2,1)S(1)}, bf16[1,512,128]{2,1,0:T(8,128)(2,1)S(1)}, u32[]{:S(2)}, u32[]{:S(2)}) collective-permute-start(bf16[1,512,128]{2,1,0:T(8,128)(2,1)S(1)} %bitcast.8), channel_id=1, source_target_pairs={{0,24},{1,25},{2,26},{3,27},{4,28},{5,29},{6,30},{7,31},{8,16},{9,... | collective-permute-start | bytes 393224 | tf_op jit(solution)/shard_map/ppermute | solution.py:288
  93.5 4.7 %collective-permute-done.5.refs_3_ = bf16[1,512,128]{2,1,0:T(8,128)(2,1)S(1)} collective-permute-done((bf16[1,512,128]{2,1,0:T(8,128)(2,1)S(1)}, bf16[1,512,128]{2,1,0:T(8,128)(2,1)S(1)}, u32[]{:S(2)}, u32[]{:S(2)}) %collective-permute-start.5) | collective-permute-done | bytes 131104 | tf_op jit(solution)/shard_map/ppermute | solution.py:288
  98.2 4.6 %partial_product.3 = (bf16[1024,128]{1,0:T(8,128)(2,1)S(1)}, bf16[1024,128]{1,0:T(8,128)(2,1)S(1)}) custom-call(bf16[1,512,128]{2,1,0:T(8,128)(2,1)S(1)} %bitcast.9, bf16[1,512,128]{2,1,0:T(8,128)(2,1)S(1)} %collective-permute-done.3.refs_1_, bf16[1,512,128]{2,1,0:T(8,128)(2,1)S(1)} %collective-permute-done.4.refs_2_, ...), custom_call_target="tpu_custom_call" | custom-call | flops 1073741824 | bytes 8388608 | tf_op jit(solution)/shard_map/partial_product/pallas_call | solution.py:147
  102.8 0.0 copy-start.4
  102.9 0.5 diagonal.1
  103.4 1.8 %collective-permute-start.29 = (bf16[128,128]{1,0:T(8,128)(2,1)S(1)}, bf16[128,128]{1,0:T(8,128)(2,1)S(1)}, u32[]{:S(2)}, u32[]{:S(2)}) collective-permute-start(bf16[128,128]{1,0:T(8,128)(2,1)S(1)} %get-tuple-element.37), channel_id=1, source_target_pairs={{0,8},{1,9},{2,10},{3,11},{4,12},{5,13},{6,14},{7,15},{8,0},{9,1},... | collective-permute-start | bytes 98312 | tf_op jit(solution)/shard_map/ppermute | solution.py:288
  105.2 1.7 %collective-permute-start.31 = (bf16[128,128]{1,0:T(8,128)(2,1)S(1)}, bf16[128,128]{1,0:T(8,128)(2,1)S(1)}, u32[]{:S(2)}, u32[]{:S(2)}) collective-permute-start(bf16[128,128]{1,0:T(8,128)(2,1)S(1)} %get-tuple-element.37), channel_id=1, source_target_pairs={{0,24},{1,25},{2,26},{3,27},{4,28},{5,29},{6,30},{7,31},{8,16},{9,... | collective-permute-start | bytes 98312 | tf_op jit(solution)/shard_map/ppermute | solution.py:288
  107.0 1.7 %masked.1 = f32[128,2048]{1,0:T(8,128)} custom-call(s32[8,64]{1,0:T(8,128)S(1)} %copy-done.3, f32[128,2048]{1,0:T(8,128)S(1)} %get-tuple-element.35.product), custom_call_target="tpu_custom_call" | custom-call | flops 524288 | bytes 2097152 | tf_op jit(solution)/shard_map/masked/pallas_call | solution.py:259
  108.7 0.5 collective-permute-done.30
  109.1 0.9 collective-permute-done.31
  110.0 0.6 bitcast_add_fusion
  (28 shorter events, 0.1 us)
Async XLA Ops:
  0.6 38.7 %collective-permute-start.6 = (bf16[2048,1024]{1,0:T(8,128)(2,1)}, bf16[2048,1024]{1,0:T(8,128)(2,1)}, u32[]{:S(2)}, u32[]{:S(2)}) collective-permute-start(bf16[2048,1024]{1,0:T(8,128)(2,1)} %tile.1), channel_id=1, source_target_pairs={{0,1},{1,0},{2,3},{3,2},{4,5},{5,4},{6,7},{7,6},{8,9},{9,8},{10,11... | collective-permute-start | bytes 12582920 | tf_op jit(solution)/shard_map/ppermute | solution.py:288
  3.8 7.1 %collective-permute-start = (bf16[512,128]{1,0:T(8,128)(2,1)}, bf16[512,128]{1,0:T(8,128)(2,1)S(1)}, u32[]{:S(2)}, u32[]{:S(2)}) collective-permute-start(bf16[512,128]{1,0:T(8,128)(2,1)} %get-tuple-element.22), channel_id=1, source_target_pairs={{0,8},{1,9},{2,10},{3,11},{4,12},{5,13},{6,14},{7,15},{8,0},{9,1},... | collective-permute-start | bytes 393224 | tf_op jit(solution)/shard_map/ppermute | solution.py:288
  6.4 8.6 %collective-permute-start.1 = (bf16[512,128]{1,0:T(8,128)(2,1)}, bf16[512,128]{1,0:T(8,128)(2,1)S(1)}, u32[]{:S(2)}, u32[]{:S(2)}) collective-permute-start(bf16[512,128]{1,0:T(8,128)(2,1)} %get-tuple-element.23), channel_id=1, source_target_pairs={{0,16},{1,17},{2,18},{3,19},{4,20},{5,21},{6,22},{7,23},{8,24},{9,... | collective-permute-start | bytes 393224 | tf_op jit(solution)/shard_map/ppermute | solution.py:288
  7.9 7.1 %collective-permute-start.2 = (bf16[512,128]{1,0:T(8,128)(2,1)}, bf16[512,128]{1,0:T(8,128)(2,1)S(1)}, u32[]{:S(2)}, u32[]{:S(2)}) collective-permute-start(bf16[512,128]{1,0:T(8,128)(2,1)} %get-tuple-element.24), channel_id=1, source_target_pairs={{0,24},{1,25},{2,26},{3,27},{4,28},{5,29},{6,30},{7,31},{8,16},{9,... | collective-permute-start | bytes 393224 | tf_op jit(solution)/shard_map/ppermute | solution.py:288
  15.0 0.9 copy-start.2
  16.0 12.4 %collective-permute-start.11 = (bf16[512,128]{1,0:T(8,128)(2,1)S(1)}, bf16[512,128]{1,0:T(8,128)(2,1)S(1)}, u32[]{:S(2)}, u32[]{:S(2)}) collective-permute-start(bf16[512,128]{1,0:T(8,128)(2,1)S(1)} %get-tuple-element.29), channel_id=1, source_target_pairs={{0,4},{1,5},{2,6},{3,7},{4,0},{5,1},{6,2},{7,3},{8,12},{9,13},{10,... | collective-permute-start | bytes 393224 | tf_op jit(solution)/shard_map/ppermute | solution.py:288
  18.6 13.2 %collective-permute-start.15 = (bf16[512,128]{1,0:T(8,128)(2,1)S(1)}, bf16[512,128]{1,0:T(8,128)(2,1)S(1)}, u32[]{:S(2)}, u32[]{:S(2)}) collective-permute-start(bf16[512,128]{1,0:T(8,128)(2,1)S(1)} %get-tuple-element.31), channel_id=1, source_target_pairs={{0,6},{1,7},{2,4},{3,5},{4,2},{5,3},{6,0},{7,1},{8,14},{9,15},{10,... | collective-permute-start | bytes 393224 | tf_op jit(solution)/shard_map/ppermute | solution.py:288
  28.3 6.4 %collective-permute-start.12 = (bf16[1,512,128]{2,1,0:T(8,128)(2,1)S(1)}, bf16[1,512,128]{2,1,0:T(8,128)(2,1)S(1)}, u32[]{:S(2)}, u32[]{:S(2)}) collective-permute-start(bf16[1,512,128]{2,1,0:T(8,128)(2,1)S(1)} %bitcast.18), channel_id=1, source_target_pairs={{0,8},{1,9},{2,10},{3,11},{4,12},{5,13},{6,14},{7,15},{8,0},{9,1},... | collective-permute-start | bytes 393224 | tf_op jit(solution)/shard_map/ppermute | solution.py:288
  29.9 5.2 %collective-permute-start.13 = (bf16[1,512,128]{2,1,0:T(8,128)(2,1)S(1)}, bf16[1,512,128]{2,1,0:T(8,128)(2,1)S(1)}, u32[]{:S(2)}, u32[]{:S(2)}) collective-permute-start(bf16[1,512,128]{2,1,0:T(8,128)(2,1)S(1)} %bitcast.19), channel_id=1, source_target_pairs={{0,16},{1,17},{2,18},{3,19},{4,20},{5,21},{6,22},{7,23},{8,24},{9,... | collective-permute-start | bytes 393224 | tf_op jit(solution)/shard_map/ppermute | solution.py:288
  30.5 8.9 %collective-permute-start.14 = (bf16[1,512,128]{2,1,0:T(8,128)(2,1)S(1)}, bf16[1,512,128]{2,1,0:T(8,128)(2,1)S(1)}, u32[]{:S(2)}, u32[]{:S(2)}) collective-permute-start(bf16[1,512,128]{2,1,0:T(8,128)(2,1)S(1)} %bitcast.20), channel_id=1, source_target_pairs={{0,24},{1,25},{2,26},{3,27},{4,28},{5,29},{6,30},{7,31},{8,16},{9,... | collective-permute-start | bytes 393224 | tf_op jit(solution)/shard_map/ppermute | solution.py:288
  31.8 13.9 %collective-permute-start.7 = (bf16[512,128]{1,0:T(8,128)(2,1)S(1)}, bf16[512,128]{1,0:T(8,128)(2,1)S(1)}, u32[]{:S(2)}, u32[]{:S(2)}) collective-permute-start(bf16[512,128]{1,0:T(8,128)(2,1)S(1)} %get-tuple-element.27), channel_id=1, source_target_pairs={{0,2},{1,3},{2,0},{3,1},{4,6},{5,7},{6,4},{7,5},{8,10},{9,11},{10,... | collective-permute-start | bytes 393224 | tf_op jit(solution)/shard_map/ppermute | solution.py:288
  34.7 12.8 %collective-permute-start.17 = (bf16[1,512,128]{2,1,0:T(8,128)(2,1)S(1)}, bf16[1,512,128]{2,1,0:T(8,128)(2,1)S(1)}, u32[]{:S(2)}, u32[]{:S(2)}) collective-permute-start(bf16[1,512,128]{2,1,0:T(8,128)(2,1)S(1)} %bitcast.14), channel_id=1, source_target_pairs={{0,8},{1,9},{2,10},{3,11},{4,12},{5,13},{6,14},{7,15},{8,0},{9,1},... | collective-permute-start | bytes 393224 | tf_op jit(solution)/shard_map/ppermute | solution.py:288
  35.2 14.0 %collective-permute-start.18 = (bf16[1,512,128]{2,1,0:T(8,128)(2,1)S(1)}, bf16[1,512,128]{2,1,0:T(8,128)(2,1)S(1)}, u32[]{:S(2)}, u32[]{:S(2)}) collective-permute-start(bf16[1,512,128]{2,1,0:T(8,128)(2,1)S(1)} %bitcast.15), channel_id=1, source_target_pairs={{0,16},{1,17},{2,18},{3,19},{4,20},{5,21},{6,22},{7,23},{8,24},{9,... | collective-permute-start | bytes 393224 | tf_op jit(solution)/shard_map/ppermute | solution.py:288
  36.8 2.2 %copy-start = (bf16[2048,1024]{1,0:T(8,128)(2,1)S(1)}, bf16[2048,1024]{1,0:T(8,128)(2,1)}, u32[]{:S(2)}) copy-start(bf16[2048,1024]{1,0:T(8,128)(2,1)} %tile.1) | copy-start | bytes 12582916
  43.9 23.7 %collective-permute-start.27 = (bf16[1024,128]{1,0:T(8,128)(2,1)S(1)}, bf16[1024,128]{1,0:T(8,128)(2,1)S(1)}, u32[]{:S(2)}, u32[]{:S(2)}) collective-permute-start(bf16[1024,128]{1,0:T(8,128)(2,1)S(1)} %get-tuple-element.34), channel_id=1, source_target_pairs={{0,2},{1,3},{2,0},{3,1},{4,6},{5,7},{6,4},{7,5},{8,10},{9,11},{10,... | collective-permute-start | bytes 786440 | tf_op jit(solution)/shard_map/ppermute | solution.py:288
  44.6 8.6 %collective-permute-start.16 = (bf16[1,512,128]{2,1,0:T(8,128)(2,1)S(1)}, bf16[1,512,128]{2,1,0:T(8,128)(2,1)S(1)}, u32[]{:S(2)}, u32[]{:S(2)}) collective-permute-start(bf16[1,512,128]{2,1,0:T(8,128)(2,1)S(1)} %bitcast.16), channel_id=1, source_target_pairs={{0,24},{1,25},{2,26},{3,27},{4,28},{5,29},{6,30},{7,31},{8,16},{9,... | collective-permute-start | bytes 393224 | tf_op jit(solution)/shard_map/ppermute | solution.py:288
  45.7 12.1 %collective-permute-start.10 = (bf16[1,512,128]{2,1,0:T(8,128)(2,1)S(1)}, bf16[1,512,128]{2,1,0:T(8,128)(2,1)S(1)}, u32[]{:S(2)}, u32[]{:S(2)}) collective-permute-start(bf16[1,512,128]{2,1,0:T(8,128)(2,1)S(1)} %bitcast.10), channel_id=1, source_target_pairs={{0,24},{1,25},{2,26},{3,27},{4,28},{5,29},{6,30},{7,31},{8,16},{9,... | collective-permute-start | bytes 393224 | tf_op jit(solution)/shard_map/ppermute | solution.py:288
  47.5 10.8 %collective-permute-start.8 = (bf16[1,512,128]{2,1,0:T(8,128)(2,1)S(1)}, bf16[1,512,128]{2,1,0:T(8,128)(2,1)S(1)}, u32[]{:S(2)}, u32[]{:S(2)}) collective-permute-start(bf16[1,512,128]{2,1,0:T(8,128)(2,1)S(1)} %bitcast.11), channel_id=1, source_target_pairs={{0,8},{1,9},{2,10},{3,11},{4,12},{5,13},{6,14},{7,15},{8,0},{9,1},... | collective-permute-start | bytes 393224 | tf_op jit(solution)/shard_map/ppermute | solution.py:288
  49.2 10.6 %collective-permute-start.9 = (bf16[1,512,128]{2,1,0:T(8,128)(2,1)S(1)}, bf16[1,512,128]{2,1,0:T(8,128)(2,1)S(1)}, u32[]{:S(2)}, u32[]{:S(2)}) collective-permute-start(bf16[1,512,128]{2,1,0:T(8,128)(2,1)S(1)} %bitcast.12), channel_id=1, source_target_pairs={{0,16},{1,17},{2,18},{3,19},{4,20},{5,21},{6,22},{7,23},{8,24},{9,... | collective-permute-start | bytes 393224 | tf_op jit(solution)/shard_map/ppermute | solution.py:288
  53.2 39.0 %collective-permute-start.3 = (bf16[1,512,128]{2,1,0:T(8,128)(2,1)S(1)}, bf16[1,512,128]{2,1,0:T(8,128)(2,1)S(1)}, u32[]{:S(2)}, u32[]{:S(2)}) collective-permute-start(bf16[1,512,128]{2,1,0:T(8,128)(2,1)S(1)} %bitcast.6), channel_id=1, source_target_pairs={{0,8},{1,9},{2,10},{3,11},{4,12},{5,13},{6,14},{7,15},{8,0},{9,1},... | collective-permute-start | bytes 393224 | tf_op jit(solution)/shard_map/ppermute | solution.py:288
  57.8 34.5 %collective-permute-start.4 = (bf16[1,512,128]{2,1,0:T(8,128)(2,1)S(1)}, bf16[1,512,128]{2,1,0:T(8,128)(2,1)S(1)}, u32[]{:S(2)}, u32[]{:S(2)}) collective-permute-start(bf16[1,512,128]{2,1,0:T(8,128)(2,1)S(1)} %bitcast.7), channel_id=1, source_target_pairs={{0,16},{1,17},{2,18},{3,19},{4,20},{5,21},{6,22},{7,23},{8,24},{9,... | collective-permute-start | bytes 393224 | tf_op jit(solution)/shard_map/ppermute | solution.py:288
  58.4 10.8 %collective-permute-start.24 = (bf16[1024,128]{1,0:T(8,128)(2,1)S(1)}, bf16[1024,128]{1,0:T(8,128)(2,1)S(1)}, u32[]{:S(2)}, u32[]{:S(2)}) collective-permute-start(bf16[1024,128]{1,0:T(8,128)(2,1)S(1)} %piece_product.5), channel_id=1, source_target_pairs={{0,2},{1,3},{2,0},{3,1},{4,6},{5,7},{6,4},{7,5},{8,10},{9,11},{10,... | collective-permute-start | bytes 786440 | tf_op jit(solution)/shard_map/ppermute | solution.py:288
  59.8 15.0 %collective-permute-start.22 = (bf16[1024,128]{1,0:T(8,128)(2,1)S(1)}, bf16[1024,128]{1,0:T(8,128)(2,1)S(1)}, u32[]{:S(2)}, u32[]{:S(2)}) collective-permute-start(bf16[1024,128]{1,0:T(8,128)(2,1)S(1)} %get-tuple-element.30), channel_id=1, source_target_pairs={{0,2},{1,3},{2,0},{3,1},{4,6},{5,7},{6,4},{7,5},{8,10},{9,11},{10,... | collective-permute-start | bytes 786440 | tf_op jit(solution)/shard_map/ppermute | solution.py:288
  67.6 6.4 %collective-permute-start.19 = (bf16[1024,128]{1,0:T(8,128)(2,1)S(1)}, bf16[1024,128]{1,0:T(8,128)(2,1)S(1)}, u32[]{:S(2)}, u32[]{:S(2)}) collective-permute-start(bf16[1024,128]{1,0:T(8,128)(2,1)S(1)} %piece_product.4), channel_id=1, source_target_pairs={{0,2},{1,3},{2,0},{3,1},{4,6},{5,7},{6,4},{7,5},{8,10},{9,11},{10,... | collective-permute-start | bytes 786440 | tf_op jit(solution)/shard_map/ppermute | solution.py:288
  69.2 33.7 %collective-permute-start.28 = (bf16[1024,128]{1,0:T(8,128)(2,1)S(1)}, bf16[1024,128]{1,0:T(8,128)(2,1)S(1)}, u32[]{:S(2)}, u32[]{:S(2)}) collective-permute-start(bf16[1024,128]{1,0:T(8,128)(2,1)S(1)} %add_convert_fusion), channel_id=1, source_target_pairs={{2,4},{3,5},{4,2},{5,3},{10,12},{11,13},{12,10},{13,11},{18,20},{1... | collective-permute-start | bytes 786440 | tf_op jit(solution)/shard_map/ppermute | solution.py:288
  74.1 1.5 %collective-permute-start.25 = (bf16[1024,128]{1,0:T(8,128)(2,1)S(1)}, bf16[1024,128]{1,0:T(8,128)(2,1)S(1)}, u32[]{:S(2)}, u32[]{:S(2)}) collective-permute-start(bf16[1024,128]{1,0:T(8,128)(2,1)S(1)} %add_convert_fusion.2), channel_id=1, source_target_pairs={{2,4},{3,5},{4,2},{5,3},{10,12},{11,13},{12,10},{13,11},{18,20},{1... | collective-permute-start | bytes 786440 | tf_op jit(solution)/shard_map/ppermute | solution.py:288
  74.8 1.5 %collective-permute-start.20 = (bf16[1024,128]{1,0:T(8,128)(2,1)S(1)}, bf16[1024,128]{1,0:T(8,128)(2,1)S(1)}, u32[]{:S(2)}, u32[]{:S(2)}) collective-permute-start(bf16[1024,128]{1,0:T(8,128)(2,1)S(1)} %add_convert_fusion.5), channel_id=1, source_target_pairs={{2,4},{3,5},{4,2},{5,3},{10,12},{11,13},{12,10},{13,11},{18,20},{1... | collective-permute-start | bytes 786440 | tf_op jit(solution)/shard_map/ppermute | solution.py:288
  75.6 27.2 %collective-permute-start.23 = (bf16[1024,128]{1,0:T(8,128)(2,1)S(1)}, bf16[1024,128]{1,0:T(8,128)(2,1)S(1)}, u32[]{:S(2)}, u32[]{:S(2)}) collective-permute-start(bf16[1024,128]{1,0:T(8,128)(2,1)S(1)} %add_convert_fusion.3), channel_id=1, source_target_pairs={{2,4},{3,5},{4,2},{5,3},{10,12},{11,13},{12,10},{13,11},{18,20},{1... | collective-permute-start | bytes 786440 | tf_op jit(solution)/shard_map/ppermute | solution.py:288
  76.4 26.5 %collective-permute-start.26 = (bf16[1024,128]{1,0:T(8,128)(2,1)S(1)}, bf16[1024,128]{1,0:T(8,128)(2,1)S(1)}, u32[]{:S(2)}, u32[]{:S(2)}) collective-permute-start(bf16[1024,128]{1,0:T(8,128)(2,1)S(1)} %add_convert_fusion.1), channel_id=1, source_target_pairs={{0,2},{1,3},{2,0},{3,1},{4,6},{5,7},{6,4},{7,5},{8,10},{9,11},{10,... | collective-permute-start | bytes 786440 | tf_op jit(solution)/shard_map/ppermute | solution.py:288
  92.2 10.7 %copy-start.1 = (bf16[2048,128]{1,0:T(8,128)(2,1)S(1)}, bf16[2048,128]{1,0:T(8,128)(2,1)}, u32[]{:S(2)}) copy-start(bf16[2048,128]{1,0:T(8,128)(2,1)} %get-tuple-element.20.lhat) | copy-start | bytes 1572868
  92.2 14.8 %copy-start.3 = (s32[8,64]{1,0:T(8,128)S(1)}, s32[8,64]{1,0:T(8,128)}, u32[]{:S(2)}) copy-start(s32[8,64]{1,0:T(8,128)} %listed.3) | copy-start | bytes 6148
  92.2 10.6 %collective-permute-start.21 = (bf16[1024,128]{1,0:T(8,128)(2,1)S(1)}, bf16[1024,128]{1,0:T(8,128)(2,1)S(1)}, u32[]{:S(2)}, u32[]{:S(2)}) collective-permute-start(bf16[1024,128]{1,0:T(8,128)(2,1)S(1)} %add_convert_fusion.4), channel_id=1, source_target_pairs={{0,2},{1,3},{2,0},{3,1},{4,6},{5,7},{6,4},{7,5},{8,10},{9,11},{10,... | collective-permute-start | bytes 786440 | tf_op jit(solution)/shard_map/ppermute | solution.py:288
  92.3 5.9 %collective-permute-start.5 = (bf16[1,512,128]{2,1,0:T(8,128)(2,1)S(1)}, bf16[1,512,128]{2,1,0:T(8,128)(2,1)S(1)}, u32[]{:S(2)}, u32[]{:S(2)}) collective-permute-start(bf16[1,512,128]{2,1,0:T(8,128)(2,1)S(1)} %bitcast.8), channel_id=1, source_target_pairs={{0,24},{1,25},{2,26},{3,27},{4,28},{5,29},{6,30},{7,31},{8,16},{9,... | collective-permute-start | bytes 393224 | tf_op jit(solution)/shard_map/ppermute | solution.py:288
  102.8 7.2 %copy-start.4 = (f32[1,128,128]{2,1,0:T(8,128)S(1)}, f32[1,128,128]{2,1,0:T(8,128)}, u32[]{:S(2)}) copy-start(f32[1,128,128]{2,1,0:T(8,128)} %param.8) | copy-start | bytes 196612
  103.4 5.2 %collective-permute-start.29 = (bf16[128,128]{1,0:T(8,128)(2,1)S(1)}, bf16[128,128]{1,0:T(8,128)(2,1)S(1)}, u32[]{:S(2)}, u32[]{:S(2)}) collective-permute-start(bf16[128,128]{1,0:T(8,128)(2,1)S(1)} %get-tuple-element.37), channel_id=1, source_target_pairs={{0,8},{1,9},{2,10},{3,11},{4,12},{5,13},{6,14},{7,15},{8,0},{9,1},... | collective-permute-start | bytes 98312 | tf_op jit(solution)/shard_map/ppermute | solution.py:288
  105.2 3.9 %collective-permute-start.30 = (bf16[128,128]{1,0:T(8,128)(2,1)S(1)}, bf16[128,128]{1,0:T(8,128)(2,1)S(1)}, u32[]{:S(2)}, u32[]{:S(2)}) collective-permute-start(bf16[128,128]{1,0:T(8,128)(2,1)S(1)} %get-tuple-element.37), channel_id=1, source_target_pairs={{0,16},{1,17},{2,18},{3,19},{4,20},{5,21},{6,22},{7,23},{8,24},{9,... | collective-permute-start | bytes 98312 | tf_op jit(solution)/shard_map/ppermute | solution.py:288
  105.2 4.8 %collective-permute-start.31 = (bf16[128,128]{1,0:T(8,128)(2,1)S(1)}, bf16[128,128]{1,0:T(8,128)(2,1)S(1)}, u32[]{:S(2)}, u32[]{:S(2)}) collective-permute-start(bf16[128,128]{1,0:T(8,128)(2,1)S(1)} %get-tuple-element.37), channel_id=1, source_target_pairs={{0,24},{1,25},{2,26},{3,27},{4,28},{5,29},{6,30},{7,31},{8,16},{9,... | collective-permute-start | bytes 98312 | tf_op jit(solution)/shard_map/ppermute | solution.py:288

commit v3 on v2

--- a/solution.py
+++ b/solution.py
@@ -22,7 +22,7 @@
 
 
 def normalize_kernel(n, listed, panel, unit, *refs):
-    outs, rows, right, keeps, came = refs[: n + 1], refs[n + 1], refs[n + 2], refs[n + 3], refs[n + 4]
+    outs, (rows, right, keeps, ordered, came) = refs[:-5], refs[-5:]
     p = lax.axis_index("prow")
     c = lax.axis_index("pcol")
     part = panel.shape[0] // n
@@ -48,22 +48,28 @@
             keep = keeps[0, (p * n + g) * per + b].astype(jnp.float32)
             v = (t[b * BLOCK : (b + 1) * BLOCK] * keep).astype(jnp.bfloat16)
             outs[a][b * BLOCK : (b + 1) * BLOCK, :] = v
-            outs[n][pl.ds(pl.multiple_of(g * part + b * BLOCK, BLOCK), BLOCK), :] = v
+            ordered[pl.ds(pl.multiple_of(g * part + b * BLOCK, BLOCK), BLOCK), :] = v
+    tall = panel.shape[0] // HALVES
+    for h in range(HALVES):
+        outs[n + h][...] = ordered[h * tall : (h + 1) * tall, :]
 
 
 def normalize(n, listed, panel, unit):
     rows, width = panel.shape
     part = rows // n
-    shapes = [jax.ShapeDtypeStruct((part, width), jnp.bfloat16)] * n + [jax.ShapeDtypeStruct((rows, width), jnp.bfloat16)]
+    shapes = [jax.ShapeDtypeStruct((part, width), jnp.bfloat16)] * n + [
+        jax.ShapeDtypeStruct((rows // HALVES, width), jnp.bfloat16)
+    ] * HALVES
     return pl.pallas_call(
         functools.partial(normalize_kernel, n),
         out_shape=shapes,
         in_specs=[whole(pltpu.HBM)] * 3,
-        out_specs=[whole(VMEM)] * (n + 1),
+        out_specs=[whole(VMEM)] * (n + HALVES),
         scratch_shapes=[
             pltpu.VMEM((n, part, width), jnp.bfloat16),
             pltpu.VMEM((width, width), jnp.bfloat16),
             pltpu.SMEM((1, listed.shape[1]), jnp.int32),
+            pltpu.VMEM((rows, width), jnp.bfloat16),
             pltpu.SemaphoreType.DMA((n + 2,)),
         ],
         compiler_params=pltpu.CompilerParams(vmem_limit_bytes=FULL),
@@ -198,74 +204,121 @@
     )(*pieces, *tiles, *before)
 
 
-def diagonal_kernel(lhat, *refs):
-    ins, product, diag, sent = refs[:-3], refs[-3], refs[-2], refs[-1]
-    count = len(ins) // HALVES
-    tall = ins[0].shape[0]
+def among(z, planes):
+    return functools.reduce(jnp.logical_or, [z == y for y in planes])
+
+
+def add_kernel(n, q, planes, x, y, out):
+    z = lax.axis_index("pcol") // q
+    total = x[...].astype(jnp.float32) + y[...].astype(jnp.float32)
+    if len(planes) < n:
+        total = jnp.where(among(z, planes), total, x[...].astype(jnp.float32))
+    out[...] = total.astype(out.dtype)
+
+
+def add(n, q, x, came):
+    if came is None:
+        return x
+    y, planes = came
+    return pl.pallas_call(
+        functools.partial(add_kernel, n, q, planes),
+        out_shape=jax.ShapeDtypeStruct(x.shape, x.dtype),
+        in_specs=[whole(VMEM)] * 2,
+        out_specs=whole(VMEM),
+        compiler_params=pltpu.CompilerParams(vmem_limit_bytes=LIMIT),
+        cost_estimate=pl.CostEstimate(flops=x.size, bytes_accessed=6 * x.size, transcendentals=0),
+        name="add",
+    )(x, y)
+
+
+def ahead_kernel(*refs):
+    loads, rows, out = refs[:HALVES], refs[HALVES : 2 * HALVES], refs[-1]
+    tall = loads[0].shape[0]
     step = min(tall, 512)
     total = None
-    for h in range(HALVES):
-        first, *came = ins[h * count : (h + 1) * count]
+    for load, right in zip(loads, rows):
         for r in range(tall // step):
             here = slice(r * step, (r + 1) * step)
-            there = slice(h * tall + r * step, h * tall + (r + 1) * step)
-            x = first[here, :].astype(jnp.float32)
-            for y in came:
-                x = x + y[here, :].astype(jnp.float32)
-            x = x.T
-            product[:, there] = x
-            high = x.astype(jnp.bfloat16)
-            low = (x - high.astype(jnp.float32)).astype(jnp.bfloat16)
-            for y in (high, low):
-                term = jnp.dot(y, lhat[there, :], preferred_element_type=jnp.float32)
-                total = term if total is None else total + term
-    diag[...] = total
-    sent[...] = total.astype(jnp.bfloat16)
-
-
-def diagonal(lhat, parts):
-    rows, width = lhat.shape
-    ins = [x for half in parts for x in half]
-    return pl.pallas_call(
-        diagonal_kernel,
-        out_shape=[
-            jax.ShapeDtypeStruct((width, rows), jnp.float32),
-            jax.ShapeDtypeStruct((width, width), jnp.float32),
-            jax.ShapeDtypeStruct((width, width), jnp.bfloat16),
-        ],
-        in_specs=[whole(VMEM)] * (1 + len(ins)),
-        out_specs=[whole(VMEM)] * 3,
-        compiler_params=pltpu.CompilerParams(vmem_limit_bytes=LIMIT),
-        cost_estimate=pl.CostEstimate(flops=4 * rows * width * width, bytes_accessed=10 * rows * width, transcendentals=0),
-        name="diagonal",
-    )(lhat, *ins)
-
-
-def masked_kernel(listed, product, off):
+            left = load[here, :].astype(jnp.float32).T.astype(jnp.bfloat16)
+            term = jnp.dot(left, right[here, :], preferred_element_type=jnp.float32)
+            total = term if total is None else total + term
+    out[...] = total.astype(out.dtype)
+
+
+def ahead(loads, rows, dtype):
+    tall, width = loads[0].shape
+    return pl.pallas_call(
+        ahead_kernel,
+        out_shape=jax.ShapeDtypeStruct((width, width), dtype),
+        in_specs=[whole(VMEM)] * (2 * HALVES),
+        out_specs=whole(VMEM),
+        compiler_params=pltpu.CompilerParams(vmem_limit_bytes=LIMIT),
+        cost_estimate=pl.CostEstimate(
+            flops=2 * HALVES * tall * width * width, bytes_accessed=4 * HALVES * tall * width, transcendentals=0
+        ),
+        name="ahead",
+    )(*loads, *rows)
+
+
+def chosen_planes(n, q, planes):
+    z = lax.axis_index("pcol") // q
+    return [None if len(at) == n else among(z, at) for at in planes]
+
+
+def gathered_kernel(n, q, planes, diag, *refs):
+    early, total, sent = refs[:-2], refs[-2], refs[-1]
+    x = diag[...]
+    for y, take in zip(early, chosen_planes(n, q, planes)):
+        y = y[...].astype(jnp.float32)
+        x = x + (y if take is None else jnp.where(take, y, 0.0))
+    total[...] = x
+    sent[...] = x.astype(jnp.bfloat16)
+
+
+def gathered(n, q, planes, diag, early):
+    return pl.pallas_call(
+        functools.partial(gathered_kernel, n, q, planes),
+        out_shape=[jax.ShapeDtypeStruct(diag.shape, jnp.float32), jax.ShapeDtypeStruct(diag.shape, jnp.bfloat16)],
+        in_specs=[whole(VMEM)] * (1 + len(early)),
+        out_specs=[whole(VMEM)] * 2,
+        compiler_params=pltpu.CompilerParams(vmem_limit_bytes=LIMIT),
+        cost_estimate=pl.CostEstimate(flops=4 * diag.size, bytes_accessed=16 * diag.size, transcendentals=0),
+        name="gathered",
+    )(diag, *early)
+
+
+def masked_kernel(n, q, planes, rows, h, count, listed, *refs):
+    parts, off = refs[:count], refs[-1]
     p = lax.axis_index("prow")
     c = lax.axis_index("pcol")
-    i = pl.program_id(0)
+    takes = chosen_planes(n, q, planes)
     per = off.shape[1] // BLOCK
-    base = (p * pl.num_programs(0) + i) * per
+    base = p * (rows // BLOCK) + (h * pl.num_programs(0) + pl.program_id(0)) * per
+    x = parts[0][...].astype(jnp.float32)
+    for y, take in zip(parts[1:], takes):
+        y = y[...].astype(jnp.float32)
+        x = x + (y if take is None else jnp.where(take, y, 0.0))
+    x = x.T
     for b in range(per):
         keep = listed[c, base + b].astype(jnp.float32)
-        off[:, b * BLOCK : (b + 1) * BLOCK] = -(product[:, b * BLOCK : (b + 1) * BLOCK] * keep)
-
-
-def masked(listed, product):
-    width, rows = product.shape
-    step = min(rows, 1024)
-    block = pl.BlockSpec((width, step), lambda i: (0, i))
-    return pl.pallas_call(
-        masked_kernel,
-        grid=(rows // step,),
+        off[:, b * BLOCK : (b + 1) * BLOCK] = -(x[:, b * BLOCK : (b + 1) * BLOCK] * keep)
+
+
+def masked(n, q, planes, rows, h, listed, parts, before):
+    tall, width = parts[0].shape
+    step = min(tall, 512)
+    count = tall // step
+    return pl.pallas_call(
+        functools.partial(masked_kernel, n, q, planes, rows, h, len(parts)),
+        grid=(count,),
         out_shape=jax.ShapeDtypeStruct((width, rows), jnp.float32),
-        in_specs=[whole(SMEM), block],
-        out_specs=block,
-        compiler_params=pltpu.CompilerParams(vmem_limit_bytes=LIMIT),
-        cost_estimate=pl.CostEstimate(flops=2 * rows * width, bytes_accessed=8 * rows * width, transcendentals=0),
+        in_specs=[whole(SMEM)] + [pl.BlockSpec((step, width), lambda i: (i, 0))] * len(parts) + [whole(pl.ANY)] * len(before),
+        out_specs=pl.BlockSpec((width, step), lambda i: (0, h * count + i)),
+        input_output_aliases={1 + len(parts): 0} if before else {},
+        compiler_params=pltpu.CompilerParams(vmem_limit_bytes=LIMIT),
+        cost_estimate=pl.CostEstimate(flops=4 * tall * width, bytes_accessed=10 * tall * width, transcendentals=0),
         name="masked",
-    )(listed, product)
+    )(listed, *parts, *before)
 
 
 def per_device(n, ncol, l_panel, inverse_tile, unit_inverse, pivot_inverse, listed):
@@ -290,10 +343,21 @@
     def over_rows(x, a):
         return swap(x, lambda p, z, k: (p ^ a, z, k))
 
-    *pieces, lhat = normalize(n, listed, l_panel, unit_inverse)
+    made = normalize(n, listed, l_panel, unit_inverse)
+    pieces, lhat = made[:n], made[n:]
     tiles = [load(inverse_tile)]
     tiles += [swap(inverse_tile, lambda p, z, k: (p, z, k ^ e)) for e in range(1, q)]
     tiles = [pltpu.with_memory_space_constraint(t, pltpu.VMEM) for t in tiles]
+
+    def line_swap(x, odd, d):
+        to = {}
+        for z in line_pairs(n, d, odd):
+            to[z], to[z + 1] = z + 1, z
+        got = swap(x, lambda p, z, k: (p, to[z], k) if z in to else (p, z, k ^ (q > 1)))
+        return got, tuple(sorted(to))
+
+    sides = [odd for odd in (0, 1) if line_pairs(n, 1, odd)]
+    theirs = {odd: [line_swap(lhat[h], odd, 1)[0] for h in range(HALVES)] for odd in sides}
 
     scattered = [pieces[0]] + [over_rows(pieces[a], a) for a in range(1, n)]
     chosen = pick(n, q, scattered)
@@ -331,33 +395,33 @@
             x = jnp.where(here, chunk[m][h], x)
         return x
 
-    def add(x, y):
-        if y is None:
-            return x
-        return (x.astype(jnp.float32) + y.astype(jnp.float32)).astype(jnp.bfloat16)
-
+    early, loads = [], ([], [])
     came = [[None, None] for _ in range(HALVES)]
     for d in range(n - 1, 0, -1):
         for h in range(HALVES):
             sent = [None, None]
             for odd in (0, 1):
-                pairs = line_pairs(n, d, odd)
-                if not pairs:
+                if not line_pairs(n, d, odd):
                     continue
-                to = {}
-                for z in pairs:
-                    to[z], to[z + 1] = z + 1, z
-                load_ = add(own(odd, d, h), came[h][1 - odd])
-                sent[odd] = swap(load_, lambda p, z, k: (p, to[z], k) if z in to else None)
+                load_ = add(n, q, own(odd, d, h), came[h][1 - odd])
+                sent[odd] = line_swap(load_, odd, d)
+                loads[odd].append(load_)
+                if d == 1 and h == HALVES - 1:
+                    term = ahead(loads[odd][-HALVES:], theirs[odd], jnp.bfloat16)
+                    early.append(line_swap(term, odd, d)[0])
             came[h] = sent
 
-    parts = [[chunk[0][h]] + [x for x in came[h] if x is not None] for h in range(HALVES)]
-    product, part, travel = diagonal(lhat, parts)
-    off = masked(listed, product)
+    parts = [[chunk[0][h]] + [x[0] for x in came[h] if x is not None] for h in range(HALVES)]
+    planes = [x[1] for x in came[0] if x is not None]
+    part = ahead(chunk[0], lhat, jnp.float32)
+    part, travel = gathered(n, q, planes, part, early)
+    off = []
+    for h in range(HALVES):
+        off = [masked(n, q, planes, inverse_tile.shape[0], h, listed, parts[h], off)]
     total = part
     for a in range(1, n):
         total = total + over_rows(travel, a).astype(jnp.float32)
-    return off, pivot_inverse + total[None]
+    return off[0], pivot_inverse + total[None]
 
 
 def groups(n):

time: 111 us -> 118 us (1.063)
  waiting for transfers between devices: 28.6 us -> 33.6 us
  Pallas kernels: 28.1 us -> 30.8 us
    ppermute x32 -> x38, waiting for transfers between devices: 28.6 us -> 33.6 us  [swap(): return lax.ppermute(x, AXES, pairs)]
    pallas_call x2 -> x12, Pallas kernels: 2.22 us -> 4.82 us  [the longest x2 3.27 us: masked(): pl.pallas_call(functools.partial(masked_kernel, n, q, planes, rows, h, le...]
    ppermute x32 -> x38, starting transfers between devices: 48.8 us -> 48.1 us  [swap(): return lax.ppermute(x, AXES, pairs)]
    unnamed x10 -> x12, local copies, waits for them, and re-layouts: 3.11 us -> 3.11 us
  transfers between devices with their start and end apart: 32 -> 38, of which waited for: 8 -> 13; matrix products, arithmetic and copies ran while one was open for 0% -> 1% of each run, Pallas kernels for 25% -> 25%
where the time goes in v3:
time: 118 us; the launch traced here: 117 us
  starting transfers between devices  48.1 us (41%)
  waiting for transfers between devices  33.6 us (28%)
  Pallas kernels  30.8 us (26%)
  local copies, waits for them, and re-layouts  3.11 us (3%)
    ppermute x38, starting transfers between devices, swap(): return lax.ppermute(x, AXES, pairs)  48.1 us
    ppermute x38, waiting for transfers between devices, swap(): return lax.ppermute(x, AXES, pairs)  33.6 us
    pallas_call x3, Pallas kernels, partial_product(): pl.pallas_call(functools.partial(partial_kernel, n, q, halves, min(tall,...  13.7 us
    pallas_call x3, Pallas kernels, piece_product(): pl.pallas_call(functools.partial(piece_kernel, n, q, which, base, min(tal...  9.28 us
    pallas_call x2, Pallas kernels, masked(): pl.pallas_call(functools.partial(masked_kernel, n, q, planes, rows, h, le...  3.27 us
    unnamed x12, local copies, waits for them, and re-layouts  3.11 us
    pallas_call x1, Pallas kernels, normalize(): pl.pallas_call(functools.partial(normalize_kernel, n), out_shape=shapes,...  2.66 us
  transfers between devices with their start and end apart: 38, of which 13 were waited for; matrix products, arithmetic and copies ran while one was open for 1% of the time, Pallas kernels for 25%

profile of v3, /device:TPU:0, one launch (start us, length us, event | category | flops | bytes accessed | tf_op | source)
XLA Modules:
  0.0 117.1 jit_solution(2415388549555454227)
XLA Ops:
  0.6 0.6 collective-permute-start.6
  1.2 2.7 %normalize.1 = (bf16[512,128]{1,0:T(8,128)(2,1)}, bf16[512,128]{1,0:T(8,128)(2,1)}, bf16[512,128]{1,0:T(8,128)(2,1)}, bf16[512,128]{1,0:T(8,128)(2,1)}, bf16[102...) custom-call(s32[8,64]{1,0:T(8,128)} %listed.5, bf16[2048,128]{1,0:T(8,128)(2,1)} %panel.1, bf16[1,128,128]{2,1,0:T(8,128)(2,1)} %unit.1), custom_call_target="tpu_custom_call" | custom-call | flops 67108864 | bytes 1572864 | tf_op jit(solution)/shard_map/normalize/pallas_call | solution.py:63
  3.9 2.6 %collective-permute-start = (bf16[512,128]{1,0:T(8,128)(2,1)}, bf16[512,128]{1,0:T(8,128)(2,1)S(1)}, u32[]{:S(2)}, u32[]{:S(2)}) collective-permute-start(bf16[512,128]{1,0:T(8,128)(2,1)} %get-tuple-element.21), channel_id=1, source_target_pairs={{0,8},{1,9},{2,10},{3,11},{4,12},{5,13},{6,14},{7,15},{8,0},{9,1},... | collective-permute-start | bytes 393224 | tf_op jit(solution)/shard_map/ppermute | solution.py:341
  6.4 1.5 %collective-permute-start.1 = (bf16[512,128]{1,0:T(8,128)(2,1)}, bf16[512,128]{1,0:T(8,128)(2,1)S(1)}, u32[]{:S(2)}, u32[]{:S(2)}) collective-permute-start(bf16[512,128]{1,0:T(8,128)(2,1)} %get-tuple-element.22), channel_id=1, source_target_pairs={{0,16},{1,17},{2,18},{3,19},{4,20},{5,21},{6,22},{7,23},{8,24},{9,... | collective-permute-start | bytes 393224 | tf_op jit(solution)/shard_map/ppermute | solution.py:341
  8.0 3.0 %collective-permute-done.refs_1_ = bf16[512,128]{1,0:T(8,128)(2,1)S(1)} collective-permute-done((bf16[512,128]{1,0:T(8,128)(2,1)}, bf16[512,128]{1,0:T(8,128)(2,1)S(1)}, u32[]{:S(2)}, u32[]{:S(2)}) %collective-permute-start) | collective-permute-done | bytes 131104 | tf_op jit(solution)/shard_map/ppermute | solution.py:341
  10.9 4.1 %collective-permute-done.1.refs_2_ = bf16[512,128]{1,0:T(8,128)(2,1)S(1)} collective-permute-done((bf16[512,128]{1,0:T(8,128)(2,1)}, bf16[512,128]{1,0:T(8,128)(2,1)S(1)}, u32[]{:S(2)}, u32[]{:S(2)}) %collective-permute-start.1) | collective-permute-done | bytes 131104 | tf_op jit(solution)/shard_map/ppermute | solution.py:341
  15.0 0.9 copy-done.3
  16.0 3.6 %collective-permute-start.15 = (bf16[512,128]{1,0:T(8,128)(2,1)S(1)}, bf16[512,128]{1,0:T(8,128)(2,1)S(1)}, u32[]{:S(2)}, u32[]{:S(2)}) collective-permute-start(bf16[512,128]{1,0:T(8,128)(2,1)S(1)} %get-tuple-element.30), channel_id=1, source_target_pairs={{0,6},{1,7},{2,4},{3,5},{4,2},{5,3},{6,0},{7,1},{8,14},{9,15},{10,... | collective-permute-start | bytes 393224 | tf_op jit(solution)/shard_map/ppermute | solution.py:341
  19.7 4.4 %collective-permute-done.15 = bf16[512,128]{1,0:T(8,128)(2,1)S(1)} collective-permute-done((bf16[512,128]{1,0:T(8,128)(2,1)S(1)}, bf16[512,128]{1,0:T(8,128)(2,1)S(1)}, u32[]{:S(2)}, u32[]{:S(2)}) %collective-permute-start.15) | collective-permute-done | bytes 131104 | tf_op jit(solution)/shard_map/ppermute | solution.py:341
  24.1 1.4 %collective-permute-start.17 = (bf16[1,512,128]{2,1,0:T(8,128)(2,1)S(1)}, bf16[1,512,128]{2,1,0:T(8,128)(2,1)S(1)}, u32[]{:S(2)}, u32[]{:S(2)}) collective-permute-start(bf16[1,512,128]{2,1,0:T(8,128)(2,1)S(1)} %bitcast.18), channel_id=1, source_target_pairs={{0,8},{1,9},{2,10},{3,11},{4,12},{5,13},{6,14},{7,15},{8,0},{9,1},... | collective-permute-start | bytes 393224 | tf_op jit(solution)/shard_map/ppermute | solution.py:341
  25.5 0.8 collective-permute-start.18
  26.3 1.3 %collective-permute-start.16 = (bf16[1,512,128]{2,1,0:T(8,128)(2,1)S(1)}, bf16[1,512,128]{2,1,0:T(8,128)(2,1)S(1)}, u32[]{:S(2)}, u32[]{:S(2)}) collective-permute-start(bf16[1,512,128]{2,1,0:T(8,128)(2,1)S(1)} %bitcast.20), channel_id=1, source_target_pairs={{0,24},{1,25},{2,26},{3,27},{4,28},{5,29},{6,30},{7,31},{8,16},{9,... | collective-permute-start | bytes 393224 | tf_op jit(solution)/shard_map/ppermute | solution.py:341
  27.6 2.6 %collective-permute-done.11 = bf16[512,128]{1,0:T(8,128)(2,1)S(1)} collective-permute-done((bf16[512,128]{1,0:T(8,128)(2,1)S(1)}, bf16[512,128]{1,0:T(8,128)(2,1)S(1)}, u32[]{:S(2)}, u32[]{:S(2)}) %collective-permute-start.11) | collective-permute-done | bytes 131104 | tf_op jit(solution)/shard_map/ppermute | solution.py:341
  30.2 1.6 %collective-permute-start.12 = (bf16[1,512,128]{2,1,0:T(8,128)(2,1)S(1)}, bf16[1,512,128]{2,1,0:T(8,128)(2,1)S(1)}, u32[]{:S(2)}, u32[]{:S(2)}) collective-permute-start(bf16[1,512,128]{2,1,0:T(8,128)(2,1)S(1)} %bitcast.14), channel_id=1, source_target_pairs={{0,8},{1,9},{2,10},{3,11},{4,12},{5,13},{6,14},{7,15},{8,0},{9,1},... | collective-permute-start | bytes 393224 | tf_op jit(solution)/shard_map/ppermute | solution.py:341
  31.8 0.6 collective-permute-start.13
  32.4 1.3 %collective-permute-start.14 = (bf16[1,512,128]{2,1,0:T(8,128)(2,1)S(1)}, bf16[1,512,128]{2,1,0:T(8,128)(2,1)S(1)}, u32[]{:S(2)}, u32[]{:S(2)}) collective-permute-start(bf16[1,512,128]{2,1,0:T(8,128)(2,1)S(1)} %bitcast.16), channel_id=1, source_target_pairs={{0,24},{1,25},{2,26},{3,27},{4,28},{5,29},{6,30},{7,31},{8,16},{9,... | collective-permute-start | bytes 393224 | tf_op jit(solution)/shard_map/ppermute | solution.py:341
  33.7 2.2 %copy-done = bf16[2048,1024]{1,0:T(8,128)(2,1)S(1)} copy-done((bf16[2048,1024]{1,0:T(8,128)(2,1)S(1)}, bf16[2048,1024]{1,0:T(8,128)(2,1)}, u32[]{:S(2)}) %copy-start) | copy-done | bytes 4194328
  35.9 0.3 load.1.refs_4_.refs_3_.refs_1_
  36.2 4.0 %piece_product.3.refs_3_ = f32[2048,128]{1,0:T(8,128)S(1)} custom-call(bf16[1,512,128]{2,1,0:T(8,128)(2,1)S(1)} %bitcast.21, bf16[1,512,128]{2,1,0:T(8,128)(2,1)S(1)} %collective-permute-done.17.refs_1_, bf16[1,512,128]{2,1,0:T(8,128)(2,1)S(1)} %collective-permute-done.18.refs_2_, bf16[2048,1024]{1,0:T(8,128)(2,1)S(1)} %load.1.refs_4_.refs_3_.refs_1_, ...), custom_call_target="tpu_custom_call" | custom-call | flops 805306368 | bytes 6291456 | tf_op jit(solution)/shard_map/piece_product/pallas_call | solution.py:194
  40.2 2.6 %piece_product.5.x = bf16[1024,128]{1,0:T(8,128)(2,1)S(1)} custom-call(bf16[1,512,128]{2,1,0:T(8,128)(2,1)S(1)} %collective-permute-done.16.refs_0_, bf16[2048,1024]{1,0:T(8,128)(2,1)S(1)} %load.1.refs_4_.refs_3_.refs_1_, bf16[2048,1024]{1,0:T(8,128)(2,1)} %collective-permute-done.6.refs_5_.refs_4_.refs_2_, f32[2048,128]{1,0:T(8,128)S(1)} %piece_product.3.refs_3_), custom_call_target="tpu_custom_call" | custom-call | flops 134217728 | bytes 1048576 | tf_op jit(solution)/shard_map/piece_product/pallas_call | solution.py:194
  42.9 9.5 %collective-permute-start.24 = (bf16[1024,128]{1,0:T(8,128)(2,1)S(1)}, bf16[1024,128]{1,0:T(8,128)(2,1)S(1)}, u32[]{:S(2)}, u32[]{:S(2)}) collective-permute-start(bf16[1024,128]{1,0:T(8,128)(2,1)S(1)} %piece_product.5.x), channel_id=1, source_target_pairs={{0,2},{1,3},{2,0},{3,1},{4,6},{5,7},{6,4},{7,5},{8,10},{9,11},{10,... | collective-permute-start | bytes 786440 | tf_op jit(solution)/shard_map/ppermute | solution.py:341
  52.4 2.6 %piece_product.4.x = bf16[1024,128]{1,0:T(8,128)(2,1)S(1)} custom-call(bf16[1,512,128]{2,1,0:T(8,128)(2,1)S(1)} %collective-permute-done.16.refs_0_, bf16[2048,1024]{1,0:T(8,128)(2,1)S(1)} %load.1.refs_4_.refs_3_.refs_1_, bf16[2048,1024]{1,0:T(8,128)(2,1)} %collective-permute-done.6.refs_5_.refs_4_.refs_2_, f32[2048,128]{1,0:T(8,128)S(1)} %piece_product.3.refs_3_), custom_call_target="tpu_custom_call" | custom-call | flops 134217728 | bytes 1048576 | tf_op jit(solution)/shard_map/piece_product/pallas_call | solution.py:194
  55.1 0.1 collective-permute-start.19
  55.2 2.0 %collective-permute-start.7 = (bf16[512,128]{1,0:T(8,128)(2,1)S(1)}, bf16[512,128]{1,0:T(8,128)(2,1)S(1)}, u32[]{:S(2)}, u32[]{:S(2)}) collective-permute-start(bf16[512,128]{1,0:T(8,128)(2,1)S(1)} %get-tuple-element.26), channel_id=1, source_target_pairs={{0,2},{1,3},{2,0},{3,1},{4,6},{5,7},{6,4},{7,5},{8,10},{9,11},{10,... | collective-permute-start | bytes 393224 | tf_op jit(solution)/shard_map/ppermute | solution.py:341
  57.2 4.6 %partial_product.5 = (bf16[1024,128]{1,0:T(8,128)(2,1)S(1)}, bf16[1024,128]{1,0:T(8,128)(2,1)S(1)}) custom-call(bf16[1,512,128]{2,1,0:T(8,128)(2,1)S(1)} %bitcast.17, bf16[1,512,128]{2,1,0:T(8,128)(2,1)S(1)} %collective-permute-done.12.refs_1_, bf16[1,512,128]{2,1,0:T(8,128)(2,1)S(1)} %collective-permute-done.13.refs_2_, ...), custom_call_target="tpu_custom_call" | custom-call | flops 1073741824 | bytes 8388608 | tf_op jit(solution)/shard_map/partial_product/pallas_call | solution.py:153
  61.7 0.2 collective-permute-start.27
  62.0 4.6 %collective-permute-done.7 = bf16[512,128]{1,0:T(8,128)(2,1)S(1)} collective-permute-done((bf16[512,128]{1,0:T(8,128)(2,1)S(1)}, bf16[512,128]{1,0:T(8,128)(2,1)S(1)}, u32[]{:S(2)}, u32[]{:S(2)}) %collective-permute-start.7) | collective-permute-done | bytes 131104 | tf_op jit(solution)/shard_map/ppermute | solution.py:341
  66.6 1.7 %collective-permute-start.10 = (bf16[1,512,128]{2,1,0:T(8,128)(2,1)S(1)}, bf16[1,512,128]{2,1,0:T(8,128)(2,1)S(1)}, u32[]{:S(2)}, u32[]{:S(2)}) collective-permute-start(bf16[1,512,128]{2,1,0:T(8,128)(2,1)S(1)} %bitcast.10), channel_id=1, source_target_pairs={{0,24},{1,25},{2,26},{3,27},{4,28},{5,29},{6,30},{7,31},{8,16},{9,... | collective-permute-start | bytes 393224 | tf_op jit(solution)/shard_map/ppermute | solution.py:341
  68.3 1.4 %collective-permute-start.8 = (bf16[1,512,128]{2,1,0:T(8,128)(2,1)S(1)}, bf16[1,512,128]{2,1,0:T(8,128)(2,1)S(1)}, u32[]{:S(2)}, u32[]{:S(2)}) collective-permute-start(bf16[1,512,128]{2,1,0:T(8,128)(2,1)S(1)} %bitcast.11), channel_id=1, source_target_pairs={{0,8},{1,9},{2,10},{3,11},{4,12},{5,13},{6,14},{7,15},{8,0},{9,1},... | collective-permute-start | bytes 393224 | tf_op jit(solution)/shard_map/ppermute | solution.py:341
  69.7 0.3 collective-permute-start.9
  70.1 2.0 %collective-permute-start.22 = (bf16[1024,128]{1,0:T(8,128)(2,1)S(1)}, bf16[1024,128]{1,0:T(8,128)(2,1)S(1)}, u32[]{:S(2)}, u32[]{:S(2)}) collective-permute-start(bf16[1024,128]{1,0:T(8,128)(2,1)S(1)} %get-tuple-element.29.x), channel_id=1, source_target_pairs={{0,2},{1,3},{2,0},{3,1},{4,6},{5,7},{6,4},{7,5},{8,10},{9,11},{10,... | collective-permute-start | bytes 786440 | tf_op jit(solution)/shard_map/ppermute | solution.py:341
  72.1 0.1 add.29
  72.2 0.1 add.26
  72.3 0.2 collective-permute-done.10.refs_3_
  72.5 1.6 %collective-permute-done.8.refs_1_ = bf16[1,512,128]{2,1,0:T(8,128)(2,1)S(1)} collective-permute-done((bf16[1,512,128]{2,1,0:T(8,128)(2,1)S(1)}, bf16[1,512,128]{2,1,0:T(8,128)(2,1)S(1)}, u32[]{:S(2)}, u32[]{:S(2)}) %collective-permute-start.8) | collective-permute-done | bytes 131104 | tf_op jit(solution)/shard_map/ppermute | solution.py:341
  74.1 0.6 collective-permute-done.9.refs_2_
  74.7 2.7 %collective-permute-start.29 = (bf16[1024,128]{1,0:T(8,128)(2,1)S(1)}, bf16[1024,128]{1,0:T(8,128)(2,1)S(1)}, u32[]{:S(2)}, u32[]{:S(2)}) collective-permute-start(bf16[1024,128]{1,0:T(8,128)(2,1)S(1)} %copy-done.1), channel_id=1, source_target_pairs={{0,2},{1,3},{2,0},{3,1},{4,6},{5,7},{6,4},{7,5},{8,10},{9,11},{10,... | collective-permute-start | bytes 786440 | tf_op jit(solution)/shard_map/ppermute | solution.py:341
  77.4 0.1 collective-permute-start.30
  77.5 2.2 %collective-permute-start.3 = (bf16[1,512,128]{2,1,0:T(8,128)(2,1)S(1)}, bf16[1,512,128]{2,1,0:T(8,128)(2,1)S(1)}, u32[]{:S(2)}, u32[]{:S(2)}) collective-permute-start(bf16[1,512,128]{2,1,0:T(8,128)(2,1)S(1)} %bitcast.6), channel_id=1, source_target_pairs={{0,8},{1,9},{2,10},{3,11},{4,12},{5,13},{6,14},{7,15},{8,0},{9,1},... | collective-permute-start | bytes 393224 | tf_op jit(solution)/shard_map/ppermute | solution.py:341
  79.7 1.5 %collective-permute-start.5 = (bf16[1,512,128]{2,1,0:T(8,128)(2,1)S(1)}, bf16[1,512,128]{2,1,0:T(8,128)(2,1)S(1)}, u32[]{:S(2)}, u32[]{:S(2)}) collective-permute-start(bf16[1,512,128]{2,1,0:T(8,128)(2,1)S(1)} %bitcast.8), channel_id=1, source_target_pairs={{0,24},{1,25},{2,26},{3,27},{4,28},{5,29},{6,30},{7,31},{8,16},{9,... | collective-permute-start | bytes 393224 | tf_op jit(solution)/shard_map/ppermute | solution.py:341
  81.2 4.6 %partial_product.4 = (bf16[1024,128]{1,0:T(8,128)(2,1)S(1)}, bf16[1024,128]{1,0:T(8,128)(2,1)S(1)}) custom-call(bf16[1,512,128]{2,1,0:T(8,128)(2,1)S(1)} %bitcast.13, bf16[1,512,128]{2,1,0:T(8,128)(2,1)S(1)} %collective-permute-done.8.refs_1_, bf16[1,512,128]{2,1,0:T(8,128)(2,1)S(1)} %collective-permute-done.9.refs_2_, ...), custom_call_target="tpu_custom_call" | custom-call | flops 1073741824 | bytes 8388608 | tf_op jit(solution)/shard_map/partial_product/pallas_call | solution.py:153
  85.8 0.1 add.31.refs_0_
  85.9 0.1 add.28.refs_1_
  85.9 0.4 ahead.5
  86.3 0.1 add.30.refs_0_
  86.4 0.1 add.27.refs_1_
  86.5 0.1 collective-permute-start.34
  86.6 1.8 %collective-permute-done.30.refs_3_ = bf16[1024,128]{1,0:T(8,128)(2,1)S(1)} collective-permute-done((bf16[1024,128]{1,0:T(8,128)(2,1)S(1)}, bf16[1024,128]{1,0:T(8,128)(2,1)S(1)}, u32[]{:S(2)}, u32[]{:S(2)}) %collective-permute-start.30) | collective-permute-done | bytes 262176 | tf_op jit(solution)/shard_map/ppermute | solution.py:341
  88.4 0.4 ahead.4
  88.8 3.8 %collective-permute-start.31 = (bf16[128,128]{1,0:T(8,128)(2,1)S(1)}, bf16[128,128]{1,0:T(8,128)(2,1)S(1)}, u32[]{:S(2)}, u32[]{:S(2)}) collective-permute-start(bf16[128,128]{1,0:T(8,128)(2,1)S(1)} %ahead.4), channel_id=1, source_target_pairs={{0,2},{1,3},{2,0},{3,1},{4,6},{5,7},{6,4},{7,5},{8,10},{9,11},{10,... | collective-permute-start | bytes 98312 | tf_op jit(solution)/shard_map/ppermute | solution.py:341
  92.6 4.6 %partial_product.3 = (bf16[1024,128]{1,0:T(8,128)(2,1)S(1)}, bf16[1024,128]{1,0:T(8,128)(2,1)S(1)}) custom-call(bf16[1,512,128]{2,1,0:T(8,128)(2,1)S(1)} %bitcast.9, bf16[1,512,128]{2,1,0:T(8,128)(2,1)S(1)} %collective-permute-done.3.refs_1_, bf16[1,512,128]{2,1,0:T(8,128)(2,1)S(1)} %collective-permute-done.4.refs_2_, ...), custom_call_target="tpu_custom_call" | custom-call | flops 1073741824 | bytes 8388608 | tf_op jit(solution)/shard_map/partial_product/pallas_call | solution.py:153
  97.2 0.4 ahead.3.diag
  97.6 1.4 %collective-permute-start.35 = (bf16[128,128]{1,0:T(8,128)(2,1)S(1)}, bf16[128,128]{1,0:T(8,128)(2,1)S(1)}, u32[]{:S(2)}, u32[]{:S(2)}) collective-permute-start(bf16[128,128]{1,0:T(8,128)(2,1)S(1)} %get-tuple-element.37), channel_id=1, source_target_pairs={{0,8},{1,9},{2,10},{3,11},{4,12},{5,13},{6,14},{7,15},{8,0},{9,1},... | collective-permute-start | bytes 98312 | tf_op jit(solution)/shard_map/ppermute | solution.py:341
  99.0 0.1 collective-permute-start.36
  99.2 2.0 %collective-permute-start.37 = (bf16[128,128]{1,0:T(8,128)(2,1)S(1)}, bf16[128,128]{1,0:T(8,128)(2,1)S(1)}, u32[]{:S(2)}, u32[]{:S(2)}) collective-permute-start(bf16[128,128]{1,0:T(8,128)(2,1)S(1)} %get-tuple-element.37), channel_id=1, source_target_pairs={{0,24},{1,25},{2,26},{3,27},{4,28},{5,29},{6,30},{7,31},{8,16},{9,... | collective-permute-start | bytes 98312 | tf_op jit(solution)/shard_map/ppermute | solution.py:341
  101.2 0.7 collective-permute-start.26
  101.8 1.1 collective-permute-done.36
  103.0 0.9 collective-permute-start.21
  103.8 0.2 collective-permute-done.37
  104.0 0.7 bitcast_add_fusion
  104.6 5.7 %collective-permute-done.26.refs_1_ = bf16[1024,128]{1,0:T(8,128)(2,1)S(1)} collective-permute-done((bf16[1024,128]{1,0:T(8,128)(2,1)S(1)}, bf16[1024,128]{1,0:T(8,128)(2,1)S(1)}, u32[]{:S(2)}, u32[]{:S(2)}) %collective-permute-start.26) | collective-permute-done | bytes 262176 | tf_op jit(solution)/shard_map/ppermute | solution.py:341
  110.4 1.6 %masked.2.refs_3_ = f32[128,2048]{1,0:T(8,128)} custom-call(s32[8,64]{1,0:T(8,128)S(1)} %copy-done.4, bf16[1024,128]{1,0:T(8,128)(2,1)S(1)} %get-tuple-element.31.refs_0_, bf16[1024,128]{1,0:T(8,128)(2,1)S(1)} %collective-permute-done.26.refs_1_, bf16[1024,128]{1,0:T(8,128)(2,1)S(1)} %collective-permute-done.28.refs_2_), custom_call_target="tpu_custom_call" | custom-call | flops 524288 | bytes 1310720 | tf_op jit(solution)/shard_map/masked/pallas_call | solution.py:311
  112.0 3.5 %collective-permute-done.21.refs_1_ = bf16[1024,128]{1,0:T(8,128)(2,1)S(1)} collective-permute-done((bf16[1024,128]{1,0:T(8,128)(2,1)S(1)}, bf16[1024,128]{1,0:T(8,128)(2,1)S(1)}, u32[]{:S(2)}, u32[]{:S(2)}) %collective-permute-start.21) | collective-permute-done | bytes 262176 | tf_op jit(solution)/shard_map/ppermute | solution.py:341
  115.5 1.6 %masked.3 = f32[128,2048]{1,0:T(8,128)} custom-call(s32[8,64]{1,0:T(8,128)S(1)} %copy-done.4, bf16[1024,128]{1,0:T(8,128)(2,1)S(1)} %get-tuple-element.25.refs_0_.refs_1_, bf16[1024,128]{1,0:T(8,128)(2,1)S(1)} %collective-permute-done.21.refs_1_, bf16[1024,128]{1,0:T(8,128)(2,1)S(1)} %collective-permute-done.23.refs_2_, ...), custom_call_target="tpu_custom_call", output_to_operand_aliasing={{}: (4, {})} | custom-call | flops 524288 | bytes 1310720 | tf_op jit(solution)/shard_map/masked/pallas_call | solution.py:311
  (46 shorter events, 0.2 us)
Async XLA Ops:
  0.6 33.1 %collective-permute-start.6 = (bf16[2048,1024]{1,0:T(8,128)(2,1)}, bf16[2048,1024]{1,0:T(8,128)(2,1)}, u32[]{:S(2)}, u32[]{:S(2)}) collective-permute-start(bf16[2048,1024]{1,0:T(8,128)(2,1)} %tile.1), channel_id=1, source_target_pairs={{0,1},{1,0},{2,3},{3,2},{4,5},{5,4},{6,7},{7,6},{8,9},{9,8},{10,11... | collective-permute-start | bytes 12582920 | tf_op jit(solution)/shard_map/ppermute | solution.py:341
  3.9 7.1 %collective-permute-start = (bf16[512,128]{1,0:T(8,128)(2,1)}, bf16[512,128]{1,0:T(8,128)(2,1)S(1)}, u32[]{:S(2)}, u32[]{:S(2)}) collective-permute-start(bf16[512,128]{1,0:T(8,128)(2,1)} %get-tuple-element.21), channel_id=1, source_target_pairs={{0,8},{1,9},{2,10},{3,11},{4,12},{5,13},{6,14},{7,15},{8,0},{9,1},... | collective-permute-start | bytes 393224 | tf_op jit(solution)/shard_map/ppermute | solution.py:341
  6.4 8.6 %collective-permute-start.1 = (bf16[512,128]{1,0:T(8,128)(2,1)}, bf16[512,128]{1,0:T(8,128)(2,1)S(1)}, u32[]{:S(2)}, u32[]{:S(2)}) collective-permute-start(bf16[512,128]{1,0:T(8,128)(2,1)} %get-tuple-element.22), channel_id=1, source_target_pairs={{0,16},{1,17},{2,18},{3,19},{4,20},{5,21},{6,22},{7,23},{8,24},{9,... | collective-permute-start | bytes 393224 | tf_op jit(solution)/shard_map/ppermute | solution.py:341
  7.9 7.1 %collective-permute-start.2 = (bf16[512,128]{1,0:T(8,128)(2,1)}, bf16[512,128]{1,0:T(8,128)(2,1)S(1)}, u32[]{:S(2)}, u32[]{:S(2)}) collective-permute-start(bf16[512,128]{1,0:T(8,128)(2,1)} %get-tuple-element.23), channel_id=1, source_target_pairs={{0,24},{1,25},{2,26},{3,27},{4,28},{5,29},{6,30},{7,31},{8,16},{9,... | collective-permute-start | bytes 393224 | tf_op jit(solution)/shard_map/ppermute | solution.py:341
  15.0 0.9 copy-start.3
  16.0 8.1 %collective-permute-start.15 = (bf16[512,128]{1,0:T(8,128)(2,1)S(1)}, bf16[512,128]{1,0:T(8,128)(2,1)S(1)}, u32[]{:S(2)}, u32[]{:S(2)}) collective-permute-start(bf16[512,128]{1,0:T(8,128)(2,1)S(1)} %get-tuple-element.30), channel_id=1, source_target_pairs={{0,6},{1,7},{2,4},{3,5},{4,2},{5,3},{6,0},{7,1},{8,14},{9,15},{10,... | collective-permute-start | bytes 393224 | tf_op jit(solution)/shard_map/ppermute | solution.py:341
  19.7 10.5 %collective-permute-start.11 = (bf16[512,128]{1,0:T(8,128)(2,1)S(1)}, bf16[512,128]{1,0:T(8,128)(2,1)S(1)}, u32[]{:S(2)}, u32[]{:S(2)}) collective-permute-start(bf16[512,128]{1,0:T(8,128)(2,1)S(1)} %get-tuple-element.28), channel_id=1, source_target_pairs={{0,4},{1,5},{2,6},{3,7},{4,0},{5,1},{6,2},{7,3},{8,12},{9,13},{10,... | collective-permute-start | bytes 393224 | tf_op jit(solution)/shard_map/ppermute | solution.py:341
  24.1 7.7 %collective-permute-start.17 = (bf16[1,512,128]{2,1,0:T(8,128)(2,1)S(1)}, bf16[1,512,128]{2,1,0:T(8,128)(2,1)S(1)}, u32[]{:S(2)}, u32[]{:S(2)}) collective-permute-start(bf16[1,512,128]{2,1,0:T(8,128)(2,1)S(1)} %bitcast.18), channel_id=1, source_target_pairs={{0,8},{1,9},{2,10},{3,11},{4,12},{5,13},{6,14},{7,15},{8,0},{9,1},... | collective-permute-start | bytes 393224 | tf_op jit(solution)/shard_map/ppermute | solution.py:341
  25.5 6.3 %collective-permute-start.18 = (bf16[1,512,128]{2,1,0:T(8,128)(2,1)S(1)}, bf16[1,512,128]{2,1,0:T(8,128)(2,1)S(1)}, u32[]{:S(2)}, u32[]{:S(2)}) collective-permute-start(bf16[1,512,128]{2,1,0:T(8,128)(2,1)S(1)} %bitcast.19), channel_id=1, source_target_pairs={{0,16},{1,17},{2,18},{3,19},{4,20},{5,21},{6,22},{7,23},{8,24},{9,... | collective-permute-start | bytes 393224 | tf_op jit(solution)/shard_map/ppermute | solution.py:341
  26.3 6.1 %collective-permute-start.16 = (bf16[1,512,128]{2,1,0:T(8,128)(2,1)S(1)}, bf16[1,512,128]{2,1,0:T(8,128)(2,1)S(1)}, u32[]{:S(2)}, u32[]{:S(2)}) collective-permute-start(bf16[1,512,128]{2,1,0:T(8,128)(2,1)S(1)} %bitcast.20), channel_id=1, source_target_pairs={{0,24},{1,25},{2,26},{3,27},{4,28},{5,29},{6,30},{7,31},{8,16},{9,... | collective-permute-start | bytes 393224 | tf_op jit(solution)/shard_map/ppermute | solution.py:341
  30.2 12.7 %collective-permute-start.12 = (bf16[1,512,128]{2,1,0:T(8,128)(2,1)S(1)}, bf16[1,512,128]{2,1,0:T(8,128)(2,1)S(1)}, u32[]{:S(2)}, u32[]{:S(2)}) collective-permute-start(bf16[1,512,128]{2,1,0:T(8,128)(2,1)S(1)} %bitcast.14), channel_id=1, source_target_pairs={{0,8},{1,9},{2,10},{3,11},{4,12},{5,13},{6,14},{7,15},{8,0},{9,1},... | collective-permute-start | bytes 393224 | tf_op jit(solution)/shard_map/ppermute | solution.py:341
  31.8 30.0 %collective-permute-start.32 = (bf16[1024,128]{1,0:T(8,128)(2,1)}, bf16[1024,128]{1,0:T(8,128)(2,1)S(1)}, u32[]{:S(2)}, u32[]{:S(2)}) collective-permute-start(bf16[1024,128]{1,0:T(8,128)(2,1)} %get-tuple-element.34.refs_2_), channel_id=1, source_target_pairs={{0,1},{1,0},{2,4},{3,5},{4,2},{5,3},{6,7},{7,6},{8,9},{9,8},{10,12... | collective-permute-start | bytes 786440 | tf_op jit(solution)/shard_map/ppermute | solution.py:341
  31.8 23.3 %collective-permute-start.13 = (bf16[1,512,128]{2,1,0:T(8,128)(2,1)S(1)}, bf16[1,512,128]{2,1,0:T(8,128)(2,1)S(1)}, u32[]{:S(2)}, u32[]{:S(2)}) collective-permute-start(bf16[1,512,128]{2,1,0:T(8,128)(2,1)S(1)} %bitcast.15), channel_id=1, source_target_pairs={{0,16},{1,17},{2,18},{3,19},{4,20},{5,21},{6,22},{7,23},{8,24},{9,... | collective-permute-start | bytes 393224 | tf_op jit(solution)/shard_map/ppermute | solution.py:341
  32.4 22.7 %collective-permute-start.14 = (bf16[1,512,128]{2,1,0:T(8,128)(2,1)S(1)}, bf16[1,512,128]{2,1,0:T(8,128)(2,1)S(1)}, u32[]{:S(2)}, u32[]{:S(2)}) collective-permute-start(bf16[1,512,128]{2,1,0:T(8,128)(2,1)S(1)} %bitcast.16), channel_id=1, source_target_pairs={{0,24},{1,25},{2,26},{3,27},{4,28},{5,29},{6,30},{7,31},{8,16},{9,... | collective-permute-start | bytes 393224 | tf_op jit(solution)/shard_map/ppermute | solution.py:341
  33.7 34.6 %collective-permute-start.33 = (bf16[1024,128]{1,0:T(8,128)(2,1)}, bf16[1024,128]{1,0:T(8,128)(2,1)S(1)}, u32[]{:S(2)}, u32[]{:S(2)}) collective-permute-start(bf16[1024,128]{1,0:T(8,128)(2,1)} %get-tuple-element.35.refs_3_), channel_id=1, source_target_pairs={{0,1},{1,0},{2,4},{3,5},{4,2},{5,3},{6,7},{7,6},{8,9},{9,8},{10,12... | collective-permute-start | bytes 786440 | tf_op jit(solution)/shard_map/ppermute | solution.py:341
  33.7 2.2 %copy-start = (bf16[2048,1024]{1,0:T(8,128)(2,1)S(1)}, bf16[2048,1024]{1,0:T(8,128)(2,1)}, u32[]{:S(2)}) copy-start(bf16[2048,1024]{1,0:T(8,128)(2,1)} %tile.1) | copy-start | bytes 12582916
  42.9 26.9 %collective-permute-start.24 = (bf16[1024,128]{1,0:T(8,128)(2,1)S(1)}, bf16[1024,128]{1,0:T(8,128)(2,1)S(1)}, u32[]{:S(2)}, u32[]{:S(2)}) collective-permute-start(bf16[1024,128]{1,0:T(8,128)(2,1)S(1)} %piece_product.5.x), channel_id=1, source_target_pairs={{0,2},{1,3},{2,0},{3,1},{4,6},{5,7},{6,4},{7,5},{8,10},{9,11},{10,... | collective-permute-start | bytes 786440 | tf_op jit(solution)/shard_map/ppermute | solution.py:341
  55.1 15.0 %collective-permute-start.19 = (bf16[1024,128]{1,0:T(8,128)(2,1)S(1)}, bf16[1024,128]{1,0:T(8,128)(2,1)S(1)}, u32[]{:S(2)}, u32[]{:S(2)}) collective-permute-start(bf16[1024,128]{1,0:T(8,128)(2,1)S(1)} %piece_product.4.x), channel_id=1, source_target_pairs={{0,2},{1,3},{2,0},{3,1},{4,6},{5,7},{6,4},{7,5},{8,10},{9,11},{10,... | collective-permute-start | bytes 786440 | tf_op jit(solution)/shard_map/ppermute | solution.py:341
  55.2 19.6 %copy-start.1 = (bf16[1024,128]{1,0:T(8,128)(2,1)S(1)}, bf16[1024,128]{1,0:T(8,128)(2,1)}, u32[]{:S(2)}) copy-start(bf16[1024,128]{1,0:T(8,128)(2,1)} %get-tuple-element.34.refs_2_) | copy-start | bytes 786436
  55.2 22.2 %copy-start.2 = (bf16[1024,128]{1,0:T(8,128)(2,1)S(1)}, bf16[1024,128]{1,0:T(8,128)(2,1)}, u32[]{:S(2)}) copy-start(bf16[1024,128]{1,0:T(8,128)(2,1)} %get-tuple-element.35.refs_3_) | copy-start | bytes 786436
  55.2 11.4 %collective-permute-start.7 = (bf16[512,128]{1,0:T(8,128)(2,1)S(1)}, bf16[512,128]{1,0:T(8,128)(2,1)S(1)}, u32[]{:S(2)}, u32[]{:S(2)}) collective-permute-start(bf16[512,128]{1,0:T(8,128)(2,1)S(1)} %get-tuple-element.26), channel_id=1, source_target_pairs={{0,2},{1,3},{2,0},{3,1},{4,6},{5,7},{6,4},{7,5},{8,10},{9,11},{10,... | collective-permute-start | bytes 393224 | tf_op jit(solution)/shard_map/ppermute | solution.py:341
  61.7 15.7 %collective-permute-start.27 = (bf16[1024,128]{1,0:T(8,128)(2,1)S(1)}, bf16[1024,128]{1,0:T(8,128)(2,1)S(1)}, u32[]{:S(2)}, u32[]{:S(2)}) collective-permute-start(bf16[1024,128]{1,0:T(8,128)(2,1)S(1)} %get-tuple-element.33.x), channel_id=1, source_target_pairs={{0,2},{1,3},{2,0},{3,1},{4,6},{5,7},{6,4},{7,5},{8,10},{9,11},{10,... | collective-permute-start | bytes 786440 | tf_op jit(solution)/shard_map/ppermute | solution.py:341
  66.6 5.9 %collective-permute-start.10 = (bf16[1,512,128]{2,1,0:T(8,128)(2,1)S(1)}, bf16[1,512,128]{2,1,0:T(8,128)(2,1)S(1)}, u32[]{:S(2)}, u32[]{:S(2)}) collective-permute-start(bf16[1,512,128]{2,1,0:T(8,128)(2,1)S(1)} %bitcast.10), channel_id=1, source_target_pairs={{0,24},{1,25},{2,26},{3,27},{4,28},{5,29},{6,30},{7,31},{8,16},{9,... | collective-permute-start | bytes 393224 | tf_op jit(solution)/shard_map/ppermute | solution.py:341
  68.3 5.7 %collective-permute-start.8 = (bf16[1,512,128]{2,1,0:T(8,128)(2,1)S(1)}, bf16[1,512,128]{2,1,0:T(8,128)(2,1)S(1)}, u32[]{:S(2)}, u32[]{:S(2)}) collective-permute-start(bf16[1,512,128]{2,1,0:T(8,128)(2,1)S(1)} %bitcast.11), channel_id=1, source_target_pairs={{0,8},{1,9},{2,10},{3,11},{4,12},{5,13},{6,14},{7,15},{8,0},{9,1},... | collective-permute-start | bytes 393224 | tf_op jit(solution)/shard_map/ppermute | solution.py:341
  69.7 5.0 %collective-permute-start.9 = (bf16[1,512,128]{2,1,0:T(8,128)(2,1)S(1)}, bf16[1,512,128]{2,1,0:T(8,128)(2,1)S(1)}, u32[]{:S(2)}, u32[]{:S(2)}) collective-permute-start(bf16[1,512,128]{2,1,0:T(8,128)(2,1)S(1)} %bitcast.12), channel_id=1, source_target_pairs={{0,16},{1,17},{2,18},{3,19},{4,20},{5,21},{6,22},{7,23},{8,24},{9,... | collective-permute-start | bytes 393224 | tf_op jit(solution)/shard_map/ppermute | solution.py:341
  70.1 7.4 %collective-permute-start.22 = (bf16[1024,128]{1,0:T(8,128)(2,1)S(1)}, bf16[1024,128]{1,0:T(8,128)(2,1)S(1)}, u32[]{:S(2)}, u32[]{:S(2)}) collective-permute-start(bf16[1024,128]{1,0:T(8,128)(2,1)S(1)} %get-tuple-element.29.x), channel_id=1, source_target_pairs={{0,2},{1,3},{2,0},{3,1},{4,6},{5,7},{6,4},{7,5},{8,10},{9,11},{10,... | collective-permute-start | bytes 786440 | tf_op jit(solution)/shard_map/ppermute | solution.py:341
  72.5 7.3 %collective-permute-start.25 = (bf16[1024,128]{1,0:T(8,128)(2,1)S(1)}, bf16[1024,128]{1,0:T(8,128)(2,1)S(1)}, u32[]{:S(2)}, u32[]{:S(2)}) collective-permute-start(bf16[1024,128]{1,0:T(8,128)(2,1)S(1)} %add.29), channel_id=1, source_target_pairs={{0,1},{1,0},{2,4},{3,5},{4,2},{5,3},{6,7},{7,6},{8,9},{9,8},{10,12... | collective-permute-start | bytes 786440 | tf_op jit(solution)/shard_map/ppermute | solution.py:341
  74.1 5.7 %collective-permute-start.20 = (bf16[1024,128]{1,0:T(8,128)(2,1)S(1)}, bf16[1024,128]{1,0:T(8,128)(2,1)S(1)}, u32[]{:S(2)}, u32[]{:S(2)}) collective-permute-start(bf16[1024,128]{1,0:T(8,128)(2,1)S(1)} %add.26), channel_id=1, source_target_pairs={{0,1},{1,0},{2,4},{3,5},{4,2},{5,3},{6,7},{7,6},{8,9},{9,8},{10,12... | collective-permute-start | bytes 786440 | tf_op jit(solution)/shard_map/ppermute | solution.py:341
  74.7 11.8 %collective-permute-start.29 = (bf16[1024,128]{1,0:T(8,128)(2,1)S(1)}, bf16[1024,128]{1,0:T(8,128)(2,1)S(1)}, u32[]{:S(2)}, u32[]{:S(2)}) collective-permute-start(bf16[1024,128]{1,0:T(8,128)(2,1)S(1)} %copy-done.1), channel_id=1, source_target_pairs={{0,2},{1,3},{2,0},{3,1},{4,6},{5,7},{6,4},{7,5},{8,10},{9,11},{10,... | collective-permute-start | bytes 786440 | tf_op jit(solution)/shard_map/ppermute | solution.py:341
  77.4 11.0 %collective-permute-start.30 = (bf16[1024,128]{1,0:T(8,128)(2,1)S(1)}, bf16[1024,128]{1,0:T(8,128)(2,1)S(1)}, u32[]{:S(2)}, u32[]{:S(2)}) collective-permute-start(bf16[1024,128]{1,0:T(8,128)(2,1)S(1)} %copy-done.2), channel_id=1, source_target_pairs={{0,2},{1,3},{2,0},{3,1},{4,6},{5,7},{6,4},{7,5},{8,10},{9,11},{10,... | collective-permute-start | bytes 786440 | tf_op jit(solution)/shard_map/ppermute | solution.py:341
  77.5 15.1 %collective-permute-start.3 = (bf16[1,512,128]{2,1,0:T(8,128)(2,1)S(1)}, bf16[1,512,128]{2,1,0:T(8,128)(2,1)S(1)}, u32[]{:S(2)}, u32[]{:S(2)}) collective-permute-start(bf16[1,512,128]{2,1,0:T(8,128)(2,1)S(1)} %bitcast.6), channel_id=1, source_target_pairs={{0,8},{1,9},{2,10},{3,11},{4,12},{5,13},{6,14},{7,15},{8,0},{9,1},... | collective-permute-start | bytes 393224 | tf_op jit(solution)/shard_map/ppermute | solution.py:341
  79.7 12.9 %collective-permute-start.4 = (bf16[1,512,128]{2,1,0:T(8,128)(2,1)S(1)}, bf16[1,512,128]{2,1,0:T(8,128)(2,1)S(1)}, u32[]{:S(2)}, u32[]{:S(2)}) collective-permute-start(bf16[1,512,128]{2,1,0:T(8,128)(2,1)S(1)} %bitcast.7), channel_id=1, source_target_pairs={{0,16},{1,17},{2,18},{3,19},{4,20},{5,21},{6,22},{7,23},{8,24},{9,... | collective-permute-start | bytes 393224 | tf_op jit(solution)/shard_map/ppermute | solution.py:341
  79.7 12.9 %collective-permute-start.5 = (bf16[1,512,128]{2,1,0:T(8,128)(2,1)S(1)}, bf16[1,512,128]{2,1,0:T(8,128)(2,1)S(1)}, u32[]{:S(2)}, u32[]{:S(2)}) collective-permute-start(bf16[1,512,128]{2,1,0:T(8,128)(2,1)S(1)} %bitcast.8), channel_id=1, source_target_pairs={{0,24},{1,25},{2,26},{3,27},{4,28},{5,29},{6,30},{7,31},{8,16},{9,... | collective-permute-start | bytes 393224 | tf_op jit(solution)/shard_map/ppermute | solution.py:341
  86.5 11.1 %collective-permute-start.34 = (bf16[128,128]{1,0:T(8,128)(2,1)S(1)}, bf16[128,128]{1,0:T(8,128)(2,1)S(1)}, u32[]{:S(2)}, u32[]{:S(2)}) collective-permute-start(bf16[128,128]{1,0:T(8,128)(2,1)S(1)} %ahead.5), channel_id=1, source_target_pairs={{0,1},{1,0},{2,4},{3,5},{4,2},{5,3},{6,7},{7,6},{8,9},{9,8},{10,12... | collective-permute-start | bytes 98312 | tf_op jit(solution)/shard_map/ppermute | solution.py:341
  88.8 15.2 %copy-start.5 = (f32[1,128,128]{2,1,0:T(8,128)S(1)}, f32[1,128,128]{2,1,0:T(8,128)}, u32[]{:S(2)}) copy-start(f32[1,128,128]{2,1,0:T(8,128)} %param.8) | copy-start | bytes 196612
  88.8 21.6 %copy-start.4 = (s32[8,64]{1,0:T(8,128)S(1)}, s32[8,64]{1,0:T(8,128)}, u32[]{:S(2)}) copy-start(s32[8,64]{1,0:T(8,128)} %listed.5) | copy-start | bytes 6148
  88.8 8.8 %collective-permute-start.31 = (bf16[128,128]{1,0:T(8,128)(2,1)S(1)}, bf16[128,128]{1,0:T(8,128)(2,1)S(1)}, u32[]{:S(2)}, u32[]{:S(2)}) collective-permute-start(bf16[128,128]{1,0:T(8,128)(2,1)S(1)} %ahead.4), channel_id=1, source_target_pairs={{0,2},{1,3},{2,0},{3,1},{4,6},{5,7},{6,4},{7,5},{8,10},{9,11},{10,... | collective-permute-start | bytes 98312 | tf_op jit(solution)/shard_map/ppermute | solution.py:341
  97.6 4.2 %collective-permute-start.35 = (bf16[128,128]{1,0:T(8,128)(2,1)S(1)}, bf16[128,128]{1,0:T(8,128)(2,1)S(1)}, u32[]{:S(2)}, u32[]{:S(2)}) collective-permute-start(bf16[128,128]{1,0:T(8,128)(2,1)S(1)} %get-tuple-element.37), channel_id=1, source_target_pairs={{0,8},{1,9},{2,10},{3,11},{4,12},{5,13},{6,14},{7,15},{8,0},{9,1},... | collective-permute-start | bytes 98312 | tf_op jit(solution)/shard_map/ppermute | solution.py:341
  99.0 3.9 %collective-permute-start.36 = (bf16[128,128]{1,0:T(8,128)(2,1)S(1)}, bf16[128,128]{1,0:T(8,128)(2,1)S(1)}, u32[]{:S(2)}, u32[]{:S(2)}) collective-permute-start(bf16[128,128]{1,0:T(8,128)(2,1)S(1)} %get-tuple-element.37), channel_id=1, source_target_pairs={{0,16},{1,17},{2,18},{3,19},{4,20},{5,21},{6,22},{7,23},{8,24},{9,... | collective-permute-start | bytes 98312 | tf_op jit(solution)/shard_map/ppermute | solution.py:341
  99.2 4.8 %collective-permute-start.37 = (bf16[128,128]{1,0:T(8,128)(2,1)S(1)}, bf16[128,128]{1,0:T(8,128)(2,1)S(1)}, u32[]{:S(2)}, u32[]{:S(2)}) collective-permute-start(bf16[128,128]{1,0:T(8,128)(2,1)S(1)} %get-tuple-element.37), channel_id=1, source_target_pairs={{0,24},{1,25},{2,26},{3,27},{4,28},{5,29},{6,30},{7,31},{8,16},{9,... | collective-permute-start | bytes 98312 | tf_op jit(solution)/shard_map/ppermute | solution.py:341
  101.2 3.5 %collective-permute-start.28 = (bf16[1024,128]{1,0:T(8,128)(2,1)S(1)}, bf16[1024,128]{1,0:T(8,128)(2,1)S(1)}, u32[]{:S(2)}, u32[]{:S(2)}) collective-permute-start(bf16[1024,128]{1,0:T(8,128)(2,1)S(1)} %add.31.refs_0_), channel_id=1, source_target_pairs={{0,1},{1,0},{2,4},{3,5},{4,2},{5,3},{6,7},{7,6},{8,9},{9,8},{10,12... | collective-permute-start | bytes 786440 | tf_op jit(solution)/shard_map/ppermute | solution.py:341
  101.2 9.2 %collective-permute-start.26 = (bf16[1024,128]{1,0:T(8,128)(2,1)S(1)}, bf16[1024,128]{1,0:T(8,128)(2,1)S(1)}, u32[]{:S(2)}, u32[]{:S(2)}) collective-permute-start(bf16[1024,128]{1,0:T(8,128)(2,1)S(1)} %add.30.refs_0_), channel_id=1, source_target_pairs={{0,2},{1,3},{2,0},{3,1},{4,6},{5,7},{6,4},{7,5},{8,10},{9,11},{10,... | collective-permute-start | bytes 786440 | tf_op jit(solution)/shard_map/ppermute | solution.py:341
  101.8 10.2 %collective-permute-start.23 = (bf16[1024,128]{1,0:T(8,128)(2,1)S(1)}, bf16[1024,128]{1,0:T(8,128)(2,1)S(1)}, u32[]{:S(2)}, u32[]{:S(2)}) collective-permute-start(bf16[1024,128]{1,0:T(8,128)(2,1)S(1)} %add.28.refs_1_), channel_id=1, source_target_pairs={{0,1},{1,0},{2,4},{3,5},{4,2},{5,3},{6,7},{7,6},{8,9},{9,8},{10,12... | collective-permute-start | bytes 786440 | tf_op jit(solution)/shard_map/ppermute | solution.py:341
  103.0 12.6 %collective-permute-start.21 = (bf16[1024,128]{1,0:T(8,128)(2,1)S(1)}, bf16[1024,128]{1,0:T(8,128)(2,1)S(1)}, u32[]{:S(2)}, u32[]{:S(2)}) collective-permute-start(bf16[1024,128]{1,0:T(8,128)(2,1)S(1)} %add.27.refs_1_), channel_id=1, source_target_pairs={{0,2},{1,3},{2,0},{3,1},{4,6},{5,7},{6,4},{7,5},{8,10},{9,11},{10,... | collective-permute-start | bytes 786440 | tf_op jit(solution)/shard_map/ppermute | solution.py:341

commit v4 on v3

--- a/solution.py
+++ b/solution.py
@@ -13,7 +13,6 @@
 VMEM = pltpu.VMEM
 SMEM = pltpu.SMEM
 LIMIT = 24 << 20
-FULL = 62 << 20
 HALVES = 2
 
 
@@ -72,7 +71,7 @@
             pltpu.VMEM((rows, width), jnp.bfloat16),
             pltpu.SemaphoreType.DMA((n + 2,)),
         ],
-        compiler_params=pltpu.CompilerParams(vmem_limit_bytes=FULL),
+        compiler_params=pltpu.CompilerParams(vmem_limit_bytes=LIMIT),
         cost_estimate=pl.CostEstimate(flops=2 * rows * width * width, bytes_accessed=6 * rows * width, transcendentals=0),
         name="normalize",
     )(listed, panel, unit)
@@ -306,7 +305,7 @@
 
 def masked(n, q, planes, rows, h, listed, parts, before):
     tall, width = parts[0].shape
-    step = min(tall, 512)
+    step = min(tall, 1024)
     count = tall // step
     return pl.pallas_call(
         functools.partial(masked_kernel, n, q, planes, rows, h, len(parts)),
@@ -343,7 +342,7 @@
     def over_rows(x, a):
         return swap(x, lambda p, z, k: (p ^ a, z, k))
 
-    made = normalize(n, listed, l_panel, unit_inverse)
+    made = normalize(n, *[pltpu.with_memory_space_constraint(x, pltpu.HBM) for x in (listed, l_panel, unit_inverse)])
     pieces, lhat = made[:n], made[n:]
     tiles = [load(inverse_tile)]
     tiles += [swap(inverse_tile, lambda p, z, k: (p, z, k ^ e)) for e in range(1, q)]

time: 118 us -> 105 us (0.89)
  Pallas kernels: 30.8 us -> 16.8 us
  waiting for transfers between devices: 33.6 us -> 38 us
  starting transfers between devices: 48.1 us -> 46.5 us
    pallas_call x3, Pallas kernels: 13.7 us -> 7.1 us  [partial_product(): pl.pallas_call(functools.partial(partial_kernel, n, q, halves, min(tall,...]
    pallas_call x3, Pallas kernels: 9.28 us -> 2.73 us  [piece_product(): pl.pallas_call(functools.partial(piece_kernel, n, q, which, base, min(tal...]
    ppermute x38, waiting for transfers between devices: 33.6 us -> 38 us  [swap(): return lax.ppermute(x, AXES, pairs)]
    ppermute x38, starting transfers between devices: 48.1 us -> 46.5 us  [swap(): return lax.ppermute(x, AXES, pairs)]
    unnamed x12 -> x6, local copies, waits for them, and re-layouts: 3.11 us -> 2.2 us
  transfers between devices with their start and end apart: 38 -> 38, of which waited for: 13 -> 13; matrix products, arithmetic and copies ran while one was open for 1% -> 1% of each run, Pallas kernels for 25% -> 14%
where the time goes in v4:
time: 105 us
  starting transfers between devices  46.5 us (44%)
  waiting for transfers between devices  38 us (36%)
  Pallas kernels  16.8 us (16%)
  local copies, waits for them, and re-layouts  2.2 us (2%)
    ppermute x38, starting transfers between devices, swap(): return lax.ppermute(x, AXES, pairs)  46.5 us
    ppermute x38, waiting for transfers between devices, swap(): return lax.ppermute(x, AXES, pairs)  38 us
    pallas_call x3, Pallas kernels, partial_product(): pl.pallas_call(functools.partial(partial_kernel, n, q, halves, min(tall,...  7.1 us
    pallas_call x2, Pallas kernels, masked(): pl.pallas_call(functools.partial(masked_kernel, n, q, planes, rows, h, le...  3.23 us
    pallas_call x3, Pallas kernels, piece_product(): pl.pallas_call(functools.partial(piece_kernel, n, q, which, base, min(tal...  2.73 us
    unnamed x6, local copies, waits for them, and re-layouts  2.2 us
  transfers between devices with their start and end apart: 38, of which 13 were waited for; matrix products, arithmetic and copies ran while one was open for 1% of the time, Pallas kernels for 14%

profile of v4, /device:TPU:0, one launch (start us, length us, event | category | flops | bytes accessed | tf_op | source)
XLA Modules:
  0.0 105.1 jit_solution(9131340528261862513)
XLA Ops:
  0.6 0.6 collective-permute-start.6
  1.2 1.9 %normalize.1 = (bf16[512,128]{1,0:T(8,128)(2,1)S(1)}, bf16[512,128]{1,0:T(8,128)(2,1)S(1)}, bf16[512,128]{1,0:T(8,128)(2,1)S(1)}, bf16[512,128]{1,0:T(8,128)(2,1...) custom-call(s32[8,64]{1,0:T(8,128)} %listed.5, bf16[2048,128]{1,0:T(8,128)(2,1)} %panel.1, ...), custom_call_target="tpu_custom_call" | custom-call | flops 67108864 | bytes 1572864 | tf_op jit(solution)/shard_map/normalize/pallas_call | solution.py:62
  3.1 2.6 %collective-permute-start = (bf16[512,128]{1,0:T(8,128)(2,1)S(1)}, bf16[512,128]{1,0:T(8,128)(2,1)S(1)}, u32[]{:S(2)}, u32[]{:S(2)}) collective-permute-start(bf16[512,128]{1,0:T(8,128)(2,1)S(1)} %get-tuple-element.21), channel_id=1, source_target_pairs={{0,8},{1,9},{2,10},{3,11},{4,12},{5,13},{6,14},{7,15},{8,0},{9,1},... | collective-permute-start | bytes 393224 | tf_op jit(solution)/shard_map/ppermute | solution.py:340
  5.6 1.5 %collective-permute-start.1 = (bf16[512,128]{1,0:T(8,128)(2,1)S(1)}, bf16[512,128]{1,0:T(8,128)(2,1)S(1)}, u32[]{:S(2)}, u32[]{:S(2)}) collective-permute-start(bf16[512,128]{1,0:T(8,128)(2,1)S(1)} %get-tuple-element.22), channel_id=1, source_target_pairs={{0,16},{1,17},{2,18},{3,19},{4,20},{5,21},{6,22},{7,23},{8,24},{9,... | collective-permute-start | bytes 393224 | tf_op jit(solution)/shard_map/ppermute | solution.py:340
  7.1 0.1 collective-permute-start.2
  7.2 2.8 %collective-permute-done.refs_1_ = bf16[512,128]{1,0:T(8,128)(2,1)S(1)} collective-permute-done((bf16[512,128]{1,0:T(8,128)(2,1)S(1)}, bf16[512,128]{1,0:T(8,128)(2,1)S(1)}, u32[]{:S(2)}, u32[]{:S(2)}) %collective-permute-start) | collective-permute-done | bytes 131104 | tf_op jit(solution)/shard_map/ppermute | solution.py:340
  9.9 4.1 %collective-permute-done.1.refs_2_ = bf16[512,128]{1,0:T(8,128)(2,1)S(1)} collective-permute-done((bf16[512,128]{1,0:T(8,128)(2,1)S(1)}, bf16[512,128]{1,0:T(8,128)(2,1)S(1)}, u32[]{:S(2)}, u32[]{:S(2)}) %collective-permute-start.1) | collective-permute-done | bytes 131104 | tf_op jit(solution)/shard_map/ppermute | solution.py:340
  14.1 3.7 %collective-permute-start.15 = (bf16[512,128]{1,0:T(8,128)(2,1)S(1)}, bf16[512,128]{1,0:T(8,128)(2,1)S(1)}, u32[]{:S(2)}, u32[]{:S(2)}) collective-permute-start(bf16[512,128]{1,0:T(8,128)(2,1)S(1)} %get-tuple-element.30), channel_id=1, source_target_pairs={{0,6},{1,7},{2,4},{3,5},{4,2},{5,3},{6,0},{7,1},{8,14},{9,15},{10,... | collective-permute-start | bytes 393224 | tf_op jit(solution)/shard_map/ppermute | solution.py:340
  17.7 4.4 %collective-permute-done.15 = bf16[512,128]{1,0:T(8,128)(2,1)S(1)} collective-permute-done((bf16[512,128]{1,0:T(8,128)(2,1)S(1)}, bf16[512,128]{1,0:T(8,128)(2,1)S(1)}, u32[]{:S(2)}, u32[]{:S(2)}) %collective-permute-start.15) | collective-permute-done | bytes 131104 | tf_op jit(solution)/shard_map/ppermute | solution.py:340
  22.2 1.4 %collective-permute-start.17 = (bf16[1,512,128]{2,1,0:T(8,128)(2,1)S(1)}, bf16[1,512,128]{2,1,0:T(8,128)(2,1)S(1)}, u32[]{:S(2)}, u32[]{:S(2)}) collective-permute-start(bf16[1,512,128]{2,1,0:T(8,128)(2,1)S(1)} %bitcast.18), channel_id=1, source_target_pairs={{0,8},{1,9},{2,10},{3,11},{4,12},{5,13},{6,14},{7,15},{8,0},{9,1},... | collective-permute-start | bytes 393224 | tf_op jit(solution)/shard_map/ppermute | solution.py:340
  23.6 0.8 collective-permute-start.18
  24.4 1.3 %collective-permute-start.16 = (bf16[1,512,128]{2,1,0:T(8,128)(2,1)S(1)}, bf16[1,512,128]{2,1,0:T(8,128)(2,1)S(1)}, u32[]{:S(2)}, u32[]{:S(2)}) collective-permute-start(bf16[1,512,128]{2,1,0:T(8,128)(2,1)S(1)} %bitcast.20), channel_id=1, source_target_pairs={{0,24},{1,25},{2,26},{3,27},{4,28},{5,29},{6,30},{7,31},{8,16},{9,... | collective-permute-start | bytes 393224 | tf_op jit(solution)/shard_map/ppermute | solution.py:340
  25.7 2.6 %collective-permute-done.11 = bf16[512,128]{1,0:T(8,128)(2,1)S(1)} collective-permute-done((bf16[512,128]{1,0:T(8,128)(2,1)S(1)}, bf16[512,128]{1,0:T(8,128)(2,1)S(1)}, u32[]{:S(2)}, u32[]{:S(2)}) %collective-permute-start.11) | collective-permute-done | bytes 131104 | tf_op jit(solution)/shard_map/ppermute | solution.py:340
  28.2 1.6 %collective-permute-start.12 = (bf16[1,512,128]{2,1,0:T(8,128)(2,1)S(1)}, bf16[1,512,128]{2,1,0:T(8,128)(2,1)S(1)}, u32[]{:S(2)}, u32[]{:S(2)}) collective-permute-start(bf16[1,512,128]{2,1,0:T(8,128)(2,1)S(1)} %bitcast.14), channel_id=1, source_target_pairs={{0,8},{1,9},{2,10},{3,11},{4,12},{5,13},{6,14},{7,15},{8,0},{9,1},... | collective-permute-start | bytes 393224 | tf_op jit(solution)/shard_map/ppermute | solution.py:340
  29.8 0.6 collective-permute-start.13
  30.5 1.3 %collective-permute-start.14 = (bf16[1,512,128]{2,1,0:T(8,128)(2,1)S(1)}, bf16[1,512,128]{2,1,0:T(8,128)(2,1)S(1)}, u32[]{:S(2)}, u32[]{:S(2)}) collective-permute-start(bf16[1,512,128]{2,1,0:T(8,128)(2,1)S(1)} %bitcast.16), channel_id=1, source_target_pairs={{0,24},{1,25},{2,26},{3,27},{4,28},{5,29},{6,30},{7,31},{8,16},{9,... | collective-permute-start | bytes 393224 | tf_op jit(solution)/shard_map/ppermute | solution.py:340
  31.8 2.2 %copy-done = bf16[2048,1024]{1,0:T(8,128)(2,1)S(1)} copy-done((bf16[2048,1024]{1,0:T(8,128)(2,1)S(1)}, bf16[2048,1024]{1,0:T(8,128)(2,1)}, u32[]{:S(2)}) %copy-start) | copy-done | bytes 4194328
  34.0 0.3 load.1.refs_4_.refs_3_.refs_1_
  34.3 1.8 %piece_product.3.refs_3_ = f32[2048,128]{1,0:T(8,128)S(1)} custom-call(bf16[1,512,128]{2,1,0:T(8,128)(2,1)S(1)} %bitcast.21, bf16[1,512,128]{2,1,0:T(8,128)(2,1)S(1)} %collective-permute-done.17.refs_1_, bf16[1,512,128]{2,1,0:T(8,128)(2,1)S(1)} %collective-permute-done.18.refs_2_, bf16[2048,1024]{1,0:T(8,128)(2,1)S(1)} %load.1.refs_4_.refs_3_.refs_1_, ...), custom_call_target="tpu_custom_call" | custom-call | flops 805306368 | bytes 6291456 | tf_op jit(solution)/shard_map/piece_product/pallas_call | solution.py:193
  36.1 0.5 piece_product.5.x
  36.6 9.5 %collective-permute-start.24 = (bf16[1024,128]{1,0:T(8,128)(2,1)S(1)}, bf16[1024,128]{1,0:T(8,128)(2,1)S(1)}, u32[]{:S(2)}, u32[]{:S(2)}) collective-permute-start(bf16[1024,128]{1,0:T(8,128)(2,1)S(1)} %piece_product.5.x), channel_id=1, source_target_pairs={{0,2},{1,3},{2,0},{3,1},{4,6},{5,7},{6,4},{7,5},{8,10},{9,11},{10,... | collective-permute-start | bytes 786440 | tf_op jit(solution)/shard_map/ppermute | solution.py:340
  46.1 0.5 piece_product.4.x
  46.6 0.1 collective-permute-start.19
  46.7 2.0 %collective-permute-start.7 = (bf16[512,128]{1,0:T(8,128)(2,1)S(1)}, bf16[512,128]{1,0:T(8,128)(2,1)S(1)}, u32[]{:S(2)}, u32[]{:S(2)}) collective-permute-start(bf16[512,128]{1,0:T(8,128)(2,1)S(1)} %get-tuple-element.26), channel_id=1, source_target_pairs={{0,2},{1,3},{2,0},{3,1},{4,6},{5,7},{6,4},{7,5},{8,10},{9,11},{10,... | collective-permute-start | bytes 393224 | tf_op jit(solution)/shard_map/ppermute | solution.py:340
  48.7 2.4 %partial_product.5 = (bf16[1024,128]{1,0:T(8,128)(2,1)S(1)}, bf16[1024,128]{1,0:T(8,128)(2,1)S(1)}) custom-call(bf16[1,512,128]{2,1,0:T(8,128)(2,1)S(1)} %bitcast.17, bf16[1,512,128]{2,1,0:T(8,128)(2,1)S(1)} %collective-permute-done.12.refs_1_, bf16[1,512,128]{2,1,0:T(8,128)(2,1)S(1)} %collective-permute-done.13.refs_2_, ...), custom_call_target="tpu_custom_call" | custom-call | flops 1073741824 | bytes 8388608 | tf_op jit(solution)/shard_map/partial_product/pallas_call | solution.py:152
  51.1 0.2 collective-permute-start.27
  51.3 8.2 %collective-permute-done.7 = bf16[512,128]{1,0:T(8,128)(2,1)S(1)} collective-permute-done((bf16[512,128]{1,0:T(8,128)(2,1)S(1)}, bf16[512,128]{1,0:T(8,128)(2,1)S(1)}, u32[]{:S(2)}, u32[]{:S(2)}) %collective-permute-start.7) | collective-permute-done | bytes 131104 | tf_op jit(solution)/shard_map/ppermute | solution.py:340
  59.4 1.6 %collective-permute-start.10 = (bf16[1,512,128]{2,1,0:T(8,128)(2,1)S(1)}, bf16[1,512,128]{2,1,0:T(8,128)(2,1)S(1)}, u32[]{:S(2)}, u32[]{:S(2)}) collective-permute-start(bf16[1,512,128]{2,1,0:T(8,128)(2,1)S(1)} %bitcast.10), channel_id=1, source_target_pairs={{0,24},{1,25},{2,26},{3,27},{4,28},{5,29},{6,30},{7,31},{8,16},{9,... | collective-permute-start | bytes 393224 | tf_op jit(solution)/shard_map/ppermute | solution.py:340
  61.0 1.5 %collective-permute-start.8 = (bf16[1,512,128]{2,1,0:T(8,128)(2,1)S(1)}, bf16[1,512,128]{2,1,0:T(8,128)(2,1)S(1)}, u32[]{:S(2)}, u32[]{:S(2)}) collective-permute-start(bf16[1,512,128]{2,1,0:T(8,128)(2,1)S(1)} %bitcast.11), channel_id=1, source_target_pairs={{0,8},{1,9},{2,10},{3,11},{4,12},{5,13},{6,14},{7,15},{8,0},{9,1},... | collective-permute-start | bytes 393224 | tf_op jit(solution)/shard_map/ppermute | solution.py:340
  62.5 0.4 collective-permute-start.9
  62.9 1.0 collective-permute-start.22
  63.9 0.1 add.29
  64.0 0.1 add.26
  64.1 1.2 %collective-permute-done.10.refs_3_ = bf16[1,512,128]{2,1,0:T(8,128)(2,1)S(1)} collective-permute-done((bf16[1,512,128]{2,1,0:T(8,128)(2,1)S(1)}, bf16[1,512,128]{2,1,0:T(8,128)(2,1)S(1)}, u32[]{:S(2)}, u32[]{:S(2)}) %collective-permute-start.10) | collective-permute-done | bytes 131104 | tf_op jit(solution)/shard_map/ppermute | solution.py:340
  65.3 1.5 %collective-permute-done.8.refs_1_ = bf16[1,512,128]{2,1,0:T(8,128)(2,1)S(1)} collective-permute-done((bf16[1,512,128]{2,1,0:T(8,128)(2,1)S(1)}, bf16[1,512,128]{2,1,0:T(8,128)(2,1)S(1)}, u32[]{:S(2)}, u32[]{:S(2)}) %collective-permute-start.8) | collective-permute-done | bytes 131104 | tf_op jit(solution)/shard_map/ppermute | solution.py:340
  66.8 0.6 collective-permute-done.9.refs_2_
  67.4 2.3 %collective-permute-start.29 = (bf16[1024,128]{1,0:T(8,128)(2,1)S(1)}, bf16[1024,128]{1,0:T(8,128)(2,1)S(1)}, u32[]{:S(2)}, u32[]{:S(2)}) collective-permute-start(bf16[1024,128]{1,0:T(8,128)(2,1)S(1)} %get-tuple-element.34.refs_2_), channel_id=1, source_target_pairs={{0,2},{1,3},{2,0},{3,1},{4,6},{5,7},{6,4},{7,5},{8,10},{9,11},{10,... | collective-permute-start | bytes 786440 | tf_op jit(solution)/shard_map/ppermute | solution.py:340
  69.7 0.1 collective-permute-start.30
  69.8 1.4 %collective-permute-start.3 = (bf16[1,512,128]{2,1,0:T(8,128)(2,1)S(1)}, bf16[1,512,128]{2,1,0:T(8,128)(2,1)S(1)}, u32[]{:S(2)}, u32[]{:S(2)}) collective-permute-start(bf16[1,512,128]{2,1,0:T(8,128)(2,1)S(1)} %bitcast.6), channel_id=1, source_target_pairs={{0,8},{1,9},{2,10},{3,11},{4,12},{5,13},{6,14},{7,15},{8,0},{9,1},... | collective-permute-start | bytes 393224 | tf_op jit(solution)/shard_map/ppermute | solution.py:340
  71.2 0.6 collective-permute-start.4
  71.8 1.5 %collective-permute-start.5 = (bf16[1,512,128]{2,1,0:T(8,128)(2,1)S(1)}, bf16[1,512,128]{2,1,0:T(8,128)(2,1)S(1)}, u32[]{:S(2)}, u32[]{:S(2)}) collective-permute-start(bf16[1,512,128]{2,1,0:T(8,128)(2,1)S(1)} %bitcast.8), channel_id=1, source_target_pairs={{0,24},{1,25},{2,26},{3,27},{4,28},{5,29},{6,30},{7,31},{8,16},{9,... | collective-permute-start | bytes 393224 | tf_op jit(solution)/shard_map/ppermute | solution.py:340
  73.3 2.4 %partial_product.4 = (bf16[1024,128]{1,0:T(8,128)(2,1)S(1)}, bf16[1024,128]{1,0:T(8,128)(2,1)S(1)}) custom-call(bf16[1,512,128]{2,1,0:T(8,128)(2,1)S(1)} %bitcast.13, bf16[1,512,128]{2,1,0:T(8,128)(2,1)S(1)} %collective-permute-done.8.refs_1_, bf16[1,512,128]{2,1,0:T(8,128)(2,1)S(1)} %collective-permute-done.9.refs_2_, ...), custom_call_target="tpu_custom_call" | custom-call | flops 1073741824 | bytes 8388608 | tf_op jit(solution)/shard_map/partial_product/pallas_call | solution.py:152
  75.7 0.1 add.31.refs_0_
  75.7 0.1 add.28.refs_1_
  75.8 0.4 ahead.5
  76.2 0.1 add.30.refs_0_
  76.3 0.1 add.27.refs_1_
  76.4 0.5 collective-permute-done.29.refs_2_
  76.9 4.3 %collective-permute-done.30.refs_3_ = bf16[1024,128]{1,0:T(8,128)(2,1)S(1)} collective-permute-done((bf16[1024,128]{1,0:T(8,128)(2,1)S(1)}, bf16[1024,128]{1,0:T(8,128)(2,1)S(1)}, u32[]{:S(2)}, u32[]{:S(2)}) %collective-permute-start.30) | collective-permute-done | bytes 262176 | tf_op jit(solution)/shard_map/ppermute | solution.py:340
  81.2 0.4 ahead.4
  81.5 1.1 %collective-permute-start.31 = (bf16[128,128]{1,0:T(8,128)(2,1)S(1)}, bf16[128,128]{1,0:T(8,128)(2,1)S(1)}, u32[]{:S(2)}, u32[]{:S(2)}) collective-permute-start(bf16[128,128]{1,0:T(8,128)(2,1)S(1)} %ahead.4), channel_id=1, source_target_pairs={{0,2},{1,3},{2,0},{3,1},{4,6},{5,7},{6,4},{7,5},{8,10},{9,11},{10,... | collective-permute-start | bytes 98312 | tf_op jit(solution)/shard_map/ppermute | solution.py:340
  82.7 2.4 %partial_product.3 = (bf16[1024,128]{1,0:T(8,128)(2,1)S(1)}, bf16[1024,128]{1,0:T(8,128)(2,1)S(1)}) custom-call(bf16[1,512,128]{2,1,0:T(8,128)(2,1)S(1)} %bitcast.9, bf16[1,512,128]{2,1,0:T(8,128)(2,1)S(1)} %collective-permute-done.3.refs_1_, bf16[1,512,128]{2,1,0:T(8,128)(2,1)S(1)} %collective-permute-done.4.refs_2_, ...), custom_call_target="tpu_custom_call" | custom-call | flops 1073741824 | bytes 8388608 | tf_op jit(solution)/shard_map/partial_product/pallas_call | solution.py:152
  85.1 0.4 ahead.3.diag
  85.5 0.1 collective-permute-done.31.refs_0_
  85.5 1.5 %collective-permute-start.35 = (bf16[128,128]{1,0:T(8,128)(2,1)S(1)}, bf16[128,128]{1,0:T(8,128)(2,1)S(1)}, u32[]{:S(2)}, u32[]{:S(2)}) collective-permute-start(bf16[128,128]{1,0:T(8,128)(2,1)S(1)} %get-tuple-element.37), channel_id=1, source_target_pairs={{0,8},{1,9},{2,10},{3,11},{4,12},{5,13},{6,14},{7,15},{8,0},{9,1},... | collective-permute-start | bytes 98312 | tf_op jit(solution)/shard_map/ppermute | solution.py:340
  87.0 0.6 collective-permute-start.36
  87.6 1.5 %collective-permute-start.37 = (bf16[128,128]{1,0:T(8,128)(2,1)S(1)}, bf16[128,128]{1,0:T(8,128)(2,1)S(1)}, u32[]{:S(2)}, u32[]{:S(2)}) collective-permute-start(bf16[128,128]{1,0:T(8,128)(2,1)S(1)} %get-tuple-element.37), channel_id=1, source_target_pairs={{0,24},{1,25},{2,26},{3,27},{4,28},{5,29},{6,30},{7,31},{8,16},{9,... | collective-permute-start | bytes 98312 | tf_op jit(solution)/shard_map/ppermute | solution.py:340
  89.1 3.3 %collective-permute-start.26 = (bf16[1024,128]{1,0:T(8,128)(2,1)S(1)}, bf16[1024,128]{1,0:T(8,128)(2,1)S(1)}, u32[]{:S(2)}, u32[]{:S(2)}) collective-permute-start(bf16[1024,128]{1,0:T(8,128)(2,1)S(1)} %add.30.refs_0_), channel_id=1, source_target_pairs={{0,2},{1,3},{2,0},{3,1},{4,6},{5,7},{6,4},{7,5},{8,10},{9,11},{10,... | collective-permute-start | bytes 786440 | tf_op jit(solution)/shard_map/ppermute | solution.py:340
  92.4 1.1 %collective-permute-start.21 = (bf16[1024,128]{1,0:T(8,128)(2,1)S(1)}, bf16[1024,128]{1,0:T(8,128)(2,1)S(1)}, u32[]{:S(2)}, u32[]{:S(2)}) collective-permute-start(bf16[1024,128]{1,0:T(8,128)(2,1)S(1)} %add.27.refs_1_), channel_id=1, source_target_pairs={{0,2},{1,3},{2,0},{3,1},{4,6},{5,7},{6,4},{7,5},{8,10},{9,11},{10,... | collective-permute-start | bytes 786440 | tf_op jit(solution)/shard_map/ppermute | solution.py:340
  93.5 0.7 bitcast_add_fusion
  94.2 5.4 %collective-permute-done.26.refs_1_ = bf16[1024,128]{1,0:T(8,128)(2,1)S(1)} collective-permute-done((bf16[1024,128]{1,0:T(8,128)(2,1)S(1)}, bf16[1024,128]{1,0:T(8,128)(2,1)S(1)}, u32[]{:S(2)}, u32[]{:S(2)}) %collective-permute-start.26) | collective-permute-done | bytes 262176 | tf_op jit(solution)/shard_map/ppermute | solution.py:340
  99.5 1.6 %masked.2.refs_3_ = f32[128,2048]{1,0:T(8,128)} custom-call(s32[8,64]{1,0:T(8,128)S(1)} %copy-done.1, bf16[1024,128]{1,0:T(8,128)(2,1)S(1)} %get-tuple-element.31.refs_0_, bf16[1024,128]{1,0:T(8,128)(2,1)S(1)} %collective-permute-done.26.refs_1_, bf16[1024,128]{1,0:T(8,128)(2,1)S(1)} %collective-permute-done.28.refs_2_), custom_call_target="tpu_custom_call" | custom-call | flops 524288 | bytes 1310720 | tf_op jit(solution)/shard_map/masked/pallas_call | solution.py:310
  101.2 2.3 %collective-permute-done.21.refs_1_ = bf16[1024,128]{1,0:T(8,128)(2,1)S(1)} collective-permute-done((bf16[1024,128]{1,0:T(8,128)(2,1)S(1)}, bf16[1024,128]{1,0:T(8,128)(2,1)S(1)}, u32[]{:S(2)}, u32[]{:S(2)}) %collective-permute-start.21) | collective-permute-done | bytes 262176 | tf_op jit(solution)/shard_map/ppermute | solution.py:340
  103.4 1.6 %masked.3 = f32[128,2048]{1,0:T(8,128)} custom-call(s32[8,64]{1,0:T(8,128)S(1)} %copy-done.1, bf16[1024,128]{1,0:T(8,128)(2,1)S(1)} %get-tuple-element.25.refs_0_.refs_1_, bf16[1024,128]{1,0:T(8,128)(2,1)S(1)} %collective-permute-done.21.refs_1_, bf16[1024,128]{1,0:T(8,128)(2,1)S(1)} %collective-permute-done.23.refs_2_, ...), custom_call_target="tpu_custom_call", output_to_operand_aliasing={{}: (4, {})} | custom-call | flops 524288 | bytes 1310720 | tf_op jit(solution)/shard_map/masked/pallas_call | solution.py:310
  (40 shorter events, 0.2 us)
Async XLA Ops:
  0.6 31.2 %collective-permute-start.6 = (bf16[2048,1024]{1,0:T(8,128)(2,1)}, bf16[2048,1024]{1,0:T(8,128)(2,1)S(1)}, u32[]{:S(2)}, u32[]{:S(2)}) collective-permute-start(bf16[2048,1024]{1,0:T(8,128)(2,1)} %tile.1), channel_id=1, source_target_pairs={{0,1},{1,0},{2,3},{3,2},{4,5},{5,4},{6,7},{7,6},{8,9},{9,8},{10,11... | collective-permute-start | bytes 12582920 | tf_op jit(solution)/shard_map/ppermute | solution.py:340
  3.1 6.9 %collective-permute-start = (bf16[512,128]{1,0:T(8,128)(2,1)S(1)}, bf16[512,128]{1,0:T(8,128)(2,1)S(1)}, u32[]{:S(2)}, u32[]{:S(2)}) collective-permute-start(bf16[512,128]{1,0:T(8,128)(2,1)S(1)} %get-tuple-element.21), channel_id=1, source_target_pairs={{0,8},{1,9},{2,10},{3,11},{4,12},{5,13},{6,14},{7,15},{8,0},{9,1},... | collective-permute-start | bytes 393224 | tf_op jit(solution)/shard_map/ppermute | solution.py:340
  5.6 8.4 %collective-permute-start.1 = (bf16[512,128]{1,0:T(8,128)(2,1)S(1)}, bf16[512,128]{1,0:T(8,128)(2,1)S(1)}, u32[]{:S(2)}, u32[]{:S(2)}) collective-permute-start(bf16[512,128]{1,0:T(8,128)(2,1)S(1)} %get-tuple-element.22), channel_id=1, source_target_pairs={{0,16},{1,17},{2,18},{3,19},{4,20},{5,21},{6,22},{7,23},{8,24},{9,... | collective-permute-start | bytes 393224 | tf_op jit(solution)/shard_map/ppermute | solution.py:340
  7.1 6.9 %collective-permute-start.2 = (bf16[512,128]{1,0:T(8,128)(2,1)S(1)}, bf16[512,128]{1,0:T(8,128)(2,1)S(1)}, u32[]{:S(2)}, u32[]{:S(2)}) collective-permute-start(bf16[512,128]{1,0:T(8,128)(2,1)S(1)} %get-tuple-element.23), channel_id=1, source_target_pairs={{0,24},{1,25},{2,26},{3,27},{4,28},{5,29},{6,30},{7,31},{8,16},{9,... | collective-permute-start | bytes 393224 | tf_op jit(solution)/shard_map/ppermute | solution.py:340
  14.1 8.1 %collective-permute-start.15 = (bf16[512,128]{1,0:T(8,128)(2,1)S(1)}, bf16[512,128]{1,0:T(8,128)(2,1)S(1)}, u32[]{:S(2)}, u32[]{:S(2)}) collective-permute-start(bf16[512,128]{1,0:T(8,128)(2,1)S(1)} %get-tuple-element.30), channel_id=1, source_target_pairs={{0,6},{1,7},{2,4},{3,5},{4,2},{5,3},{6,0},{7,1},{8,14},{9,15},{10,... | collective-permute-start | bytes 393224 | tf_op jit(solution)/shard_map/ppermute | solution.py:340
  17.7 10.5 %collective-permute-start.11 = (bf16[512,128]{1,0:T(8,128)(2,1)S(1)}, bf16[512,128]{1,0:T(8,128)(2,1)S(1)}, u32[]{:S(2)}, u32[]{:S(2)}) collective-permute-start(bf16[512,128]{1,0:T(8,128)(2,1)S(1)} %get-tuple-element.28), channel_id=1, source_target_pairs={{0,4},{1,5},{2,6},{3,7},{4,0},{5,1},{6,2},{7,3},{8,12},{9,13},{10,... | collective-permute-start | bytes 393224 | tf_op jit(solution)/shard_map/ppermute | solution.py:340
  22.2 7.7 %collective-permute-start.17 = (bf16[1,512,128]{2,1,0:T(8,128)(2,1)S(1)}, bf16[1,512,128]{2,1,0:T(8,128)(2,1)S(1)}, u32[]{:S(2)}, u32[]{:S(2)}) collective-permute-start(bf16[1,512,128]{2,1,0:T(8,128)(2,1)S(1)} %bitcast.18), channel_id=1, source_target_pairs={{0,8},{1,9},{2,10},{3,11},{4,12},{5,13},{6,14},{7,15},{8,0},{9,1},... | collective-permute-start | bytes 393224 | tf_op jit(solution)/shard_map/ppermute | solution.py:340
  23.6 6.3 %collective-permute-start.18 = (bf16[1,512,128]{2,1,0:T(8,128)(2,1)S(1)}, bf16[1,512,128]{2,1,0:T(8,128)(2,1)S(1)}, u32[]{:S(2)}, u32[]{:S(2)}) collective-permute-start(bf16[1,512,128]{2,1,0:T(8,128)(2,1)S(1)} %bitcast.19), channel_id=1, source_target_pairs={{0,16},{1,17},{2,18},{3,19},{4,20},{5,21},{6,22},{7,23},{8,24},{9,... | collective-permute-start | bytes 393224 | tf_op jit(solution)/shard_map/ppermute | solution.py:340
  24.4 6.1 %collective-permute-start.16 = (bf16[1,512,128]{2,1,0:T(8,128)(2,1)S(1)}, bf16[1,512,128]{2,1,0:T(8,128)(2,1)S(1)}, u32[]{:S(2)}, u32[]{:S(2)}) collective-permute-start(bf16[1,512,128]{2,1,0:T(8,128)(2,1)S(1)} %bitcast.20), channel_id=1, source_target_pairs={{0,24},{1,25},{2,26},{3,27},{4,28},{5,29},{6,30},{7,31},{8,16},{9,... | collective-permute-start | bytes 393224 | tf_op jit(solution)/shard_map/ppermute | solution.py:340
  28.2 8.4 %collective-permute-start.12 = (bf16[1,512,128]{2,1,0:T(8,128)(2,1)S(1)}, bf16[1,512,128]{2,1,0:T(8,128)(2,1)S(1)}, u32[]{:S(2)}, u32[]{:S(2)}) collective-permute-start(bf16[1,512,128]{2,1,0:T(8,128)(2,1)S(1)} %bitcast.14), channel_id=1, source_target_pairs={{0,8},{1,9},{2,10},{3,11},{4,12},{5,13},{6,14},{7,15},{8,0},{9,1},... | collective-permute-start | bytes 393224 | tf_op jit(solution)/shard_map/ppermute | solution.py:340
  29.8 21.3 %collective-permute-start.32 = (bf16[1024,128]{1,0:T(8,128)(2,1)S(1)}, bf16[1024,128]{1,0:T(8,128)(2,1)S(1)}, u32[]{:S(2)}, u32[]{:S(2)}) collective-permute-start(bf16[1024,128]{1,0:T(8,128)(2,1)S(1)} %get-tuple-element.34.refs_2_), channel_id=1, source_target_pairs={{0,1},{1,0},{2,4},{3,5},{4,2},{5,3},{6,7},{7,6},{8,9},{9,8},{10,12... | collective-permute-start | bytes 786440 | tf_op jit(solution)/shard_map/ppermute | solution.py:340
  29.8 16.8 %collective-permute-start.13 = (bf16[1,512,128]{2,1,0:T(8,128)(2,1)S(1)}, bf16[1,512,128]{2,1,0:T(8,128)(2,1)S(1)}, u32[]{:S(2)}, u32[]{:S(2)}) collective-permute-start(bf16[1,512,128]{2,1,0:T(8,128)(2,1)S(1)} %bitcast.15), channel_id=1, source_target_pairs={{0,16},{1,17},{2,18},{3,19},{4,20},{5,21},{6,22},{7,23},{8,24},{9,... | collective-permute-start | bytes 393224 | tf_op jit(solution)/shard_map/ppermute | solution.py:340
  30.5 16.2 %collective-permute-start.14 = (bf16[1,512,128]{2,1,0:T(8,128)(2,1)S(1)}, bf16[1,512,128]{2,1,0:T(8,128)(2,1)S(1)}, u32[]{:S(2)}, u32[]{:S(2)}) collective-permute-start(bf16[1,512,128]{2,1,0:T(8,128)(2,1)S(1)} %bitcast.16), channel_id=1, source_target_pairs={{0,24},{1,25},{2,26},{3,27},{4,28},{5,29},{6,30},{7,31},{8,16},{9,... | collective-permute-start | bytes 393224 | tf_op jit(solution)/shard_map/ppermute | solution.py:340
  31.8 29.2 %collective-permute-start.33 = (bf16[1024,128]{1,0:T(8,128)(2,1)S(1)}, bf16[1024,128]{1,0:T(8,128)(2,1)S(1)}, u32[]{:S(2)}, u32[]{:S(2)}) collective-permute-start(bf16[1024,128]{1,0:T(8,128)(2,1)S(1)} %get-tuple-element.35.refs_3_), channel_id=1, source_target_pairs={{0,1},{1,0},{2,4},{3,5},{4,2},{5,3},{6,7},{7,6},{8,9},{9,8},{10,12... | collective-permute-start | bytes 786440 | tf_op jit(solution)/shard_map/ppermute | solution.py:340
  31.8 2.2 %copy-start = (bf16[2048,1024]{1,0:T(8,128)(2,1)S(1)}, bf16[2048,1024]{1,0:T(8,128)(2,1)}, u32[]{:S(2)}) copy-start(bf16[2048,1024]{1,0:T(8,128)(2,1)} %tile.1) | copy-start | bytes 12582916
  36.6 25.9 %collective-permute-start.24 = (bf16[1024,128]{1,0:T(8,128)(2,1)S(1)}, bf16[1024,128]{1,0:T(8,128)(2,1)S(1)}, u32[]{:S(2)}, u32[]{:S(2)}) collective-permute-start(bf16[1024,128]{1,0:T(8,128)(2,1)S(1)} %piece_product.5.x), channel_id=1, source_target_pairs={{0,2},{1,3},{2,0},{3,1},{4,6},{5,7},{6,4},{7,5},{8,10},{9,11},{10,... | collective-permute-start | bytes 786440 | tf_op jit(solution)/shard_map/ppermute | solution.py:340
  46.6 16.3 %collective-permute-start.19 = (bf16[1024,128]{1,0:T(8,128)(2,1)S(1)}, bf16[1024,128]{1,0:T(8,128)(2,1)S(1)}, u32[]{:S(2)}, u32[]{:S(2)}) collective-permute-start(bf16[1024,128]{1,0:T(8,128)(2,1)S(1)} %piece_product.4.x), channel_id=1, source_target_pairs={{0,2},{1,3},{2,0},{3,1},{4,6},{5,7},{6,4},{7,5},{8,10},{9,11},{10,... | collective-permute-start | bytes 786440 | tf_op jit(solution)/shard_map/ppermute | solution.py:340
  46.7 12.7 %collective-permute-start.7 = (bf16[512,128]{1,0:T(8,128)(2,1)S(1)}, bf16[512,128]{1,0:T(8,128)(2,1)S(1)}, u32[]{:S(2)}, u32[]{:S(2)}) collective-permute-start(bf16[512,128]{1,0:T(8,128)(2,1)S(1)} %get-tuple-element.26), channel_id=1, source_target_pairs={{0,2},{1,3},{2,0},{3,1},{4,6},{5,7},{6,4},{7,5},{8,10},{9,11},{10,... | collective-permute-start | bytes 393224 | tf_op jit(solution)/shard_map/ppermute | solution.py:340
  51.1 18.6 %collective-permute-start.27 = (bf16[1024,128]{1,0:T(8,128)(2,1)S(1)}, bf16[1024,128]{1,0:T(8,128)(2,1)S(1)}, u32[]{:S(2)}, u32[]{:S(2)}) collective-permute-start(bf16[1024,128]{1,0:T(8,128)(2,1)S(1)} %get-tuple-element.33.x), channel_id=1, source_target_pairs={{0,2},{1,3},{2,0},{3,1},{4,6},{5,7},{6,4},{7,5},{8,10},{9,11},{10,... | collective-permute-start | bytes 786440 | tf_op jit(solution)/shard_map/ppermute | solution.py:340
  59.4 5.9 %collective-permute-start.10 = (bf16[1,512,128]{2,1,0:T(8,128)(2,1)S(1)}, bf16[1,512,128]{2,1,0:T(8,128)(2,1)S(1)}, u32[]{:S(2)}, u32[]{:S(2)}) collective-permute-start(bf16[1,512,128]{2,1,0:T(8,128)(2,1)S(1)} %bitcast.10), channel_id=1, source_target_pairs={{0,24},{1,25},{2,26},{3,27},{4,28},{5,29},{6,30},{7,31},{8,16},{9,... | collective-permute-start | bytes 393224 | tf_op jit(solution)/shard_map/ppermute | solution.py:340
  61.0 5.8 %collective-permute-start.8 = (bf16[1,512,128]{2,1,0:T(8,128)(2,1)S(1)}, bf16[1,512,128]{2,1,0:T(8,128)(2,1)S(1)}, u32[]{:S(2)}, u32[]{:S(2)}) collective-permute-start(bf16[1,512,128]{2,1,0:T(8,128)(2,1)S(1)} %bitcast.11), channel_id=1, source_target_pairs={{0,8},{1,9},{2,10},{3,11},{4,12},{5,13},{6,14},{7,15},{8,0},{9,1},... | collective-permute-start | bytes 393224 | tf_op jit(solution)/shard_map/ppermute | solution.py:340
  62.5 5.0 %collective-permute-start.9 = (bf16[1,512,128]{2,1,0:T(8,128)(2,1)S(1)}, bf16[1,512,128]{2,1,0:T(8,128)(2,1)S(1)}, u32[]{:S(2)}, u32[]{:S(2)}) collective-permute-start(bf16[1,512,128]{2,1,0:T(8,128)(2,1)S(1)} %bitcast.12), channel_id=1, source_target_pairs={{0,16},{1,17},{2,18},{3,19},{4,20},{5,21},{6,22},{7,23},{8,24},{9,... | collective-permute-start | bytes 393224 | tf_op jit(solution)/shard_map/ppermute | solution.py:340
  62.9 6.9 %collective-permute-start.22 = (bf16[1024,128]{1,0:T(8,128)(2,1)S(1)}, bf16[1024,128]{1,0:T(8,128)(2,1)S(1)}, u32[]{:S(2)}, u32[]{:S(2)}) collective-permute-start(bf16[1024,128]{1,0:T(8,128)(2,1)S(1)} %get-tuple-element.29.x), channel_id=1, source_target_pairs={{0,2},{1,3},{2,0},{3,1},{4,6},{5,7},{6,4},{7,5},{8,10},{9,11},{10,... | collective-permute-start | bytes 786440 | tf_op jit(solution)/shard_map/ppermute | solution.py:340
  65.3 5.9 %collective-permute-start.25 = (bf16[1024,128]{1,0:T(8,128)(2,1)S(1)}, bf16[1024,128]{1,0:T(8,128)(2,1)S(1)}, u32[]{:S(2)}, u32[]{:S(2)}) collective-permute-start(bf16[1024,128]{1,0:T(8,128)(2,1)S(1)} %add.29), channel_id=1, source_target_pairs={{0,1},{1,0},{2,4},{3,5},{4,2},{5,3},{6,7},{7,6},{8,9},{9,8},{10,12... | collective-permute-start | bytes 786440 | tf_op jit(solution)/shard_map/ppermute | solution.py:340
  66.8 5.0 %collective-permute-start.20 = (bf16[1024,128]{1,0:T(8,128)(2,1)S(1)}, bf16[1024,128]{1,0:T(8,128)(2,1)S(1)}, u32[]{:S(2)}, u32[]{:S(2)}) collective-permute-start(bf16[1024,128]{1,0:T(8,128)(2,1)S(1)} %add.26), channel_id=1, source_target_pairs={{0,1},{1,0},{2,4},{3,5},{4,2},{5,3},{6,7},{7,6},{8,9},{9,8},{10,12... | collective-permute-start | bytes 786440 | tf_op jit(solution)/shard_map/ppermute | solution.py:340
  67.4 9.4 %collective-permute-start.29 = (bf16[1024,128]{1,0:T(8,128)(2,1)S(1)}, bf16[1024,128]{1,0:T(8,128)(2,1)S(1)}, u32[]{:S(2)}, u32[]{:S(2)}) collective-permute-start(bf16[1024,128]{1,0:T(8,128)(2,1)S(1)} %get-tuple-element.34.refs_2_), channel_id=1, source_target_pairs={{0,2},{1,3},{2,0},{3,1},{4,6},{5,7},{6,4},{7,5},{8,10},{9,11},{10,... | collective-permute-start | bytes 786440 | tf_op jit(solution)/shard_map/ppermute | solution.py:340
  69.7 11.4 %collective-permute-start.30 = (bf16[1024,128]{1,0:T(8,128)(2,1)S(1)}, bf16[1024,128]{1,0:T(8,128)(2,1)S(1)}, u32[]{:S(2)}, u32[]{:S(2)}) collective-permute-start(bf16[1024,128]{1,0:T(8,128)(2,1)S(1)} %get-tuple-element.35.refs_3_), channel_id=1, source_target_pairs={{0,2},{1,3},{2,0},{3,1},{4,6},{5,7},{6,4},{7,5},{8,10},{9,11},{10,... | collective-permute-start | bytes 786440 | tf_op jit(solution)/shard_map/ppermute | solution.py:340
  69.8 12.9 %collective-permute-start.3 = (bf16[1,512,128]{2,1,0:T(8,128)(2,1)S(1)}, bf16[1,512,128]{2,1,0:T(8,128)(2,1)S(1)}, u32[]{:S(2)}, u32[]{:S(2)}) collective-permute-start(bf16[1,512,128]{2,1,0:T(8,128)(2,1)S(1)} %bitcast.6), channel_id=1, source_target_pairs={{0,8},{1,9},{2,10},{3,11},{4,12},{5,13},{6,14},{7,15},{8,0},{9,1},... | collective-permute-start | bytes 393224 | tf_op jit(solution)/shard_map/ppermute | solution.py:340
  71.2 11.5 %collective-permute-start.4 = (bf16[1,512,128]{2,1,0:T(8,128)(2,1)S(1)}, bf16[1,512,128]{2,1,0:T(8,128)(2,1)S(1)}, u32[]{:S(2)}, u32[]{:S(2)}) collective-permute-start(bf16[1,512,128]{2,1,0:T(8,128)(2,1)S(1)} %bitcast.7), channel_id=1, source_target_pairs={{0,16},{1,17},{2,18},{3,19},{4,20},{5,21},{6,22},{7,23},{8,24},{9,... | collective-permute-start | bytes 393224 | tf_op jit(solution)/shard_map/ppermute | solution.py:340
  71.8 10.9 %collective-permute-start.5 = (bf16[1,512,128]{2,1,0:T(8,128)(2,1)S(1)}, bf16[1,512,128]{2,1,0:T(8,128)(2,1)S(1)}, u32[]{:S(2)}, u32[]{:S(2)}) collective-permute-start(bf16[1,512,128]{2,1,0:T(8,128)(2,1)S(1)} %bitcast.8), channel_id=1, source_target_pairs={{0,24},{1,25},{2,26},{3,27},{4,28},{5,29},{6,30},{7,31},{8,16},{9,... | collective-permute-start | bytes 393224 | tf_op jit(solution)/shard_map/ppermute | solution.py:340
  76.9 8.6 %collective-permute-start.34 = (bf16[128,128]{1,0:T(8,128)(2,1)S(1)}, bf16[128,128]{1,0:T(8,128)(2,1)S(1)}, u32[]{:S(2)}, u32[]{:S(2)}) collective-permute-start(bf16[128,128]{1,0:T(8,128)(2,1)S(1)} %ahead.5), channel_id=1, source_target_pairs={{0,1},{1,0},{2,4},{3,5},{4,2},{5,3},{6,7},{7,6},{8,9},{9,8},{10,12... | collective-permute-start | bytes 98312 | tf_op jit(solution)/shard_map/ppermute | solution.py:340
  81.5 12.0 %copy-start.2 = (f32[1,128,128]{2,1,0:T(8,128)S(1)}, f32[1,128,128]{2,1,0:T(8,128)}, u32[]{:S(2)}) copy-start(f32[1,128,128]{2,1,0:T(8,128)} %param.8) | copy-start | bytes 196612
  81.5 18.0 %copy-start.1 = (s32[8,64]{1,0:T(8,128)S(1)}, s32[8,64]{1,0:T(8,128)}, u32[]{:S(2)}) copy-start(s32[8,64]{1,0:T(8,128)} %listed.5) | copy-start | bytes 6148
  81.5 4.0 %collective-permute-start.31 = (bf16[128,128]{1,0:T(8,128)(2,1)S(1)}, bf16[128,128]{1,0:T(8,128)(2,1)S(1)}, u32[]{:S(2)}, u32[]{:S(2)}) collective-permute-start(bf16[128,128]{1,0:T(8,128)(2,1)S(1)} %ahead.4), channel_id=1, source_target_pairs={{0,2},{1,3},{2,0},{3,1},{4,6},{5,7},{6,4},{7,5},{8,10},{9,11},{10,... | collective-permute-start | bytes 98312 | tf_op jit(solution)/shard_map/ppermute | solution.py:340
  85.5 6.8 %collective-permute-start.35 = (bf16[128,128]{1,0:T(8,128)(2,1)S(1)}, bf16[128,128]{1,0:T(8,128)(2,1)S(1)}, u32[]{:S(2)}, u32[]{:S(2)}) collective-permute-start(bf16[128,128]{1,0:T(8,128)(2,1)S(1)} %get-tuple-element.37), channel_id=1, source_target_pairs={{0,8},{1,9},{2,10},{3,11},{4,12},{5,13},{6,14},{7,15},{8,0},{9,1},... | collective-permute-start | bytes 98312 | tf_op jit(solution)/shard_map/ppermute | solution.py:340
  87.0 5.4 %collective-permute-start.36 = (bf16[128,128]{1,0:T(8,128)(2,1)S(1)}, bf16[128,128]{1,0:T(8,128)(2,1)S(1)}, u32[]{:S(2)}, u32[]{:S(2)}) collective-permute-start(bf16[128,128]{1,0:T(8,128)(2,1)S(1)} %get-tuple-element.37), channel_id=1, source_target_pairs={{0,16},{1,17},{2,18},{3,19},{4,20},{5,21},{6,22},{7,23},{8,24},{9,... | collective-permute-start | bytes 98312 | tf_op jit(solution)/shard_map/ppermute | solution.py:340
  87.6 5.9 %collective-permute-start.37 = (bf16[128,128]{1,0:T(8,128)(2,1)S(1)}, bf16[128,128]{1,0:T(8,128)(2,1)S(1)}, u32[]{:S(2)}, u32[]{:S(2)}) collective-permute-start(bf16[128,128]{1,0:T(8,128)(2,1)S(1)} %get-tuple-element.37), channel_id=1, source_target_pairs={{0,24},{1,25},{2,26},{3,27},{4,28},{5,29},{6,30},{7,31},{8,16},{9,... | collective-permute-start | bytes 98312 | tf_op jit(solution)/shard_map/ppermute | solution.py:340
  89.1 5.1 %collective-permute-start.28 = (bf16[1024,128]{1,0:T(8,128)(2,1)S(1)}, bf16[1024,128]{1,0:T(8,128)(2,1)S(1)}, u32[]{:S(2)}, u32[]{:S(2)}) collective-permute-start(bf16[1024,128]{1,0:T(8,128)(2,1)S(1)} %add.31.refs_0_), channel_id=1, source_target_pairs={{0,1},{1,0},{2,4},{3,5},{4,2},{5,3},{6,7},{7,6},{8,9},{9,8},{10,12... | collective-permute-start | bytes 786440 | tf_op jit(solution)/shard_map/ppermute | solution.py:340
  89.1 10.4 %collective-permute-start.26 = (bf16[1024,128]{1,0:T(8,128)(2,1)S(1)}, bf16[1024,128]{1,0:T(8,128)(2,1)S(1)}, u32[]{:S(2)}, u32[]{:S(2)}) collective-permute-start(bf16[1024,128]{1,0:T(8,128)(2,1)S(1)} %add.30.refs_0_), channel_id=1, source_target_pairs={{0,2},{1,3},{2,0},{3,1},{4,6},{5,7},{6,4},{7,5},{8,10},{9,11},{10,... | collective-permute-start | bytes 786440 | tf_op jit(solution)/shard_map/ppermute | solution.py:340
  92.4 8.8 %collective-permute-start.23 = (bf16[1024,128]{1,0:T(8,128)(2,1)S(1)}, bf16[1024,128]{1,0:T(8,128)(2,1)S(1)}, u32[]{:S(2)}, u32[]{:S(2)}) collective-permute-start(bf16[1024,128]{1,0:T(8,128)(2,1)S(1)} %add.28.refs_1_), channel_id=1, source_target_pairs={{0,1},{1,0},{2,4},{3,5},{4,2},{5,3},{6,7},{7,6},{8,9},{9,8},{10,12... | collective-permute-start | bytes 786440 | tf_op jit(solution)/shard_map/ppermute | solution.py:340
  92.4 11.0 %collective-permute-start.21 = (bf16[1024,128]{1,0:T(8,128)(2,1)S(1)}, bf16[1024,128]{1,0:T(8,128)(2,1)S(1)}, u32[]{:S(2)}, u32[]{:S(2)}) collective-permute-start(bf16[1024,128]{1,0:T(8,128)(2,1)S(1)} %add.27.refs_1_), channel_id=1, source_target_pairs={{0,2},{1,3},{2,0},{3,1},{4,6},{5,7},{6,4},{7,5},{8,10},{9,11},{10,... | collective-permute-start | bytes 786440 | tf_op jit(solution)/shard_map/ppermute | solution.py:340

commit v5 on v4

--- a/solution.py
+++ b/solution.py
@@ -231,7 +231,8 @@
 
 
 def ahead_kernel(*refs):
-    loads, rows, out = refs[:HALVES], refs[HALVES : 2 * HALVES], refs[-1]
+    count = len(refs) // 2
+    loads, rows, out = refs[:count], refs[count:-1], refs[-1]
     tall = loads[0].shape[0]
     step = min(tall, 512)
     total = None
@@ -249,11 +250,11 @@
     return pl.pallas_call(
         ahead_kernel,
         out_shape=jax.ShapeDtypeStruct((width, width), dtype),
-        in_specs=[whole(VMEM)] * (2 * HALVES),
+        in_specs=[whole(VMEM)] * (2 * len(loads)),
         out_specs=whole(VMEM),
         compiler_params=pltpu.CompilerParams(vmem_limit_bytes=LIMIT),
         cost_estimate=pl.CostEstimate(
-            flops=2 * HALVES * tall * width * width, bytes_accessed=4 * HALVES * tall * width, transcendentals=0
+            flops=2 * len(loads) * tall * width * width, bytes_accessed=4 * len(loads) * tall * width, transcendentals=0
         ),
         name="ahead",
     )(*loads, *rows)
@@ -264,26 +265,43 @@
     return [None if len(at) == n else among(z, at) for at in planes]
 
 
-def gathered_kernel(n, q, planes, diag, *refs):
-    early, total, sent = refs[:-2], refs[-2], refs[-1]
-    x = diag[...]
-    for y, take in zip(early, chosen_planes(n, q, planes)):
+def gathered_kernel(n, q, planes, own, lhat, *refs):
+    count = len(planes)
+    early, came, total, sent = refs[:count], refs[count : 2 * count], refs[-2], refs[-1]
+    takes = chosen_planes(n, q, planes)
+    sum_ = own[...]
+    for y, take in zip(early, takes):
         y = y[...].astype(jnp.float32)
-        x = x + (y if take is None else jnp.where(take, y, 0.0))
-    total[...] = x
-    sent[...] = x.astype(jnp.bfloat16)
-
-
-def gathered(n, q, planes, diag, early):
+        sum_ = sum_ + (y if take is None else jnp.where(take, y, 0.0))
+    tall = lhat.shape[0]
+    step = min(tall, 512)
+    for r in range(tall // step):
+        here = slice(r * step, (r + 1) * step)
+        x = None
+        for y, take in zip(came, takes):
+            y = y[here, :].astype(jnp.float32)
+            y = y if take is None else jnp.where(take, y, 0.0)
+            x = y if x is None else x + y
+        x = x.T
+        high = x.astype(jnp.bfloat16)
+        low = (x - high.astype(jnp.float32)).astype(jnp.bfloat16)
+        sum_ = sum_ + jnp.dot(high, lhat[here, :], preferred_element_type=jnp.float32)
+        sum_ = sum_ + jnp.dot(low, lhat[here, :], preferred_element_type=jnp.float32)
+    total[...] = sum_
+    sent[...] = sum_.astype(jnp.bfloat16)
+
+
+def gathered(n, q, planes, own, lhat, early, came):
+    tall, width = lhat.shape
     return pl.pallas_call(
         functools.partial(gathered_kernel, n, q, planes),
-        out_shape=[jax.ShapeDtypeStruct(diag.shape, jnp.float32), jax.ShapeDtypeStruct(diag.shape, jnp.bfloat16)],
-        in_specs=[whole(VMEM)] * (1 + len(early)),
+        out_shape=[jax.ShapeDtypeStruct(own.shape, jnp.float32), jax.ShapeDtypeStruct(own.shape, jnp.bfloat16)],
+        in_specs=[whole(VMEM)] * (2 + len(early) + len(came)),
         out_specs=[whole(VMEM)] * 2,
         compiler_params=pltpu.CompilerParams(vmem_limit_bytes=LIMIT),
-        cost_estimate=pl.CostEstimate(flops=4 * diag.size, bytes_accessed=16 * diag.size, transcendentals=0),
+        cost_estimate=pl.CostEstimate(flops=4 * tall * width * width, bytes_accessed=6 * tall * width, transcendentals=0),
         name="gathered",
-    )(diag, *early)
+    )(own, lhat, *early, *came)
 
 
 def masked_kernel(n, q, planes, rows, h, count, listed, *refs):
@@ -356,7 +374,7 @@
         return got, tuple(sorted(to))
 
     sides = [odd for odd in (0, 1) if line_pairs(n, 1, odd)]
-    theirs = {odd: [line_swap(lhat[h], odd, 1)[0] for h in range(HALVES)] for odd in sides}
+    theirs = {odd: line_swap(lhat[-1], odd, 1)[0] for odd in sides}
 
     scattered = [pieces[0]] + [over_rows(pieces[a], a) for a in range(1, n)]
     chosen = pick(n, q, scattered)
@@ -394,7 +412,7 @@
             x = jnp.where(here, chunk[m][h], x)
         return x
 
-    early, loads = [], ([], [])
+    early = []
     came = [[None, None] for _ in range(HALVES)]
     for d in range(n - 1, 0, -1):
         for h in range(HALVES):
@@ -404,16 +422,15 @@
                     continue
                 load_ = add(n, q, own(odd, d, h), came[h][1 - odd])
                 sent[odd] = line_swap(load_, odd, d)
-                loads[odd].append(load_)
                 if d == 1 and h == HALVES - 1:
-                    term = ahead(loads[odd][-HALVES:], theirs[odd], jnp.bfloat16)
+                    term = ahead([load_], [theirs[odd]], jnp.bfloat16)
                     early.append(line_swap(term, odd, d)[0])
             came[h] = sent
 
     parts = [[chunk[0][h]] + [x[0] for x in came[h] if x is not None] for h in range(HALVES)]
     planes = [x[1] for x in came[0] if x is not None]
     part = ahead(chunk[0], lhat, jnp.float32)
-    part, travel = gathered(n, q, planes, part, early)
+    part, travel = gathered(n, q, planes, part, lhat[0], early, parts[0][1:])
     off = []
     for h in range(HALVES):
         off = [masked(n, q, planes, inverse_tile.shape[0], h, listed, parts[h], off)]

time: 105 us -> 96.5 us (0.919)
  waiting for transfers between devices: 38 us -> 21.8 us
  starting transfers between devices: 46.5 us -> 53.7 us
    ppermute x38 -> x36, waiting for transfers between devices: 38 us -> 21.8 us  [swap(): return lax.ppermute(x, AXES, pairs)]
    ppermute x38 -> x36, starting transfers between devices: 46.5 us -> 53.7 us  [swap(): return lax.ppermute(x, AXES, pairs)]
  transfers between devices with their start and end apart: 38 -> 36, of which waited for: 13 -> 10; matrix products, arithmetic and copies ran while one was open for 1% -> 0% of each run, Pallas kernels for 14% -> 18%
where the time goes in v5:
time: 96.5 us; the launch traced here: 96.3 us
  starting transfers between devices  53.7 us (56%)
  waiting for transfers between devices  21.8 us (23%)
  Pallas kernels  17 us (18%)
  local copies, waits for them, and re-layouts  2.2 us (2%)
    ppermute x36, starting transfers between devices, swap(): return lax.ppermute(x, AXES, pairs)  53.7 us
    ppermute x36, waiting for transfers between devices, swap(): return lax.ppermute(x, AXES, pairs)  21.8 us
    pallas_call x3, Pallas kernels, partial_product(): pl.pallas_call(functools.partial(partial_kernel, n, q, halves, min(tall,...  7.1 us
    pallas_call x2, Pallas kernels, masked(): pl.pallas_call(functools.partial(masked_kernel, n, q, planes, rows, h, le...  3.23 us
    pallas_call x3, Pallas kernels, piece_product(): pl.pallas_call(functools.partial(piece_kernel, n, q, which, base, min(tal...  2.75 us
    unnamed x6, local copies, waits for them, and re-layouts  2.2 us
  transfers between devices with their start and end apart: 36, of which 10 were waited for; matrix products, arithmetic and copies ran while one was open for 0% of the time, Pallas kernels for 18%

profile of v5, /device:TPU:0, one launch (start us, length us, event | category | flops | bytes accessed | tf_op | source)
XLA Modules:
  0.0 96.3 jit_solution(8040161940060311333)
XLA Ops:
  0.6 0.6 collective-permute-start.6
  1.2 1.9 %normalize.1 = (bf16[512,128]{1,0:T(8,128)(2,1)S(1)}, bf16[512,128]{1,0:T(8,128)(2,1)S(1)}, bf16[512,128]{1,0:T(8,128)(2,1)S(1)}, bf16[512,128]{1,0:T(8,128)(2,1...) custom-call(s32[8,64]{1,0:T(8,128)} %listed.5, bf16[2048,128]{1,0:T(8,128)(2,1)} %panel.1, ...), custom_call_target="tpu_custom_call" | custom-call | flops 67108864 | bytes 1572864 | tf_op jit(solution)/shard_map/normalize/pallas_call | solution.py:62
  3.1 2.6 %collective-permute-start = (bf16[512,128]{1,0:T(8,128)(2,1)S(1)}, bf16[512,128]{1,0:T(8,128)(2,1)S(1)}, u32[]{:S(2)}, u32[]{:S(2)}) collective-permute-start(bf16[512,128]{1,0:T(8,128)(2,1)S(1)} %get-tuple-element.21), channel_id=1, source_target_pairs={{0,8},{1,9},{2,10},{3,11},{4,12},{5,13},{6,14},{7,15},{8,0},{9,1},... | collective-permute-start | bytes 393224 | tf_op jit(solution)/shard_map/ppermute | solution.py:358
  5.6 1.5 %collective-permute-start.1 = (bf16[512,128]{1,0:T(8,128)(2,1)S(1)}, bf16[512,128]{1,0:T(8,128)(2,1)S(1)}, u32[]{:S(2)}, u32[]{:S(2)}) collective-permute-start(bf16[512,128]{1,0:T(8,128)(2,1)S(1)} %get-tuple-element.22), channel_id=1, source_target_pairs={{0,16},{1,17},{2,18},{3,19},{4,20},{5,21},{6,22},{7,23},{8,24},{9,... | collective-permute-start | bytes 393224 | tf_op jit(solution)/shard_map/ppermute | solution.py:358
  7.2 2.8 %collective-permute-done.refs_1_ = bf16[512,128]{1,0:T(8,128)(2,1)S(1)} collective-permute-done((bf16[512,128]{1,0:T(8,128)(2,1)S(1)}, bf16[512,128]{1,0:T(8,128)(2,1)S(1)}, u32[]{:S(2)}, u32[]{:S(2)}) %collective-permute-start) | collective-permute-done | bytes 131104 | tf_op jit(solution)/shard_map/ppermute | solution.py:358
  9.9 4.1 %collective-permute-done.1.refs_2_ = bf16[512,128]{1,0:T(8,128)(2,1)S(1)} collective-permute-done((bf16[512,128]{1,0:T(8,128)(2,1)S(1)}, bf16[512,128]{1,0:T(8,128)(2,1)S(1)}, u32[]{:S(2)}, u32[]{:S(2)}) %collective-permute-start.1) | collective-permute-done | bytes 131104 | tf_op jit(solution)/shard_map/ppermute | solution.py:358
  14.1 3.7 %collective-permute-start.15 = (bf16[512,128]{1,0:T(8,128)(2,1)S(1)}, bf16[512,128]{1,0:T(8,128)(2,1)S(1)}, u32[]{:S(2)}, u32[]{:S(2)}) collective-permute-start(bf16[512,128]{1,0:T(8,128)(2,1)S(1)} %get-tuple-element.30), channel_id=1, source_target_pairs={{0,6},{1,7},{2,4},{3,5},{4,2},{5,3},{6,0},{7,1},{8,14},{9,15},{10,... | collective-permute-start | bytes 393224 | tf_op jit(solution)/shard_map/ppermute | solution.py:358
  17.7 4.4 %collective-permute-done.15 = bf16[512,128]{1,0:T(8,128)(2,1)S(1)} collective-permute-done((bf16[512,128]{1,0:T(8,128)(2,1)S(1)}, bf16[512,128]{1,0:T(8,128)(2,1)S(1)}, u32[]{:S(2)}, u32[]{:S(2)}) %collective-permute-start.15) | collective-permute-done | bytes 131104 | tf_op jit(solution)/shard_map/ppermute | solution.py:358
  22.2 1.4 %collective-permute-start.17 = (bf16[1,512,128]{2,1,0:T(8,128)(2,1)S(1)}, bf16[1,512,128]{2,1,0:T(8,128)(2,1)S(1)}, u32[]{:S(2)}, u32[]{:S(2)}) collective-permute-start(bf16[1,512,128]{2,1,0:T(8,128)(2,1)S(1)} %bitcast.18), channel_id=1, source_target_pairs={{0,8},{1,9},{2,10},{3,11},{4,12},{5,13},{6,14},{7,15},{8,0},{9,1},... | collective-permute-start | bytes 393224 | tf_op jit(solution)/shard_map/ppermute | solution.py:358
  23.6 0.8 collective-permute-start.18
  24.4 1.3 %collective-permute-start.16 = (bf16[1,512,128]{2,1,0:T(8,128)(2,1)S(1)}, bf16[1,512,128]{2,1,0:T(8,128)(2,1)S(1)}, u32[]{:S(2)}, u32[]{:S(2)}) collective-permute-start(bf16[1,512,128]{2,1,0:T(8,128)(2,1)S(1)} %bitcast.20), channel_id=1, source_target_pairs={{0,24},{1,25},{2,26},{3,27},{4,28},{5,29},{6,30},{7,31},{8,16},{9,... | collective-permute-start | bytes 393224 | tf_op jit(solution)/shard_map/ppermute | solution.py:358
  25.7 2.2 %copy-done = bf16[2048,1024]{1,0:T(8,128)(2,1)S(1)} copy-done((bf16[2048,1024]{1,0:T(8,128)(2,1)S(1)}, bf16[2048,1024]{1,0:T(8,128)(2,1)}, u32[]{:S(2)}) %copy-start) | copy-done | bytes 4194328
  27.8 0.3 load.1.refs_4_.refs_3_.refs_1_
  28.1 0.1 collective-permute-done.11
  28.2 1.6 %collective-permute-start.12 = (bf16[1,512,128]{2,1,0:T(8,128)(2,1)S(1)}, bf16[1,512,128]{2,1,0:T(8,128)(2,1)S(1)}, u32[]{:S(2)}, u32[]{:S(2)}) collective-permute-start(bf16[1,512,128]{2,1,0:T(8,128)(2,1)S(1)} %bitcast.14), channel_id=1, source_target_pairs={{0,8},{1,9},{2,10},{3,11},{4,12},{5,13},{6,14},{7,15},{8,0},{9,1},... | collective-permute-start | bytes 393224 | tf_op jit(solution)/shard_map/ppermute | solution.py:358
  29.8 0.6 collective-permute-start.13
  30.4 1.8 %piece_product.3.refs_3_ = f32[2048,128]{1,0:T(8,128)S(1)} custom-call(bf16[1,512,128]{2,1,0:T(8,128)(2,1)S(1)} %bitcast.21, bf16[1,512,128]{2,1,0:T(8,128)(2,1)S(1)} %collective-permute-done.17.refs_1_, bf16[1,512,128]{2,1,0:T(8,128)(2,1)S(1)} %collective-permute-done.18.refs_2_, bf16[2048,1024]{1,0:T(8,128)(2,1)S(1)} %load.1.refs_4_.refs_3_.refs_1_, ...), custom_call_target="tpu_custom_call" | custom-call | flops 805306368 | bytes 6291456 | tf_op jit(solution)/shard_map/piece_product/pallas_call | solution.py:193
  32.3 0.5 piece_product.5.x
  32.7 4.8 %collective-permute-start.24 = (bf16[1024,128]{1,0:T(8,128)(2,1)S(1)}, bf16[1024,128]{1,0:T(8,128)(2,1)S(1)}, u32[]{:S(2)}, u32[]{:S(2)}) collective-permute-start(bf16[1024,128]{1,0:T(8,128)(2,1)S(1)} %piece_product.5.x), channel_id=1, source_target_pairs={{0,2},{1,3},{2,0},{3,1},{4,6},{5,7},{6,4},{7,5},{8,10},{9,11},{10,... | collective-permute-start | bytes 786440 | tf_op jit(solution)/shard_map/ppermute | solution.py:358
  37.6 1.3 %collective-permute-start.14 = (bf16[1,512,128]{2,1,0:T(8,128)(2,1)S(1)}, bf16[1,512,128]{2,1,0:T(8,128)(2,1)S(1)}, u32[]{:S(2)}, u32[]{:S(2)}) collective-permute-start(bf16[1,512,128]{2,1,0:T(8,128)(2,1)S(1)} %bitcast.16), channel_id=1, source_target_pairs={{0,24},{1,25},{2,26},{3,27},{4,28},{5,29},{6,30},{7,31},{8,16},{9,... | collective-permute-start | bytes 393224 | tf_op jit(solution)/shard_map/ppermute | solution.py:358
  38.8 0.5 piece_product.4.x
  39.3 0.1 collective-permute-start.19
  39.5 1.6 %collective-permute-start.3 = (bf16[1,512,128]{2,1,0:T(8,128)(2,1)S(1)}, bf16[1,512,128]{2,1,0:T(8,128)(2,1)S(1)}, u32[]{:S(2)}, u32[]{:S(2)}) collective-permute-start(bf16[1,512,128]{2,1,0:T(8,128)(2,1)S(1)} %bitcast.6), channel_id=1, source_target_pairs={{0,8},{1,9},{2,10},{3,11},{4,12},{5,13},{6,14},{7,15},{8,0},{9,1},... | collective-permute-start | bytes 393224 | tf_op jit(solution)/shard_map/ppermute | solution.py:358
  41.1 1.9 %collective-permute-start.7 = (bf16[512,128]{1,0:T(8,128)(2,1)S(1)}, bf16[512,128]{1,0:T(8,128)(2,1)S(1)}, u32[]{:S(2)}, u32[]{:S(2)}) collective-permute-start(bf16[512,128]{1,0:T(8,128)(2,1)S(1)} %get-tuple-element.26), channel_id=1, source_target_pairs={{0,2},{1,3},{2,0},{3,1},{4,6},{5,7},{6,4},{7,5},{8,10},{9,11},{10,... | collective-permute-start | bytes 393224 | tf_op jit(solution)/shard_map/ppermute | solution.py:358
  43.0 0.5 collective-permute-done.14.refs_3_
  43.5 1.4 %collective-permute-start.4 = (bf16[1,512,128]{2,1,0:T(8,128)(2,1)S(1)}, bf16[1,512,128]{2,1,0:T(8,128)(2,1)S(1)}, u32[]{:S(2)}, u32[]{:S(2)}) collective-permute-start(bf16[1,512,128]{2,1,0:T(8,128)(2,1)S(1)} %bitcast.7), channel_id=1, source_target_pairs={{0,16},{1,17},{2,18},{3,19},{4,20},{5,21},{6,22},{7,23},{8,24},{9,... | collective-permute-start | bytes 393224 | tf_op jit(solution)/shard_map/ppermute | solution.py:358
  45.0 2.4 %partial_product.5 = (bf16[1024,128]{1,0:T(8,128)(2,1)S(1)}, bf16[1024,128]{1,0:T(8,128)(2,1)S(1)}) custom-call(bf16[1,512,128]{2,1,0:T(8,128)(2,1)S(1)} %bitcast.17, bf16[1,512,128]{2,1,0:T(8,128)(2,1)S(1)} %collective-permute-done.12.refs_1_, bf16[1,512,128]{2,1,0:T(8,128)(2,1)S(1)} %collective-permute-done.13.refs_2_, ...), custom_call_target="tpu_custom_call" | custom-call | flops 1073741824 | bytes 8388608 | tf_op jit(solution)/shard_map/partial_product/pallas_call | solution.py:152
  47.3 0.1 collective-permute-start.27
  47.5 4.9 %collective-permute-done.7 = bf16[512,128]{1,0:T(8,128)(2,1)S(1)} collective-permute-done((bf16[512,128]{1,0:T(8,128)(2,1)S(1)}, bf16[512,128]{1,0:T(8,128)(2,1)S(1)}, u32[]{:S(2)}, u32[]{:S(2)}) %collective-permute-start.7) | collective-permute-done | bytes 131104 | tf_op jit(solution)/shard_map/ppermute | solution.py:358
  52.4 1.5 %collective-permute-start.8 = (bf16[1,512,128]{2,1,0:T(8,128)(2,1)S(1)}, bf16[1,512,128]{2,1,0:T(8,128)(2,1)S(1)}, u32[]{:S(2)}, u32[]{:S(2)}) collective-permute-start(bf16[1,512,128]{2,1,0:T(8,128)(2,1)S(1)} %bitcast.10), channel_id=1, source_target_pairs={{0,8},{1,9},{2,10},{3,11},{4,12},{5,13},{6,14},{7,15},{8,0},{9,1},... | collective-permute-start | bytes 393224 | tf_op jit(solution)/shard_map/ppermute | solution.py:358
  53.9 0.6 collective-permute-start.9
  54.5 0.1 add.29
  54.5 0.1 collective-permute-start.25
  54.6 1.5 %collective-permute-start.10 = (bf16[1,512,128]{2,1,0:T(8,128)(2,1)S(1)}, bf16[1,512,128]{2,1,0:T(8,128)(2,1)S(1)}, u32[]{:S(2)}, u32[]{:S(2)}) collective-permute-start(bf16[1,512,128]{2,1,0:T(8,128)(2,1)S(1)} %bitcast.12), channel_id=1, source_target_pairs={{0,24},{1,25},{2,26},{3,27},{4,28},{5,29},{6,30},{7,31},{8,16},{9,... | collective-permute-start | bytes 393224 | tf_op jit(solution)/shard_map/ppermute | solution.py:358
  56.1 0.1 add.26
  56.2 1.2 %collective-permute-done.8.refs_1_ = bf16[1,512,128]{2,1,0:T(8,128)(2,1)S(1)} collective-permute-done((bf16[1,512,128]{2,1,0:T(8,128)(2,1)S(1)}, bf16[1,512,128]{2,1,0:T(8,128)(2,1)S(1)}, u32[]{:S(2)}, u32[]{:S(2)}) %collective-permute-start.8) | collective-permute-done | bytes 131104 | tf_op jit(solution)/shard_map/ppermute | solution.py:358
  57.4 1.6 %collective-permute-start.22 = (bf16[1024,128]{1,0:T(8,128)(2,1)S(1)}, bf16[1024,128]{1,0:T(8,128)(2,1)S(1)}, u32[]{:S(2)}, u32[]{:S(2)}) collective-permute-start(bf16[1024,128]{1,0:T(8,128)(2,1)S(1)} %get-tuple-element.29.x), channel_id=1, source_target_pairs={{0,2},{1,3},{2,0},{3,1},{4,6},{5,7},{6,4},{7,5},{8,10},{9,11},{10,... | collective-permute-start | bytes 786440 | tf_op jit(solution)/shard_map/ppermute | solution.py:358
  59.0 2.7 %collective-permute-done.9.refs_2_ = bf16[1,512,128]{2,1,0:T(8,128)(2,1)S(1)} collective-permute-done((bf16[1,512,128]{2,1,0:T(8,128)(2,1)S(1)}, bf16[1,512,128]{2,1,0:T(8,128)(2,1)S(1)}, u32[]{:S(2)}, u32[]{:S(2)}) %collective-permute-start.9) | collective-permute-done | bytes 131104 | tf_op jit(solution)/shard_map/ppermute | solution.py:358
  61.7 0.5 collective-permute-start.31
  62.2 1.7 %collective-permute-start.29 = (bf16[1024,128]{1,0:T(8,128)(2,1)S(1)}, bf16[1024,128]{1,0:T(8,128)(2,1)S(1)}, u32[]{:S(2)}, u32[]{:S(2)}) collective-permute-start(bf16[1024,128]{1,0:T(8,128)(2,1)S(1)} %get-tuple-element.35.refs_3_), channel_id=1, source_target_pairs={{0,2},{1,3},{2,0},{3,1},{4,6},{5,7},{6,4},{7,5},{8,10},{9,11},{10,... | collective-permute-start | bytes 786440 | tf_op jit(solution)/shard_map/ppermute | solution.py:358
  63.8 1.5 %collective-permute-start.5 = (bf16[1,512,128]{2,1,0:T(8,128)(2,1)S(1)}, bf16[1,512,128]{2,1,0:T(8,128)(2,1)S(1)}, u32[]{:S(2)}, u32[]{:S(2)}) collective-permute-start(bf16[1,512,128]{2,1,0:T(8,128)(2,1)S(1)} %bitcast.8), channel_id=1, source_target_pairs={{0,24},{1,25},{2,26},{3,27},{4,28},{5,29},{6,30},{7,31},{8,16},{9,... | collective-permute-start | bytes 393224 | tf_op jit(solution)/shard_map/ppermute | solution.py:358
  65.4 2.4 %partial_product.4 = (bf16[1024,128]{1,0:T(8,128)(2,1)S(1)}, bf16[1024,128]{1,0:T(8,128)(2,1)S(1)}) custom-call(bf16[1,512,128]{2,1,0:T(8,128)(2,1)S(1)} %bitcast.13, bf16[1,512,128]{2,1,0:T(8,128)(2,1)S(1)} %collective-permute-done.8.refs_1_, bf16[1,512,128]{2,1,0:T(8,128)(2,1)S(1)} %collective-permute-done.9.refs_2_, ...), custom_call_target="tpu_custom_call" | custom-call | flops 1073741824 | bytes 8388608 | tf_op jit(solution)/shard_map/partial_product/pallas_call | solution.py:152
  67.7 0.1 add.31
  67.8 0.1 add.30
  67.9 0.1 collective-permute-start.28
  68.0 2.1 %collective-permute-start.26 = (bf16[1024,128]{1,0:T(8,128)(2,1)S(1)}, bf16[1024,128]{1,0:T(8,128)(2,1)S(1)}, u32[]{:S(2)}, u32[]{:S(2)}) collective-permute-start(bf16[1024,128]{1,0:T(8,128)(2,1)S(1)} %add.30), channel_id=1, source_target_pairs={{0,2},{1,3},{2,0},{3,1},{4,6},{5,7},{6,4},{7,5},{8,10},{9,11},{10,... | collective-permute-start | bytes 786440 | tf_op jit(solution)/shard_map/ppermute | solution.py:358
  70.2 0.1 add.27.refs_0_
  70.3 0.1 collective-permute-start.23
  70.4 4.8 %collective-permute-start.21 = (bf16[1024,128]{1,0:T(8,128)(2,1)S(1)}, bf16[1024,128]{1,0:T(8,128)(2,1)S(1)}, u32[]{:S(2)}, u32[]{:S(2)}) collective-permute-start(bf16[1024,128]{1,0:T(8,128)(2,1)S(1)} %add.27.refs_0_), channel_id=1, source_target_pairs={{0,2},{1,3},{2,0},{3,1},{4,6},{5,7},{6,4},{7,5},{8,10},{9,11},{10,... | collective-permute-start | bytes 786440 | tf_op jit(solution)/shard_map/ppermute | solution.py:358
  75.1 0.3 ahead.5
  75.4 0.1 collective-permute-start.32
  75.5 0.3 ahead.4
  75.8 0.9 collective-permute-done.32.refs_1_
  76.7 8.8 %collective-permute-start.30 = (bf16[128,128]{1,0:T(8,128)(2,1)S(1)}, bf16[128,128]{1,0:T(8,128)(2,1)S(1)}, u32[]{:S(2)}, u32[]{:S(2)}) collective-permute-start(bf16[128,128]{1,0:T(8,128)(2,1)S(1)} %ahead.4), channel_id=1, source_target_pairs={{0,2},{1,3},{2,0},{3,1},{4,6},{5,7},{6,4},{7,5},{8,10},{9,11},{10,... | collective-permute-start | bytes 98312 | tf_op jit(solution)/shard_map/ppermute | solution.py:358
  85.5 2.4 %partial_product.3 = (bf16[1024,128]{1,0:T(8,128)(2,1)S(1)}, bf16[1024,128]{1,0:T(8,128)(2,1)S(1)}) custom-call(bf16[1,512,128]{2,1,0:T(8,128)(2,1)S(1)} %bitcast.9, bf16[1,512,128]{2,1,0:T(8,128)(2,1)S(1)} %collective-permute-done.3.refs_1_, bf16[1,512,128]{2,1,0:T(8,128)(2,1)S(1)} %collective-permute-done.4.refs_2_, ...), custom_call_target="tpu_custom_call" | custom-call | flops 1073741824 | bytes 8388608 | tf_op jit(solution)/shard_map/partial_product/pallas_call | solution.py:152
  87.9 0.4 ahead.3.own
  88.3 0.4 gathered.1
  88.7 1.6 %collective-permute-start.35 = (bf16[128,128]{1,0:T(8,128)(2,1)S(1)}, bf16[128,128]{1,0:T(8,128)(2,1)S(1)}, u32[]{:S(2)}, u32[]{:S(2)}) collective-permute-start(bf16[128,128]{1,0:T(8,128)(2,1)S(1)} %get-tuple-element.37), channel_id=1, source_target_pairs={{0,24},{1,25},{2,26},{3,27},{4,28},{5,29},{6,30},{7,31},{8,16},{9,... | collective-permute-start | bytes 98312 | tf_op jit(solution)/shard_map/ppermute | solution.py:358
  90.3 1.5 %collective-permute-start.34 = (bf16[128,128]{1,0:T(8,128)(2,1)S(1)}, bf16[128,128]{1,0:T(8,128)(2,1)S(1)}, u32[]{:S(2)}, u32[]{:S(2)}) collective-permute-start(bf16[128,128]{1,0:T(8,128)(2,1)S(1)} %get-tuple-element.37), channel_id=1, source_target_pairs={{0,16},{1,17},{2,18},{3,19},{4,20},{5,21},{6,22},{7,23},{8,24},{9,... | collective-permute-start | bytes 98312 | tf_op jit(solution)/shard_map/ppermute | solution.py:358
  91.7 0.5 collective-permute-start.33
  92.3 1.6 %masked.2.refs_3_ = f32[128,2048]{1,0:T(8,128)} custom-call(s32[8,64]{1,0:T(8,128)S(1)} %copy-done.1, bf16[1024,128]{1,0:T(8,128)(2,1)S(1)} %get-tuple-element.31.refs_0_, bf16[1024,128]{1,0:T(8,128)(2,1)S(1)} %collective-permute-done.26.refs_1_.refs_2_, bf16[1024,128]{1,0:T(8,128)(2,1)S(1)} %collective-permute-done.28.refs_2_.refs_3_), custom_call_target="tpu_custom_call" | custom-call | flops 524288 | bytes 1310720 | tf_op jit(solution)/shard_map/masked/pallas_call | solution.py:328
  93.9 1.6 %masked.3 = f32[128,2048]{1,0:T(8,128)} custom-call(s32[8,64]{1,0:T(8,128)S(1)} %copy-done.1, bf16[1024,128]{1,0:T(8,128)(2,1)S(1)} %get-tuple-element.25.refs_0_.refs_1_, bf16[1024,128]{1,0:T(8,128)(2,1)S(1)} %collective-permute-done.21.refs_1_, bf16[1024,128]{1,0:T(8,128)(2,1)S(1)} %collective-permute-done.23.refs_2_, ...), custom_call_target="tpu_custom_call", output_to_operand_aliasing={{}: (4, {})} | custom-call | flops 524288 | bytes 1310720 | tf_op jit(solution)/shard_map/masked/pallas_call | solution.py:328
  95.5 0.1 collective-permute-done.33
  95.6 0.6 bitcast_add_fusion
  (36 shorter events, 0.2 us)
Async XLA Ops:
  0.6 29.8 %collective-permute-start.6 = (bf16[2048,1024]{1,0:T(8,128)(2,1)}, bf16[2048,1024]{1,0:T(8,128)(2,1)S(1)}, u32[]{:S(2)}, u32[]{:S(2)}) collective-permute-start(bf16[2048,1024]{1,0:T(8,128)(2,1)} %tile.1), channel_id=1, source_target_pairs={{0,1},{1,0},{2,3},{3,2},{4,5},{5,4},{6,7},{7,6},{8,9},{9,8},{10,11... | collective-permute-start | bytes 12582920 | tf_op jit(solution)/shard_map/ppermute | solution.py:358
  3.1 6.9 %collective-permute-start = (bf16[512,128]{1,0:T(8,128)(2,1)S(1)}, bf16[512,128]{1,0:T(8,128)(2,1)S(1)}, u32[]{:S(2)}, u32[]{:S(2)}) collective-permute-start(bf16[512,128]{1,0:T(8,128)(2,1)S(1)} %get-tuple-element.21), channel_id=1, source_target_pairs={{0,8},{1,9},{2,10},{3,11},{4,12},{5,13},{6,14},{7,15},{8,0},{9,1},... | collective-permute-start | bytes 393224 | tf_op jit(solution)/shard_map/ppermute | solution.py:358
  5.6 8.4 %collective-permute-start.1 = (bf16[512,128]{1,0:T(8,128)(2,1)S(1)}, bf16[512,128]{1,0:T(8,128)(2,1)S(1)}, u32[]{:S(2)}, u32[]{:S(2)}) collective-permute-start(bf16[512,128]{1,0:T(8,128)(2,1)S(1)} %get-tuple-element.22), channel_id=1, source_target_pairs={{0,16},{1,17},{2,18},{3,19},{4,20},{5,21},{6,22},{7,23},{8,24},{9,... | collective-permute-start | bytes 393224 | tf_op jit(solution)/shard_map/ppermute | solution.py:358
  7.1 6.9 %collective-permute-start.2 = (bf16[512,128]{1,0:T(8,128)(2,1)S(1)}, bf16[512,128]{1,0:T(8,128)(2,1)S(1)}, u32[]{:S(2)}, u32[]{:S(2)}) collective-permute-start(bf16[512,128]{1,0:T(8,128)(2,1)S(1)} %get-tuple-element.23), channel_id=1, source_target_pairs={{0,24},{1,25},{2,26},{3,27},{4,28},{5,29},{6,30},{7,31},{8,16},{9,... | collective-permute-start | bytes 393224 | tf_op jit(solution)/shard_map/ppermute | solution.py:358
  14.1 8.1 %collective-permute-start.15 = (bf16[512,128]{1,0:T(8,128)(2,1)S(1)}, bf16[512,128]{1,0:T(8,128)(2,1)S(1)}, u32[]{:S(2)}, u32[]{:S(2)}) collective-permute-start(bf16[512,128]{1,0:T(8,128)(2,1)S(1)} %get-tuple-element.30), channel_id=1, source_target_pairs={{0,6},{1,7},{2,4},{3,5},{4,2},{5,3},{6,0},{7,1},{8,14},{9,15},{10,... | collective-permute-start | bytes 393224 | tf_op jit(solution)/shard_map/ppermute | solution.py:358
  17.7 10.5 %collective-permute-start.11 = (bf16[512,128]{1,0:T(8,128)(2,1)S(1)}, bf16[512,128]{1,0:T(8,128)(2,1)S(1)}, u32[]{:S(2)}, u32[]{:S(2)}) collective-permute-start(bf16[512,128]{1,0:T(8,128)(2,1)S(1)} %get-tuple-element.28), channel_id=1, source_target_pairs={{0,4},{1,5},{2,6},{3,7},{4,0},{5,1},{6,2},{7,3},{8,12},{9,13},{10,... | collective-permute-start | bytes 393224 | tf_op jit(solution)/shard_map/ppermute | solution.py:358
  22.2 7.7 %collective-permute-start.17 = (bf16[1,512,128]{2,1,0:T(8,128)(2,1)S(1)}, bf16[1,512,128]{2,1,0:T(8,128)(2,1)S(1)}, u32[]{:S(2)}, u32[]{:S(2)}) collective-permute-start(bf16[1,512,128]{2,1,0:T(8,128)(2,1)S(1)} %bitcast.18), channel_id=1, source_target_pairs={{0,8},{1,9},{2,10},{3,11},{4,12},{5,13},{6,14},{7,15},{8,0},{9,1},... | collective-permute-start | bytes 393224 | tf_op jit(solution)/shard_map/ppermute | solution.py:358
  23.6 6.8 %collective-permute-start.18 = (bf16[1,512,128]{2,1,0:T(8,128)(2,1)S(1)}, bf16[1,512,128]{2,1,0:T(8,128)(2,1)S(1)}, u32[]{:S(2)}, u32[]{:S(2)}) collective-permute-start(bf16[1,512,128]{2,1,0:T(8,128)(2,1)S(1)} %bitcast.19), channel_id=1, source_target_pairs={{0,16},{1,17},{2,18},{3,19},{4,20},{5,21},{6,22},{7,23},{8,24},{9,... | collective-permute-start | bytes 393224 | tf_op jit(solution)/shard_map/ppermute | solution.py:358
  24.4 7.9 %collective-permute-start.16 = (bf16[1,512,128]{2,1,0:T(8,128)(2,1)S(1)}, bf16[1,512,128]{2,1,0:T(8,128)(2,1)S(1)}, u32[]{:S(2)}, u32[]{:S(2)}) collective-permute-start(bf16[1,512,128]{2,1,0:T(8,128)(2,1)S(1)} %bitcast.20), channel_id=1, source_target_pairs={{0,24},{1,25},{2,26},{3,27},{4,28},{5,29},{6,30},{7,31},{8,16},{9,... | collective-permute-start | bytes 393224 | tf_op jit(solution)/shard_map/ppermute | solution.py:358
  25.7 2.2 %copy-start = (bf16[2048,1024]{1,0:T(8,128)(2,1)S(1)}, bf16[2048,1024]{1,0:T(8,128)(2,1)}, u32[]{:S(2)}) copy-start(bf16[2048,1024]{1,0:T(8,128)(2,1)} %tile.1) | copy-start | bytes 12582916
  28.2 11.2 %collective-permute-start.12 = (bf16[1,512,128]{2,1,0:T(8,128)(2,1)S(1)}, bf16[1,512,128]{2,1,0:T(8,128)(2,1)S(1)}, u32[]{:S(2)}, u32[]{:S(2)}) collective-permute-start(bf16[1,512,128]{2,1,0:T(8,128)(2,1)S(1)} %bitcast.14), channel_id=1, source_target_pairs={{0,8},{1,9},{2,10},{3,11},{4,12},{5,13},{6,14},{7,15},{8,0},{9,1},... | collective-permute-start | bytes 393224 | tf_op jit(solution)/shard_map/ppermute | solution.py:358
  29.8 11.2 %collective-permute-start.13 = (bf16[1,512,128]{2,1,0:T(8,128)(2,1)S(1)}, bf16[1,512,128]{2,1,0:T(8,128)(2,1)S(1)}, u32[]{:S(2)}, u32[]{:S(2)}) collective-permute-start(bf16[1,512,128]{2,1,0:T(8,128)(2,1)S(1)} %bitcast.15), channel_id=1, source_target_pairs={{0,16},{1,17},{2,18},{3,19},{4,20},{5,21},{6,22},{7,23},{8,24},{9,... | collective-permute-start | bytes 393224 | tf_op jit(solution)/shard_map/ppermute | solution.py:358
  32.7 21.1 %collective-permute-start.24 = (bf16[1024,128]{1,0:T(8,128)(2,1)S(1)}, bf16[1024,128]{1,0:T(8,128)(2,1)S(1)}, u32[]{:S(2)}, u32[]{:S(2)}) collective-permute-start(bf16[1024,128]{1,0:T(8,128)(2,1)S(1)} %piece_product.5.x), channel_id=1, source_target_pairs={{0,2},{1,3},{2,0},{3,1},{4,6},{5,7},{6,4},{7,5},{8,10},{9,11},{10,... | collective-permute-start | bytes 786440 | tf_op jit(solution)/shard_map/ppermute | solution.py:358
  37.6 6.0 %collective-permute-start.14 = (bf16[1,512,128]{2,1,0:T(8,128)(2,1)S(1)}, bf16[1,512,128]{2,1,0:T(8,128)(2,1)S(1)}, u32[]{:S(2)}, u32[]{:S(2)}) collective-permute-start(bf16[1,512,128]{2,1,0:T(8,128)(2,1)S(1)} %bitcast.16), channel_id=1, source_target_pairs={{0,24},{1,25},{2,26},{3,27},{4,28},{5,29},{6,30},{7,31},{8,16},{9,... | collective-permute-start | bytes 393224 | tf_op jit(solution)/shard_map/ppermute | solution.py:358
  39.3 15.3 %collective-permute-start.19 = (bf16[1024,128]{1,0:T(8,128)(2,1)S(1)}, bf16[1024,128]{1,0:T(8,128)(2,1)S(1)}, u32[]{:S(2)}, u32[]{:S(2)}) collective-permute-start(bf16[1024,128]{1,0:T(8,128)(2,1)S(1)} %piece_product.4.x), channel_id=1, source_target_pairs={{0,2},{1,3},{2,0},{3,1},{4,6},{5,7},{6,4},{7,5},{8,10},{9,11},{10,... | collective-permute-start | bytes 786440 | tf_op jit(solution)/shard_map/ppermute | solution.py:358
  39.5 7.9 %collective-permute-start.3 = (bf16[1,512,128]{2,1,0:T(8,128)(2,1)S(1)}, bf16[1,512,128]{2,1,0:T(8,128)(2,1)S(1)}, u32[]{:S(2)}, u32[]{:S(2)}) collective-permute-start(bf16[1,512,128]{2,1,0:T(8,128)(2,1)S(1)} %bitcast.6), channel_id=1, source_target_pairs={{0,8},{1,9},{2,10},{3,11},{4,12},{5,13},{6,14},{7,15},{8,0},{9,1},... | collective-permute-start | bytes 393224 | tf_op jit(solution)/shard_map/ppermute | solution.py:358
  41.1 11.3 %collective-permute-start.7 = (bf16[512,128]{1,0:T(8,128)(2,1)S(1)}, bf16[512,128]{1,0:T(8,128)(2,1)S(1)}, u32[]{:S(2)}, u32[]{:S(2)}) collective-permute-start(bf16[512,128]{1,0:T(8,128)(2,1)S(1)} %get-tuple-element.26), channel_id=1, source_target_pairs={{0,2},{1,3},{2,0},{3,1},{4,6},{5,7},{6,4},{7,5},{8,10},{9,11},{10,... | collective-permute-start | bytes 393224 | tf_op jit(solution)/shard_map/ppermute | solution.py:358
  43.5 11.0 %collective-permute-start.4 = (bf16[1,512,128]{2,1,0:T(8,128)(2,1)S(1)}, bf16[1,512,128]{2,1,0:T(8,128)(2,1)S(1)}, u32[]{:S(2)}, u32[]{:S(2)}) collective-permute-start(bf16[1,512,128]{2,1,0:T(8,128)(2,1)S(1)} %bitcast.7), channel_id=1, source_target_pairs={{0,16},{1,17},{2,18},{3,19},{4,20},{5,21},{6,22},{7,23},{8,24},{9,... | collective-permute-start | bytes 393224 | tf_op jit(solution)/shard_map/ppermute | solution.py:358
  47.3 14.8 %collective-permute-start.27 = (bf16[1024,128]{1,0:T(8,128)(2,1)S(1)}, bf16[1024,128]{1,0:T(8,128)(2,1)S(1)}, u32[]{:S(2)}, u32[]{:S(2)}) collective-permute-start(bf16[1024,128]{1,0:T(8,128)(2,1)S(1)} %get-tuple-element.33.x), channel_id=1, source_target_pairs={{0,2},{1,3},{2,0},{3,1},{4,6},{5,7},{6,4},{7,5},{8,10},{9,11},{10,... | collective-permute-start | bytes 786440 | tf_op jit(solution)/shard_map/ppermute | solution.py:358
  52.4 5.0 %collective-permute-start.8 = (bf16[1,512,128]{2,1,0:T(8,128)(2,1)S(1)}, bf16[1,512,128]{2,1,0:T(8,128)(2,1)S(1)}, u32[]{:S(2)}, u32[]{:S(2)}) collective-permute-start(bf16[1,512,128]{2,1,0:T(8,128)(2,1)S(1)} %bitcast.10), channel_id=1, source_target_pairs={{0,8},{1,9},{2,10},{3,11},{4,12},{5,13},{6,14},{7,15},{8,0},{9,1},... | collective-permute-start | bytes 393224 | tf_op jit(solution)/shard_map/ppermute | solution.py:358
  53.9 7.8 %collective-permute-start.9 = (bf16[1,512,128]{2,1,0:T(8,128)(2,1)S(1)}, bf16[1,512,128]{2,1,0:T(8,128)(2,1)S(1)}, u32[]{:S(2)}, u32[]{:S(2)}) collective-permute-start(bf16[1,512,128]{2,1,0:T(8,128)(2,1)S(1)} %bitcast.11), channel_id=1, source_target_pairs={{0,16},{1,17},{2,18},{3,19},{4,20},{5,21},{6,22},{7,23},{8,24},{9,... | collective-permute-start | bytes 393224 | tf_op jit(solution)/shard_map/ppermute | solution.py:358
  54.5 9.3 %collective-permute-start.25 = (bf16[1024,128]{1,0:T(8,128)(2,1)S(1)}, bf16[1024,128]{1,0:T(8,128)(2,1)S(1)}, u32[]{:S(2)}, u32[]{:S(2)}) collective-permute-start(bf16[1024,128]{1,0:T(8,128)(2,1)S(1)} %add.29), channel_id=1, source_target_pairs={{0,1},{1,0},{2,4},{3,5},{4,2},{5,3},{6,7},{7,6},{8,9},{9,8},{10,12... | collective-permute-start | bytes 786440 | tf_op jit(solution)/shard_map/ppermute | solution.py:358
  54.6 7.0 %collective-permute-start.10 = (bf16[1,512,128]{2,1,0:T(8,128)(2,1)S(1)}, bf16[1,512,128]{2,1,0:T(8,128)(2,1)S(1)}, u32[]{:S(2)}, u32[]{:S(2)}) collective-permute-start(bf16[1,512,128]{2,1,0:T(8,128)(2,1)S(1)} %bitcast.12), channel_id=1, source_target_pairs={{0,24},{1,25},{2,26},{3,27},{4,28},{5,29},{6,30},{7,31},{8,16},{9,... | collective-permute-start | bytes 393224 | tf_op jit(solution)/shard_map/ppermute | solution.py:358
  57.4 10.5 %collective-permute-start.22 = (bf16[1024,128]{1,0:T(8,128)(2,1)S(1)}, bf16[1024,128]{1,0:T(8,128)(2,1)S(1)}, u32[]{:S(2)}, u32[]{:S(2)}) collective-permute-start(bf16[1024,128]{1,0:T(8,128)(2,1)S(1)} %get-tuple-element.29.x), channel_id=1, source_target_pairs={{0,2},{1,3},{2,0},{3,1},{4,6},{5,7},{6,4},{7,5},{8,10},{9,11},{10,... | collective-permute-start | bytes 786440 | tf_op jit(solution)/shard_map/ppermute | solution.py:358
  61.7 6.3 %collective-permute-start.20 = (bf16[1024,128]{1,0:T(8,128)(2,1)S(1)}, bf16[1024,128]{1,0:T(8,128)(2,1)S(1)}, u32[]{:S(2)}, u32[]{:S(2)}) collective-permute-start(bf16[1024,128]{1,0:T(8,128)(2,1)S(1)} %add.26), channel_id=1, source_target_pairs={{0,1},{1,0},{2,4},{3,5},{4,2},{5,3},{6,7},{7,6},{8,9},{9,8},{10,12... | collective-permute-start | bytes 786440 | tf_op jit(solution)/shard_map/ppermute | solution.py:358
  61.7 8.7 %collective-permute-start.31 = (bf16[1024,128]{1,0:T(8,128)(2,1)S(1)}, bf16[1024,128]{1,0:T(8,128)(2,1)S(1)}, u32[]{:S(2)}, u32[]{:S(2)}) collective-permute-start(bf16[1024,128]{1,0:T(8,128)(2,1)S(1)} %get-tuple-element.35.refs_3_), channel_id=1, source_target_pairs={{0,1},{1,0},{2,4},{3,5},{4,2},{5,3},{6,7},{7,6},{8,9},{9,8},{10,12... | collective-permute-start | bytes 786440 | tf_op jit(solution)/shard_map/ppermute | solution.py:358
  62.2 13.2 %collective-permute-start.29 = (bf16[1024,128]{1,0:T(8,128)(2,1)S(1)}, bf16[1024,128]{1,0:T(8,128)(2,1)S(1)}, u32[]{:S(2)}, u32[]{:S(2)}) collective-permute-start(bf16[1024,128]{1,0:T(8,128)(2,1)S(1)} %get-tuple-element.35.refs_3_), channel_id=1, source_target_pairs={{0,2},{1,3},{2,0},{3,1},{4,6},{5,7},{6,4},{7,5},{8,10},{9,11},{10,... | collective-permute-start | bytes 786440 | tf_op jit(solution)/shard_map/ppermute | solution.py:358
  63.8 6.4 %collective-permute-start.5 = (bf16[1,512,128]{2,1,0:T(8,128)(2,1)S(1)}, bf16[1,512,128]{2,1,0:T(8,128)(2,1)S(1)}, u32[]{:S(2)}, u32[]{:S(2)}) collective-permute-start(bf16[1,512,128]{2,1,0:T(8,128)(2,1)S(1)} %bitcast.8), channel_id=1, source_target_pairs={{0,24},{1,25},{2,26},{3,27},{4,28},{5,29},{6,30},{7,31},{8,16},{9,... | collective-permute-start | bytes 393224 | tf_op jit(solution)/shard_map/ppermute | solution.py:358
  67.9 20.3 %collective-permute-start.28 = (bf16[1024,128]{1,0:T(8,128)(2,1)S(1)}, bf16[1024,128]{1,0:T(8,128)(2,1)S(1)}, u32[]{:S(2)}, u32[]{:S(2)}) collective-permute-start(bf16[1024,128]{1,0:T(8,128)(2,1)S(1)} %add.31), channel_id=1, source_target_pairs={{0,1},{1,0},{2,4},{3,5},{4,2},{5,3},{6,7},{7,6},{8,9},{9,8},{10,12... | collective-permute-start | bytes 786440 | tf_op jit(solution)/shard_map/ppermute | solution.py:358
  68.0 20.3 %collective-permute-start.26 = (bf16[1024,128]{1,0:T(8,128)(2,1)S(1)}, bf16[1024,128]{1,0:T(8,128)(2,1)S(1)}, u32[]{:S(2)}, u32[]{:S(2)}) collective-permute-start(bf16[1024,128]{1,0:T(8,128)(2,1)S(1)} %add.30), channel_id=1, source_target_pairs={{0,2},{1,3},{2,0},{3,1},{4,6},{5,7},{6,4},{7,5},{8,10},{9,11},{10,... | collective-permute-start | bytes 786440 | tf_op jit(solution)/shard_map/ppermute | solution.py:358
  70.3 23.6 %collective-permute-start.23 = (bf16[1024,128]{1,0:T(8,128)(2,1)S(1)}, bf16[1024,128]{1,0:T(8,128)(2,1)S(1)}, u32[]{:S(2)}, u32[]{:S(2)}) collective-permute-start(bf16[1024,128]{1,0:T(8,128)(2,1)S(1)} %add.28.refs_0_), channel_id=1, source_target_pairs={{0,1},{1,0},{2,4},{3,5},{4,2},{5,3},{6,7},{7,6},{8,9},{9,8},{10,12... | collective-permute-start | bytes 786440 | tf_op jit(solution)/shard_map/ppermute | solution.py:358
  70.4 23.5 %collective-permute-start.21 = (bf16[1024,128]{1,0:T(8,128)(2,1)S(1)}, bf16[1024,128]{1,0:T(8,128)(2,1)S(1)}, u32[]{:S(2)}, u32[]{:S(2)}) collective-permute-start(bf16[1024,128]{1,0:T(8,128)(2,1)S(1)} %add.27.refs_0_), channel_id=1, source_target_pairs={{0,2},{1,3},{2,0},{3,1},{4,6},{5,7},{6,4},{7,5},{8,10},{9,11},{10,... | collective-permute-start | bytes 786440 | tf_op jit(solution)/shard_map/ppermute | solution.py:358
  75.4 1.3 %collective-permute-start.32 = (bf16[128,128]{1,0:T(8,128)(2,1)S(1)}, bf16[128,128]{1,0:T(8,128)(2,1)S(1)}, u32[]{:S(2)}, u32[]{:S(2)}) collective-permute-start(bf16[128,128]{1,0:T(8,128)(2,1)S(1)} %ahead.5), channel_id=1, source_target_pairs={{0,1},{1,0},{2,4},{3,5},{4,2},{5,3},{6,7},{7,6},{8,9},{9,8},{10,12... | collective-permute-start | bytes 98312 | tf_op jit(solution)/shard_map/ppermute | solution.py:358
  75.8 16.5 %copy-start.1 = (s32[8,64]{1,0:T(8,128)S(1)}, s32[8,64]{1,0:T(8,128)}, u32[]{:S(2)}) copy-start(s32[8,64]{1,0:T(8,128)} %listed.5) | copy-start | bytes 6148
  76.7 11.6 %collective-permute-start.30 = (bf16[128,128]{1,0:T(8,128)(2,1)S(1)}, bf16[128,128]{1,0:T(8,128)(2,1)S(1)}, u32[]{:S(2)}, u32[]{:S(2)}) collective-permute-start(bf16[128,128]{1,0:T(8,128)(2,1)S(1)} %ahead.4), channel_id=1, source_target_pairs={{0,2},{1,3},{2,0},{3,1},{4,6},{5,7},{6,4},{7,5},{8,10},{9,11},{10,... | collective-permute-start | bytes 98312 | tf_op jit(solution)/shard_map/ppermute | solution.py:358
  87.9 7.8 %copy-start.2 = (f32[1,128,128]{2,1,0:T(8,128)S(1)}, f32[1,128,128]{2,1,0:T(8,128)}, u32[]{:S(2)}) copy-start(f32[1,128,128]{2,1,0:T(8,128)} %param.8) | copy-start | bytes 196612
  88.7 6.8 %collective-permute-start.35 = (bf16[128,128]{1,0:T(8,128)(2,1)S(1)}, bf16[128,128]{1,0:T(8,128)(2,1)S(1)}, u32[]{:S(2)}, u32[]{:S(2)}) collective-permute-start(bf16[128,128]{1,0:T(8,128)(2,1)S(1)} %get-tuple-element.37), channel_id=1, source_target_pairs={{0,24},{1,25},{2,26},{3,27},{4,28},{5,29},{6,30},{7,31},{8,16},{9,... | collective-permute-start | bytes 98312 | tf_op jit(solution)/shard_map/ppermute | solution.py:358
  90.3 5.2 %collective-permute-start.34 = (bf16[128,128]{1,0:T(8,128)(2,1)S(1)}, bf16[128,128]{1,0:T(8,128)(2,1)S(1)}, u32[]{:S(2)}, u32[]{:S(2)}) collective-permute-start(bf16[128,128]{1,0:T(8,128)(2,1)S(1)} %get-tuple-element.37), channel_id=1, source_target_pairs={{0,16},{1,17},{2,18},{3,19},{4,20},{5,21},{6,22},{7,23},{8,24},{9,... | collective-permute-start | bytes 98312 | tf_op jit(solution)/shard_map/ppermute | solution.py:358
  91.7 3.9 %collective-permute-start.33 = (bf16[128,128]{1,0:T(8,128)(2,1)S(1)}, bf16[128,128]{1,0:T(8,128)(2,1)S(1)}, u32[]{:S(2)}, u32[]{:S(2)}) collective-permute-start(bf16[128,128]{1,0:T(8,128)(2,1)S(1)} %get-tuple-element.37), channel_id=1, source_target_pairs={{0,8},{1,9},{2,10},{3,11},{4,12},{5,13},{6,14},{7,15},{8,0},{9,1},... | collective-permute-start | bytes 98312 | tf_op jit(solution)/shard_map/ppermute | solution.py:358

commit v6 on v5

--- a/solution.py
+++ b/solution.py
@@ -304,8 +304,14 @@
     )(own, lhat, *early, *came)
 
 
-def masked_kernel(n, q, planes, rows, h, count, listed, *refs):
-    parts, off = refs[:count], refs[-1]
+def masked_kernel(n, q, planes, rows, h, count, terms, listed, *refs):
+    parts, off = refs[:count], refs[-2] if terms else refs[-1]
+    if terms:
+        pivot, *others = refs[count : count + terms]
+        total = pivot[0]
+        for y in others:
+            total = total + y[...].astype(jnp.float32)
+        refs[-1][0] = total
     p = lax.axis_index("prow")
     c = lax.axis_index("pcol")
     takes = chosen_planes(n, q, planes)
@@ -321,21 +327,25 @@
         off[:, b * BLOCK : (b + 1) * BLOCK] = -(x[:, b * BLOCK : (b + 1) * BLOCK] * keep)
 
 
-def masked(n, q, planes, rows, h, listed, parts, before):
+def masked(n, q, planes, rows, h, listed, parts, before, terms=()):
     tall, width = parts[0].shape
     step = min(tall, 1024)
     count = tall // step
     return pl.pallas_call(
-        functools.partial(masked_kernel, n, q, planes, rows, h, len(parts)),
+        functools.partial(masked_kernel, n, q, planes, rows, h, len(parts), len(terms)),
         grid=(count,),
-        out_shape=jax.ShapeDtypeStruct((width, rows), jnp.float32),
-        in_specs=[whole(SMEM)] + [pl.BlockSpec((step, width), lambda i: (i, 0))] * len(parts) + [whole(pl.ANY)] * len(before),
-        out_specs=pl.BlockSpec((width, step), lambda i: (0, h * count + i)),
-        input_output_aliases={1 + len(parts): 0} if before else {},
+        out_shape=[jax.ShapeDtypeStruct((width, rows), jnp.float32)]
+        + [jax.ShapeDtypeStruct(x.shape, jnp.float32) for x in terms[:1]],
+        in_specs=[whole(SMEM)]
+        + [pl.BlockSpec((step, width), lambda i: (i, 0))] * len(parts)
+        + [whole(VMEM)] * len(terms)
+        + [whole(pl.ANY)] * len(before),
+        out_specs=[pl.BlockSpec((width, step), lambda i: (0, h * count + i))] + [whole(VMEM)] * len(terms[:1]),
+        input_output_aliases={1 + len(parts) + len(terms): 0} if before else {},
         compiler_params=pltpu.CompilerParams(vmem_limit_bytes=LIMIT),
         cost_estimate=pl.CostEstimate(flops=4 * tall * width, bytes_accessed=10 * tall * width, transcendentals=0),
         name="masked",
-    )(listed, *parts, *before)
+    )(listed, *parts, *terms, *before)
 
 
 def per_device(n, ncol, l_panel, inverse_tile, unit_inverse, pivot_inverse, listed):
@@ -431,13 +441,12 @@
     planes = [x[1] for x in came[0] if x is not None]
     part = ahead(chunk[0], lhat, jnp.float32)
     part, travel = gathered(n, q, planes, part, lhat[0], early, parts[0][1:])
+    terms = [pivot_inverse, part] + [over_rows(travel, a) for a in range(1, n)]
     off = []
     for h in range(HALVES):
-        off = [masked(n, q, planes, inverse_tile.shape[0], h, listed, parts[h], off)]
-    total = part
-    for a in range(1, n):
-        total = total + over_rows(travel, a).astype(jnp.float32)
-    return off[0], pivot_inverse + total[None]
+        last = h == HALVES - 1
+        off = masked(n, q, planes, inverse_tile.shape[0], h, listed, parts[h], off[:1], terms if last else ())
+    return off[0], off[1]
 
 
 def groups(n):

time: 96.5 us -> 97.4 us (level)
  waiting for transfers between devices: 21.8 us -> 23.4 us
    ppermute x36, waiting for transfers between devices: 21.8 us -> 23.4 us  [swap(): return lax.ppermute(x, AXES, pairs)]
  transfers between devices with their start and end apart: 36 -> 36, of which waited for: 10 -> 11; matrix products, arithmetic and copies ran while one was open for 0% -> 0% of each run, Pallas kernels for 18% -> 16%
where the time goes in v6:
time: 97.4 us; the launch traced here: 97.3 us
  starting transfers between devices  53.7 us (55%)
  waiting for transfers between devices  23.4 us (24%)
  Pallas kernels  17 us (17%)
  local copies, waits for them, and re-layouts  2.2 us (2%)
    ppermute x36, starting transfers between devices, swap(): return lax.ppermute(x, AXES, pairs)  53.7 us
    ppermute x36, waiting for transfers between devices, swap(): return lax.ppermute(x, AXES, pairs)  23.4 us
    pallas_call x3, Pallas kernels, partial_product(): pl.pallas_call(functools.partial(partial_kernel, n, q, halves, min(tall,...  7.1 us
    pallas_call x2, Pallas kernels, masked(): pl.pallas_call(functools.partial(masked_kernel, n, q, planes, rows, h, le...  3.23 us
    pallas_call x3, Pallas kernels, piece_product(): pl.pallas_call(functools.partial(piece_kernel, n, q, which, base, min(tal...  2.75 us
    unnamed x6, local copies, waits for them, and re-layouts  2.2 us
  transfers between devices with their start and end apart: 36, of which 11 were waited for; matrix products, arithmetic and copies ran while one was open for 0% of the time, Pallas kernels for 16%

profile of v6, /device:TPU:0, one launch (start us, length us, event | category | flops | bytes accessed | tf_op | source)
XLA Modules:
  0.0 97.3 jit_solution(14493604049959922732)
XLA Ops:
  0.6 0.6 collective-permute-start.6
  1.2 1.9 %normalize.1 = (bf16[512,128]{1,0:T(8,128)(2,1)S(1)}, bf16[512,128]{1,0:T(8,128)(2,1)S(1)}, bf16[512,128]{1,0:T(8,128)(2,1)S(1)}, bf16[512,128]{1,0:T(8,128)(2,1...) custom-call(s32[8,64]{1,0:T(8,128)} %listed.5, bf16[2048,128]{1,0:T(8,128)(2,1)} %panel.1, ...), custom_call_target="tpu_custom_call" | custom-call | flops 67108864 | bytes 1572864 | tf_op jit(solution)/shard_map/normalize/pallas_call | solution.py:62
  3.1 2.6 %collective-permute-start = (bf16[512,128]{1,0:T(8,128)(2,1)S(1)}, bf16[512,128]{1,0:T(8,128)(2,1)S(1)}, u32[]{:S(2)}, u32[]{:S(2)}) collective-permute-start(bf16[512,128]{1,0:T(8,128)(2,1)S(1)} %get-tuple-element.21), channel_id=1, source_target_pairs={{0,8},{1,9},{2,10},{3,11},{4,12},{5,13},{6,14},{7,15},{8,0},{9,1},... | collective-permute-start | bytes 393224 | tf_op jit(solution)/shard_map/ppermute | solution.py:368
  5.6 1.5 %collective-permute-start.1 = (bf16[512,128]{1,0:T(8,128)(2,1)S(1)}, bf16[512,128]{1,0:T(8,128)(2,1)S(1)}, u32[]{:S(2)}, u32[]{:S(2)}) collective-permute-start(bf16[512,128]{1,0:T(8,128)(2,1)S(1)} %get-tuple-element.22), channel_id=1, source_target_pairs={{0,16},{1,17},{2,18},{3,19},{4,20},{5,21},{6,22},{7,23},{8,24},{9,... | collective-permute-start | bytes 393224 | tf_op jit(solution)/shard_map/ppermute | solution.py:368
  7.2 2.8 %collective-permute-done.refs_1_ = bf16[512,128]{1,0:T(8,128)(2,1)S(1)} collective-permute-done((bf16[512,128]{1,0:T(8,128)(2,1)S(1)}, bf16[512,128]{1,0:T(8,128)(2,1)S(1)}, u32[]{:S(2)}, u32[]{:S(2)}) %collective-permute-start) | collective-permute-done | bytes 131104 | tf_op jit(solution)/shard_map/ppermute | solution.py:368
  9.9 4.1 %collective-permute-done.1.refs_2_ = bf16[512,128]{1,0:T(8,128)(2,1)S(1)} collective-permute-done((bf16[512,128]{1,0:T(8,128)(2,1)S(1)}, bf16[512,128]{1,0:T(8,128)(2,1)S(1)}, u32[]{:S(2)}, u32[]{:S(2)}) %collective-permute-start.1) | collective-permute-done | bytes 131104 | tf_op jit(solution)/shard_map/ppermute | solution.py:368
  14.1 3.7 %collective-permute-start.15 = (bf16[512,128]{1,0:T(8,128)(2,1)S(1)}, bf16[512,128]{1,0:T(8,128)(2,1)S(1)}, u32[]{:S(2)}, u32[]{:S(2)}) collective-permute-start(bf16[512,128]{1,0:T(8,128)(2,1)S(1)} %get-tuple-element.30), channel_id=1, source_target_pairs={{0,6},{1,7},{2,4},{3,5},{4,2},{5,3},{6,0},{7,1},{8,14},{9,15},{10,... | collective-permute-start | bytes 393224 | tf_op jit(solution)/shard_map/ppermute | solution.py:368
  17.7 4.4 %collective-permute-done.15 = bf16[512,128]{1,0:T(8,128)(2,1)S(1)} collective-permute-done((bf16[512,128]{1,0:T(8,128)(2,1)S(1)}, bf16[512,128]{1,0:T(8,128)(2,1)S(1)}, u32[]{:S(2)}, u32[]{:S(2)}) %collective-permute-start.15) | collective-permute-done | bytes 131104 | tf_op jit(solution)/shard_map/ppermute | solution.py:368
  22.2 1.4 %collective-permute-start.17 = (bf16[1,512,128]{2,1,0:T(8,128)(2,1)S(1)}, bf16[1,512,128]{2,1,0:T(8,128)(2,1)S(1)}, u32[]{:S(2)}, u32[]{:S(2)}) collective-permute-start(bf16[1,512,128]{2,1,0:T(8,128)(2,1)S(1)} %bitcast.16), channel_id=1, source_target_pairs={{0,8},{1,9},{2,10},{3,11},{4,12},{5,13},{6,14},{7,15},{8,0},{9,1},... | collective-permute-start | bytes 393224 | tf_op jit(solution)/shard_map/ppermute | solution.py:368
  23.6 0.8 collective-permute-start.18
  24.4 1.3 %collective-permute-start.16 = (bf16[1,512,128]{2,1,0:T(8,128)(2,1)S(1)}, bf16[1,512,128]{2,1,0:T(8,128)(2,1)S(1)}, u32[]{:S(2)}, u32[]{:S(2)}) collective-permute-start(bf16[1,512,128]{2,1,0:T(8,128)(2,1)S(1)} %bitcast.18), channel_id=1, source_target_pairs={{0,24},{1,25},{2,26},{3,27},{4,28},{5,29},{6,30},{7,31},{8,16},{9,... | collective-permute-start | bytes 393224 | tf_op jit(solution)/shard_map/ppermute | solution.py:368
  25.7 2.2 %copy-done = bf16[2048,1024]{1,0:T(8,128)(2,1)S(1)} copy-done((bf16[2048,1024]{1,0:T(8,128)(2,1)S(1)}, bf16[2048,1024]{1,0:T(8,128)(2,1)}, u32[]{:S(2)}) %copy-start) | copy-done | bytes 4194328
  27.8 0.3 load.1.refs_4_.refs_3_.refs_1_
  28.1 0.1 collective-permute-done.11
  28.2 1.6 %collective-permute-start.12 = (bf16[1,512,128]{2,1,0:T(8,128)(2,1)S(1)}, bf16[1,512,128]{2,1,0:T(8,128)(2,1)S(1)}, u32[]{:S(2)}, u32[]{:S(2)}) collective-permute-start(bf16[1,512,128]{2,1,0:T(8,128)(2,1)S(1)} %bitcast.12), channel_id=1, source_target_pairs={{0,8},{1,9},{2,10},{3,11},{4,12},{5,13},{6,14},{7,15},{8,0},{9,1},... | collective-permute-start | bytes 393224 | tf_op jit(solution)/shard_map/ppermute | solution.py:368
  29.8 0.6 collective-permute-start.13
  30.4 1.8 %piece_product.3.refs_3_ = f32[2048,128]{1,0:T(8,128)S(1)} custom-call(bf16[1,512,128]{2,1,0:T(8,128)(2,1)S(1)} %bitcast.19, bf16[1,512,128]{2,1,0:T(8,128)(2,1)S(1)} %collective-permute-done.17.refs_1_, bf16[1,512,128]{2,1,0:T(8,128)(2,1)S(1)} %collective-permute-done.18.refs_2_, bf16[2048,1024]{1,0:T(8,128)(2,1)S(1)} %load.1.refs_4_.refs_3_.refs_1_, ...), custom_call_target="tpu_custom_call" | custom-call | flops 805306368 | bytes 6291456 | tf_op jit(solution)/shard_map/piece_product/pallas_call | solution.py:193
  32.3 0.5 piece_product.5.x
  32.7 4.8 %collective-permute-start.28 = (bf16[1024,128]{1,0:T(8,128)(2,1)S(1)}, bf16[1024,128]{1,0:T(8,128)(2,1)S(1)}, u32[]{:S(2)}, u32[]{:S(2)}) collective-permute-start(bf16[1024,128]{1,0:T(8,128)(2,1)S(1)} %piece_product.5.x), channel_id=1, source_target_pairs={{0,2},{1,3},{2,0},{3,1},{4,6},{5,7},{6,4},{7,5},{8,10},{9,11},{10,... | collective-permute-start | bytes 786440 | tf_op jit(solution)/shard_map/ppermute | solution.py:368
  37.6 1.3 %collective-permute-start.14 = (bf16[1,512,128]{2,1,0:T(8,128)(2,1)S(1)}, bf16[1,512,128]{2,1,0:T(8,128)(2,1)S(1)}, u32[]{:S(2)}, u32[]{:S(2)}) collective-permute-start(bf16[1,512,128]{2,1,0:T(8,128)(2,1)S(1)} %bitcast.14), channel_id=1, source_target_pairs={{0,24},{1,25},{2,26},{3,27},{4,28},{5,29},{6,30},{7,31},{8,16},{9,... | collective-permute-start | bytes 393224 | tf_op jit(solution)/shard_map/ppermute | solution.py:368
  38.8 0.5 piece_product.4.x
  39.3 0.1 collective-permute-start.19
  39.5 1.6 %collective-permute-start.3 = (bf16[1,512,128]{2,1,0:T(8,128)(2,1)S(1)}, bf16[1,512,128]{2,1,0:T(8,128)(2,1)S(1)}, u32[]{:S(2)}, u32[]{:S(2)}) collective-permute-start(bf16[1,512,128]{2,1,0:T(8,128)(2,1)S(1)} %bitcast.4), channel_id=1, source_target_pairs={{0,8},{1,9},{2,10},{3,11},{4,12},{5,13},{6,14},{7,15},{8,0},{9,1},... | collective-permute-start | bytes 393224 | tf_op jit(solution)/shard_map/ppermute | solution.py:368
  41.1 1.9 %collective-permute-start.7 = (bf16[512,128]{1,0:T(8,128)(2,1)S(1)}, bf16[512,128]{1,0:T(8,128)(2,1)S(1)}, u32[]{:S(2)}, u32[]{:S(2)}) collective-permute-start(bf16[512,128]{1,0:T(8,128)(2,1)S(1)} %get-tuple-element.26), channel_id=1, source_target_pairs={{0,2},{1,3},{2,0},{3,1},{4,6},{5,7},{6,4},{7,5},{8,10},{9,11},{10,... | collective-permute-start | bytes 393224 | tf_op jit(solution)/shard_map/ppermute | solution.py:368
  43.0 0.5 collective-permute-done.14.refs_3_
  43.5 1.4 %collective-permute-start.4 = (bf16[1,512,128]{2,1,0:T(8,128)(2,1)S(1)}, bf16[1,512,128]{2,1,0:T(8,128)(2,1)S(1)}, u32[]{:S(2)}, u32[]{:S(2)}) collective-permute-start(bf16[1,512,128]{2,1,0:T(8,128)(2,1)S(1)} %bitcast.5), channel_id=1, source_target_pairs={{0,16},{1,17},{2,18},{3,19},{4,20},{5,21},{6,22},{7,23},{8,24},{9,... | collective-permute-start | bytes 393224 | tf_op jit(solution)/shard_map/ppermute | solution.py:368
  45.0 2.4 %partial_product.5 = (bf16[1024,128]{1,0:T(8,128)(2,1)S(1)}, bf16[1024,128]{1,0:T(8,128)(2,1)S(1)}) custom-call(bf16[1,512,128]{2,1,0:T(8,128)(2,1)S(1)} %bitcast.15, bf16[1,512,128]{2,1,0:T(8,128)(2,1)S(1)} %collective-permute-done.12.refs_1_, bf16[1,512,128]{2,1,0:T(8,128)(2,1)S(1)} %collective-permute-done.13.refs_2_, ...), custom_call_target="tpu_custom_call" | custom-call | flops 1073741824 | bytes 8388608 | tf_op jit(solution)/shard_map/partial_product/pallas_call | solution.py:152
  47.3 0.1 collective-permute-start.31
  47.5 4.9 %collective-permute-done.7 = bf16[512,128]{1,0:T(8,128)(2,1)S(1)} collective-permute-done((bf16[512,128]{1,0:T(8,128)(2,1)S(1)}, bf16[512,128]{1,0:T(8,128)(2,1)S(1)}, u32[]{:S(2)}, u32[]{:S(2)}) %collective-permute-start.7) | collective-permute-done | bytes 131104 | tf_op jit(solution)/shard_map/ppermute | solution.py:368
  52.4 1.5 %collective-permute-start.8 = (bf16[1,512,128]{2,1,0:T(8,128)(2,1)S(1)}, bf16[1,512,128]{2,1,0:T(8,128)(2,1)S(1)}, u32[]{:S(2)}, u32[]{:S(2)}) collective-permute-start(bf16[1,512,128]{2,1,0:T(8,128)(2,1)S(1)} %bitcast.8), channel_id=1, source_target_pairs={{0,8},{1,9},{2,10},{3,11},{4,12},{5,13},{6,14},{7,15},{8,0},{9,1},... | collective-permute-start | bytes 393224 | tf_op jit(solution)/shard_map/ppermute | solution.py:368
  53.9 0.6 collective-permute-start.9
  54.5 0.1 add.9
  54.5 0.1 collective-permute-start.29
  54.6 1.5 %collective-permute-start.10 = (bf16[1,512,128]{2,1,0:T(8,128)(2,1)S(1)}, bf16[1,512,128]{2,1,0:T(8,128)(2,1)S(1)}, u32[]{:S(2)}, u32[]{:S(2)}) collective-permute-start(bf16[1,512,128]{2,1,0:T(8,128)(2,1)S(1)} %bitcast.10), channel_id=1, source_target_pairs={{0,24},{1,25},{2,26},{3,27},{4,28},{5,29},{6,30},{7,31},{8,16},{9,... | collective-permute-start | bytes 393224 | tf_op jit(solution)/shard_map/ppermute | solution.py:368
  56.1 0.1 add.6
  56.2 1.2 %collective-permute-done.8.refs_1_ = bf16[1,512,128]{2,1,0:T(8,128)(2,1)S(1)} collective-permute-done((bf16[1,512,128]{2,1,0:T(8,128)(2,1)S(1)}, bf16[1,512,128]{2,1,0:T(8,128)(2,1)S(1)}, u32[]{:S(2)}, u32[]{:S(2)}) %collective-permute-start.8) | collective-permute-done | bytes 131104 | tf_op jit(solution)/shard_map/ppermute | solution.py:368
  57.4 1.6 %collective-permute-start.22 = (bf16[1024,128]{1,0:T(8,128)(2,1)S(1)}, bf16[1024,128]{1,0:T(8,128)(2,1)S(1)}, u32[]{:S(2)}, u32[]{:S(2)}) collective-permute-start(bf16[1024,128]{1,0:T(8,128)(2,1)S(1)} %get-tuple-element.29.x), channel_id=1, source_target_pairs={{0,2},{1,3},{2,0},{3,1},{4,6},{5,7},{6,4},{7,5},{8,10},{9,11},{10,... | collective-permute-start | bytes 786440 | tf_op jit(solution)/shard_map/ppermute | solution.py:368
  59.0 2.7 %collective-permute-done.9.refs_2_ = bf16[1,512,128]{2,1,0:T(8,128)(2,1)S(1)} collective-permute-done((bf16[1,512,128]{2,1,0:T(8,128)(2,1)S(1)}, bf16[1,512,128]{2,1,0:T(8,128)(2,1)S(1)}, u32[]{:S(2)}, u32[]{:S(2)}) %collective-permute-start.9) | collective-permute-done | bytes 131104 | tf_op jit(solution)/shard_map/ppermute | solution.py:368
  61.7 0.5 collective-permute-start.26
  62.2 1.7 %collective-permute-start.24 = (bf16[1024,128]{1,0:T(8,128)(2,1)S(1)}, bf16[1024,128]{1,0:T(8,128)(2,1)S(1)}, u32[]{:S(2)}, u32[]{:S(2)}) collective-permute-start(bf16[1024,128]{1,0:T(8,128)(2,1)S(1)} %get-tuple-element.33.refs_3_), channel_id=1, source_target_pairs={{0,2},{1,3},{2,0},{3,1},{4,6},{5,7},{6,4},{7,5},{8,10},{9,11},{10,... | collective-permute-start | bytes 786440 | tf_op jit(solution)/shard_map/ppermute | solution.py:368
  63.8 1.5 %collective-permute-start.5 = (bf16[1,512,128]{2,1,0:T(8,128)(2,1)S(1)}, bf16[1,512,128]{2,1,0:T(8,128)(2,1)S(1)}, u32[]{:S(2)}, u32[]{:S(2)}) collective-permute-start(bf16[1,512,128]{2,1,0:T(8,128)(2,1)S(1)} %bitcast.6), channel_id=1, source_target_pairs={{0,24},{1,25},{2,26},{3,27},{4,28},{5,29},{6,30},{7,31},{8,16},{9,... | collective-permute-start | bytes 393224 | tf_op jit(solution)/shard_map/ppermute | solution.py:368
  65.4 2.4 %partial_product.4 = (bf16[1024,128]{1,0:T(8,128)(2,1)S(1)}, bf16[1024,128]{1,0:T(8,128)(2,1)S(1)}) custom-call(bf16[1,512,128]{2,1,0:T(8,128)(2,1)S(1)} %bitcast.11, bf16[1,512,128]{2,1,0:T(8,128)(2,1)S(1)} %collective-permute-done.8.refs_1_, bf16[1,512,128]{2,1,0:T(8,128)(2,1)S(1)} %collective-permute-done.9.refs_2_, ...), custom_call_target="tpu_custom_call" | custom-call | flops 1073741824 | bytes 8388608 | tf_op jit(solution)/shard_map/partial_product/pallas_call | solution.py:152
  67.7 0.1 add.11
  67.8 0.1 add.10
  67.9 0.1 collective-permute-start.32
  68.0 2.1 %collective-permute-start.30 = (bf16[1024,128]{1,0:T(8,128)(2,1)S(1)}, bf16[1024,128]{1,0:T(8,128)(2,1)S(1)}, u32[]{:S(2)}, u32[]{:S(2)}) collective-permute-start(bf16[1024,128]{1,0:T(8,128)(2,1)S(1)} %add.10), channel_id=1, source_target_pairs={{0,2},{1,3},{2,0},{3,1},{4,6},{5,7},{6,4},{7,5},{8,10},{9,11},{10,... | collective-permute-start | bytes 786440 | tf_op jit(solution)/shard_map/ppermute | solution.py:368
  70.2 0.1 add.7.refs_0_
  70.3 0.1 collective-permute-start.23
  70.4 4.8 %collective-permute-start.21 = (bf16[1024,128]{1,0:T(8,128)(2,1)S(1)}, bf16[1024,128]{1,0:T(8,128)(2,1)S(1)}, u32[]{:S(2)}, u32[]{:S(2)}) collective-permute-start(bf16[1024,128]{1,0:T(8,128)(2,1)S(1)} %add.7.refs_0_), channel_id=1, source_target_pairs={{0,2},{1,3},{2,0},{3,1},{4,6},{5,7},{6,4},{7,5},{8,10},{9,11},{10,... | collective-permute-start | bytes 786440 | tf_op jit(solution)/shard_map/ppermute | solution.py:368
  75.1 0.3 ahead.5
  75.4 0.1 collective-permute-start.27
  75.5 0.3 ahead.4
  75.8 0.9 collective-permute-done.27.refs_1_
  76.7 8.8 %collective-permute-start.25 = (bf16[128,128]{1,0:T(8,128)(2,1)S(1)}, bf16[128,128]{1,0:T(8,128)(2,1)S(1)}, u32[]{:S(2)}, u32[]{:S(2)}) collective-permute-start(bf16[128,128]{1,0:T(8,128)(2,1)S(1)} %ahead.4), channel_id=1, source_target_pairs={{0,2},{1,3},{2,0},{3,1},{4,6},{5,7},{6,4},{7,5},{8,10},{9,11},{10,... | collective-permute-start | bytes 98312 | tf_op jit(solution)/shard_map/ppermute | solution.py:368
  85.5 2.4 %partial_product.3 = (bf16[1024,128]{1,0:T(8,128)(2,1)S(1)}, bf16[1024,128]{1,0:T(8,128)(2,1)S(1)}) custom-call(bf16[1,512,128]{2,1,0:T(8,128)(2,1)S(1)} %bitcast.7, bf16[1,512,128]{2,1,0:T(8,128)(2,1)S(1)} %collective-permute-done.3.refs_1_, bf16[1,512,128]{2,1,0:T(8,128)(2,1)S(1)} %collective-permute-done.4.refs_2_, ...), custom_call_target="tpu_custom_call" | custom-call | flops 1073741824 | bytes 8388608 | tf_op jit(solution)/shard_map/partial_product/pallas_call | solution.py:152
  87.9 0.4 ahead.3.own
  88.3 0.4 gathered.1
  88.7 1.6 %collective-permute-start.33 = (bf16[128,128]{1,0:T(8,128)(2,1)S(1)}, bf16[128,128]{1,0:T(8,128)(2,1)S(1)}, u32[]{:S(2)}, u32[]{:S(2)}) collective-permute-start(bf16[128,128]{1,0:T(8,128)(2,1)S(1)} %get-tuple-element.37), channel_id=1, source_target_pairs={{0,8},{1,9},{2,10},{3,11},{4,12},{5,13},{6,14},{7,15},{8,0},{9,1},... | collective-permute-start | bytes 98312 | tf_op jit(solution)/shard_map/ppermute | solution.py:368
  90.2 0.6 collective-permute-start.34
  90.8 1.4 %collective-permute-start.35 = (bf16[128,128]{1,0:T(8,128)(2,1)S(1)}, bf16[128,128]{1,0:T(8,128)(2,1)S(1)}, u32[]{:S(2)}, u32[]{:S(2)}) collective-permute-start(bf16[128,128]{1,0:T(8,128)(2,1)S(1)} %get-tuple-element.37), channel_id=1, source_target_pairs={{0,24},{1,25},{2,26},{3,27},{4,28},{5,29},{6,30},{7,31},{8,16},{9,... | collective-permute-start | bytes 98312 | tf_op jit(solution)/shard_map/ppermute | solution.py:368
  92.2 1.6 %masked.2.refs_8_ = f32[128,2048]{1,0:T(8,128)} custom-call(s32[8,64]{1,0:T(8,128)S(1)} %copy-done.2, bf16[1024,128]{1,0:T(8,128)(2,1)S(1)} %get-tuple-element.31.refs_0_, bf16[1024,128]{1,0:T(8,128)(2,1)S(1)} %collective-permute-done.30.refs_2_.refs_1_, bf16[1024,128]{1,0:T(8,128)(2,1)S(1)} %collective-permute-done.32.refs_3_.refs_2_), custom_call_target="tpu_custom_call" | custom-call | flops 524288 | bytes 1310720 | tf_op jit(solution)/shard_map/masked/pallas_call | solution.py:334
  93.9 0.3 collective-permute-done.34.refs_6_
  94.2 1.5 %collective-permute-done.35.refs_7_ = bf16[128,128]{1,0:T(8,128)(2,1)S(1)} collective-permute-done((bf16[128,128]{1,0:T(8,128)(2,1)S(1)}, bf16[128,128]{1,0:T(8,128)(2,1)S(1)}, u32[]{:S(2)}, u32[]{:S(2)}) %collective-permute-start.35) | collective-permute-done | bytes 32800 | tf_op jit(solution)/shard_map/ppermute | solution.py:368
  95.6 1.6 %masked.3 = (f32[128,2048]{1,0:T(8,128)}, f32[1,128,128]{2,1,0:T(8,128)}) custom-call(s32[8,64]{1,0:T(8,128)S(1)} %copy-done.2, bf16[1024,128]{1,0:T(8,128)(2,1)S(1)} %get-tuple-element.25.refs_1_.refs_0_, bf16[1024,128]{1,0:T(8,128)(2,1)S(1)} %collective-permute-done.21.refs_1_, ...), custom_call_target="tpu_custom_call", output_to_operand_aliasing={{0}: (9, {})} | custom-call | flops 524288 | bytes 1310720 | tf_op jit(solution)/shard_map/masked/pallas_call | solution.py:334
  (35 shorter events, 0.2 us)
Async XLA Ops:
  0.6 29.8 %collective-permute-start.6 = (bf16[2048,1024]{1,0:T(8,128)(2,1)}, bf16[2048,1024]{1,0:T(8,128)(2,1)S(1)}, u32[]{:S(2)}, u32[]{:S(2)}) collective-permute-start(bf16[2048,1024]{1,0:T(8,128)(2,1)} %tile.1), channel_id=1, source_target_pairs={{0,1},{1,0},{2,3},{3,2},{4,5},{5,4},{6,7},{7,6},{8,9},{9,8},{10,11... | collective-permute-start | bytes 12582920 | tf_op jit(solution)/shard_map/ppermute | solution.py:368
  3.1 6.9 %collective-permute-start = (bf16[512,128]{1,0:T(8,128)(2,1)S(1)}, bf16[512,128]{1,0:T(8,128)(2,1)S(1)}, u32[]{:S(2)}, u32[]{:S(2)}) collective-permute-start(bf16[512,128]{1,0:T(8,128)(2,1)S(1)} %get-tuple-element.21), channel_id=1, source_target_pairs={{0,8},{1,9},{2,10},{3,11},{4,12},{5,13},{6,14},{7,15},{8,0},{9,1},... | collective-permute-start | bytes 393224 | tf_op jit(solution)/shard_map/ppermute | solution.py:368
  5.6 8.4 %collective-permute-start.1 = (bf16[512,128]{1,0:T(8,128)(2,1)S(1)}, bf16[512,128]{1,0:T(8,128)(2,1)S(1)}, u32[]{:S(2)}, u32[]{:S(2)}) collective-permute-start(bf16[512,128]{1,0:T(8,128)(2,1)S(1)} %get-tuple-element.22), channel_id=1, source_target_pairs={{0,16},{1,17},{2,18},{3,19},{4,20},{5,21},{6,22},{7,23},{8,24},{9,... | collective-permute-start | bytes 393224 | tf_op jit(solution)/shard_map/ppermute | solution.py:368
  7.1 6.9 %collective-permute-start.2 = (bf16[512,128]{1,0:T(8,128)(2,1)S(1)}, bf16[512,128]{1,0:T(8,128)(2,1)S(1)}, u32[]{:S(2)}, u32[]{:S(2)}) collective-permute-start(bf16[512,128]{1,0:T(8,128)(2,1)S(1)} %get-tuple-element.23), channel_id=1, source_target_pairs={{0,24},{1,25},{2,26},{3,27},{4,28},{5,29},{6,30},{7,31},{8,16},{9,... | collective-permute-start | bytes 393224 | tf_op jit(solution)/shard_map/ppermute | solution.py:368
  14.1 8.1 %collective-permute-start.15 = (bf16[512,128]{1,0:T(8,128)(2,1)S(1)}, bf16[512,128]{1,0:T(8,128)(2,1)S(1)}, u32[]{:S(2)}, u32[]{:S(2)}) collective-permute-start(bf16[512,128]{1,0:T(8,128)(2,1)S(1)} %get-tuple-element.30), channel_id=1, source_target_pairs={{0,6},{1,7},{2,4},{3,5},{4,2},{5,3},{6,0},{7,1},{8,14},{9,15},{10,... | collective-permute-start | bytes 393224 | tf_op jit(solution)/shard_map/ppermute | solution.py:368
  17.7 10.5 %collective-permute-start.11 = (bf16[512,128]{1,0:T(8,128)(2,1)S(1)}, bf16[512,128]{1,0:T(8,128)(2,1)S(1)}, u32[]{:S(2)}, u32[]{:S(2)}) collective-permute-start(bf16[512,128]{1,0:T(8,128)(2,1)S(1)} %get-tuple-element.28), channel_id=1, source_target_pairs={{0,4},{1,5},{2,6},{3,7},{4,0},{5,1},{6,2},{7,3},{8,12},{9,13},{10,... | collective-permute-start | bytes 393224 | tf_op jit(solution)/shard_map/ppermute | solution.py:368
  22.2 7.7 %collective-permute-start.17 = (bf16[1,512,128]{2,1,0:T(8,128)(2,1)S(1)}, bf16[1,512,128]{2,1,0:T(8,128)(2,1)S(1)}, u32[]{:S(2)}, u32[]{:S(2)}) collective-permute-start(bf16[1,512,128]{2,1,0:T(8,128)(2,1)S(1)} %bitcast.16), channel_id=1, source_target_pairs={{0,8},{1,9},{2,10},{3,11},{4,12},{5,13},{6,14},{7,15},{8,0},{9,1},... | collective-permute-start | bytes 393224 | tf_op jit(solution)/shard_map/ppermute | solution.py:368
  23.6 6.8 %collective-permute-start.18 = (bf16[1,512,128]{2,1,0:T(8,128)(2,1)S(1)}, bf16[1,512,128]{2,1,0:T(8,128)(2,1)S(1)}, u32[]{:S(2)}, u32[]{:S(2)}) collective-permute-start(bf16[1,512,128]{2,1,0:T(8,128)(2,1)S(1)} %bitcast.17), channel_id=1, source_target_pairs={{0,16},{1,17},{2,18},{3,19},{4,20},{5,21},{6,22},{7,23},{8,24},{9,... | collective-permute-start | bytes 393224 | tf_op jit(solution)/shard_map/ppermute | solution.py:368
  24.4 7.9 %collective-permute-start.16 = (bf16[1,512,128]{2,1,0:T(8,128)(2,1)S(1)}, bf16[1,512,128]{2,1,0:T(8,128)(2,1)S(1)}, u32[]{:S(2)}, u32[]{:S(2)}) collective-permute-start(bf16[1,512,128]{2,1,0:T(8,128)(2,1)S(1)} %bitcast.18), channel_id=1, source_target_pairs={{0,24},{1,25},{2,26},{3,27},{4,28},{5,29},{6,30},{7,31},{8,16},{9,... | collective-permute-start | bytes 393224 | tf_op jit(solution)/shard_map/ppermute | solution.py:368
  25.7 2.2 %copy-start = (bf16[2048,1024]{1,0:T(8,128)(2,1)S(1)}, bf16[2048,1024]{1,0:T(8,128)(2,1)}, u32[]{:S(2)}) copy-start(bf16[2048,1024]{1,0:T(8,128)(2,1)} %tile.1) | copy-start | bytes 12582916
  28.2 11.2 %collective-permute-start.12 = (bf16[1,512,128]{2,1,0:T(8,128)(2,1)S(1)}, bf16[1,512,128]{2,1,0:T(8,128)(2,1)S(1)}, u32[]{:S(2)}, u32[]{:S(2)}) collective-permute-start(bf16[1,512,128]{2,1,0:T(8,128)(2,1)S(1)} %bitcast.12), channel_id=1, source_target_pairs={{0,8},{1,9},{2,10},{3,11},{4,12},{5,13},{6,14},{7,15},{8,0},{9,1},... | collective-permute-start | bytes 393224 | tf_op jit(solution)/shard_map/ppermute | solution.py:368
  29.8 11.2 %collective-permute-start.13 = (bf16[1,512,128]{2,1,0:T(8,128)(2,1)S(1)}, bf16[1,512,128]{2,1,0:T(8,128)(2,1)S(1)}, u32[]{:S(2)}, u32[]{:S(2)}) collective-permute-start(bf16[1,512,128]{2,1,0:T(8,128)(2,1)S(1)} %bitcast.13), channel_id=1, source_target_pairs={{0,16},{1,17},{2,18},{3,19},{4,20},{5,21},{6,22},{7,23},{8,24},{9,... | collective-permute-start | bytes 393224 | tf_op jit(solution)/shard_map/ppermute | solution.py:368
  32.7 21.1 %collective-permute-start.28 = (bf16[1024,128]{1,0:T(8,128)(2,1)S(1)}, bf16[1024,128]{1,0:T(8,128)(2,1)S(1)}, u32[]{:S(2)}, u32[]{:S(2)}) collective-permute-start(bf16[1024,128]{1,0:T(8,128)(2,1)S(1)} %piece_product.5.x), channel_id=1, source_target_pairs={{0,2},{1,3},{2,0},{3,1},{4,6},{5,7},{6,4},{7,5},{8,10},{9,11},{10,... | collective-permute-start | bytes 786440 | tf_op jit(solution)/shard_map/ppermute | solution.py:368
  37.6 6.0 %collective-permute-start.14 = (bf16[1,512,128]{2,1,0:T(8,128)(2,1)S(1)}, bf16[1,512,128]{2,1,0:T(8,128)(2,1)S(1)}, u32[]{:S(2)}, u32[]{:S(2)}) collective-permute-start(bf16[1,512,128]{2,1,0:T(8,128)(2,1)S(1)} %bitcast.14), channel_id=1, source_target_pairs={{0,24},{1,25},{2,26},{3,27},{4,28},{5,29},{6,30},{7,31},{8,16},{9,... | collective-permute-start | bytes 393224 | tf_op jit(solution)/shard_map/ppermute | solution.py:368
  39.3 15.3 %collective-permute-start.19 = (bf16[1024,128]{1,0:T(8,128)(2,1)S(1)}, bf16[1024,128]{1,0:T(8,128)(2,1)S(1)}, u32[]{:S(2)}, u32[]{:S(2)}) collective-permute-start(bf16[1024,128]{1,0:T(8,128)(2,1)S(1)} %piece_product.4.x), channel_id=1, source_target_pairs={{0,2},{1,3},{2,0},{3,1},{4,6},{5,7},{6,4},{7,5},{8,10},{9,11},{10,... | collective-permute-start | bytes 786440 | tf_op jit(solution)/shard_map/ppermute | solution.py:368
  39.5 7.9 %collective-permute-start.3 = (bf16[1,512,128]{2,1,0:T(8,128)(2,1)S(1)}, bf16[1,512,128]{2,1,0:T(8,128)(2,1)S(1)}, u32[]{:S(2)}, u32[]{:S(2)}) collective-permute-start(bf16[1,512,128]{2,1,0:T(8,128)(2,1)S(1)} %bitcast.4), channel_id=1, source_target_pairs={{0,8},{1,9},{2,10},{3,11},{4,12},{5,13},{6,14},{7,15},{8,0},{9,1},... | collective-permute-start | bytes 393224 | tf_op jit(solution)/shard_map/ppermute | solution.py:368
  41.1 11.3 %collective-permute-start.7 = (bf16[512,128]{1,0:T(8,128)(2,1)S(1)}, bf16[512,128]{1,0:T(8,128)(2,1)S(1)}, u32[]{:S(2)}, u32[]{:S(2)}) collective-permute-start(bf16[512,128]{1,0:T(8,128)(2,1)S(1)} %get-tuple-element.26), channel_id=1, source_target_pairs={{0,2},{1,3},{2,0},{3,1},{4,6},{5,7},{6,4},{7,5},{8,10},{9,11},{10,... | collective-permute-start | bytes 393224 | tf_op jit(solution)/shard_map/ppermute | solution.py:368
  43.5 11.0 %collective-permute-start.4 = (bf16[1,512,128]{2,1,0:T(8,128)(2,1)S(1)}, bf16[1,512,128]{2,1,0:T(8,128)(2,1)S(1)}, u32[]{:S(2)}, u32[]{:S(2)}) collective-permute-start(bf16[1,512,128]{2,1,0:T(8,128)(2,1)S(1)} %bitcast.5), channel_id=1, source_target_pairs={{0,16},{1,17},{2,18},{3,19},{4,20},{5,21},{6,22},{7,23},{8,24},{9,... | collective-permute-start | bytes 393224 | tf_op jit(solution)/shard_map/ppermute | solution.py:368
  47.3 14.8 %collective-permute-start.31 = (bf16[1024,128]{1,0:T(8,128)(2,1)S(1)}, bf16[1024,128]{1,0:T(8,128)(2,1)S(1)}, u32[]{:S(2)}, u32[]{:S(2)}) collective-permute-start(bf16[1024,128]{1,0:T(8,128)(2,1)S(1)} %get-tuple-element.35.x), channel_id=1, source_target_pairs={{0,2},{1,3},{2,0},{3,1},{4,6},{5,7},{6,4},{7,5},{8,10},{9,11},{10,... | collective-permute-start | bytes 786440 | tf_op jit(solution)/shard_map/ppermute | solution.py:368
  52.4 5.0 %collective-permute-start.8 = (bf16[1,512,128]{2,1,0:T(8,128)(2,1)S(1)}, bf16[1,512,128]{2,1,0:T(8,128)(2,1)S(1)}, u32[]{:S(2)}, u32[]{:S(2)}) collective-permute-start(bf16[1,512,128]{2,1,0:T(8,128)(2,1)S(1)} %bitcast.8), channel_id=1, source_target_pairs={{0,8},{1,9},{2,10},{3,11},{4,12},{5,13},{6,14},{7,15},{8,0},{9,1},... | collective-permute-start | bytes 393224 | tf_op jit(solution)/shard_map/ppermute | solution.py:368
  53.9 7.8 %collective-permute-start.9 = (bf16[1,512,128]{2,1,0:T(8,128)(2,1)S(1)}, bf16[1,512,128]{2,1,0:T(8,128)(2,1)S(1)}, u32[]{:S(2)}, u32[]{:S(2)}) collective-permute-start(bf16[1,512,128]{2,1,0:T(8,128)(2,1)S(1)} %bitcast.9), channel_id=1, source_target_pairs={{0,16},{1,17},{2,18},{3,19},{4,20},{5,21},{6,22},{7,23},{8,24},{9,... | collective-permute-start | bytes 393224 | tf_op jit(solution)/shard_map/ppermute | solution.py:368
  54.5 9.3 %collective-permute-start.29 = (bf16[1024,128]{1,0:T(8,128)(2,1)S(1)}, bf16[1024,128]{1,0:T(8,128)(2,1)S(1)}, u32[]{:S(2)}, u32[]{:S(2)}) collective-permute-start(bf16[1024,128]{1,0:T(8,128)(2,1)S(1)} %add.9), channel_id=1, source_target_pairs={{0,1},{1,0},{2,4},{3,5},{4,2},{5,3},{6,7},{7,6},{8,9},{9,8},{10,12... | collective-permute-start | bytes 786440 | tf_op jit(solution)/shard_map/ppermute | solution.py:368
  54.6 7.0 %collective-permute-start.10 = (bf16[1,512,128]{2,1,0:T(8,128)(2,1)S(1)}, bf16[1,512,128]{2,1,0:T(8,128)(2,1)S(1)}, u32[]{:S(2)}, u32[]{:S(2)}) collective-permute-start(bf16[1,512,128]{2,1,0:T(8,128)(2,1)S(1)} %bitcast.10), channel_id=1, source_target_pairs={{0,24},{1,25},{2,26},{3,27},{4,28},{5,29},{6,30},{7,31},{8,16},{9,... | collective-permute-start | bytes 393224 | tf_op jit(solution)/shard_map/ppermute | solution.py:368
  57.4 10.5 %collective-permute-start.22 = (bf16[1024,128]{1,0:T(8,128)(2,1)S(1)}, bf16[1024,128]{1,0:T(8,128)(2,1)S(1)}, u32[]{:S(2)}, u32[]{:S(2)}) collective-permute-start(bf16[1024,128]{1,0:T(8,128)(2,1)S(1)} %get-tuple-element.29.x), channel_id=1, source_target_pairs={{0,2},{1,3},{2,0},{3,1},{4,6},{5,7},{6,4},{7,5},{8,10},{9,11},{10,... | collective-permute-start | bytes 786440 | tf_op jit(solution)/shard_map/ppermute | solution.py:368
  61.7 6.3 %collective-permute-start.20 = (bf16[1024,128]{1,0:T(8,128)(2,1)S(1)}, bf16[1024,128]{1,0:T(8,128)(2,1)S(1)}, u32[]{:S(2)}, u32[]{:S(2)}) collective-permute-start(bf16[1024,128]{1,0:T(8,128)(2,1)S(1)} %add.6), channel_id=1, source_target_pairs={{0,1},{1,0},{2,4},{3,5},{4,2},{5,3},{6,7},{7,6},{8,9},{9,8},{10,12... | collective-permute-start | bytes 786440 | tf_op jit(solution)/shard_map/ppermute | solution.py:368
  61.7 8.7 %collective-permute-start.26 = (bf16[1024,128]{1,0:T(8,128)(2,1)S(1)}, bf16[1024,128]{1,0:T(8,128)(2,1)S(1)}, u32[]{:S(2)}, u32[]{:S(2)}) collective-permute-start(bf16[1024,128]{1,0:T(8,128)(2,1)S(1)} %get-tuple-element.33.refs_3_), channel_id=1, source_target_pairs={{0,1},{1,0},{2,4},{3,5},{4,2},{5,3},{6,7},{7,6},{8,9},{9,8},{10,12... | collective-permute-start | bytes 786440 | tf_op jit(solution)/shard_map/ppermute | solution.py:368
  62.2 13.2 %collective-permute-start.24 = (bf16[1024,128]{1,0:T(8,128)(2,1)S(1)}, bf16[1024,128]{1,0:T(8,128)(2,1)S(1)}, u32[]{:S(2)}, u32[]{:S(2)}) collective-permute-start(bf16[1024,128]{1,0:T(8,128)(2,1)S(1)} %get-tuple-element.33.refs_3_), channel_id=1, source_target_pairs={{0,2},{1,3},{2,0},{3,1},{4,6},{5,7},{6,4},{7,5},{8,10},{9,11},{10,... | collective-permute-start | bytes 786440 | tf_op jit(solution)/shard_map/ppermute | solution.py:368
  63.8 6.4 %collective-permute-start.5 = (bf16[1,512,128]{2,1,0:T(8,128)(2,1)S(1)}, bf16[1,512,128]{2,1,0:T(8,128)(2,1)S(1)}, u32[]{:S(2)}, u32[]{:S(2)}) collective-permute-start(bf16[1,512,128]{2,1,0:T(8,128)(2,1)S(1)} %bitcast.6), channel_id=1, source_target_pairs={{0,24},{1,25},{2,26},{3,27},{4,28},{5,29},{6,30},{7,31},{8,16},{9,... | collective-permute-start | bytes 393224 | tf_op jit(solution)/shard_map/ppermute | solution.py:368
  67.9 20.3 %collective-permute-start.32 = (bf16[1024,128]{1,0:T(8,128)(2,1)S(1)}, bf16[1024,128]{1,0:T(8,128)(2,1)S(1)}, u32[]{:S(2)}, u32[]{:S(2)}) collective-permute-start(bf16[1024,128]{1,0:T(8,128)(2,1)S(1)} %add.11), channel_id=1, source_target_pairs={{0,1},{1,0},{2,4},{3,5},{4,2},{5,3},{6,7},{7,6},{8,9},{9,8},{10,12... | collective-permute-start | bytes 786440 | tf_op jit(solution)/shard_map/ppermute | solution.py:368
  68.0 20.3 %collective-permute-start.30 = (bf16[1024,128]{1,0:T(8,128)(2,1)S(1)}, bf16[1024,128]{1,0:T(8,128)(2,1)S(1)}, u32[]{:S(2)}, u32[]{:S(2)}) collective-permute-start(bf16[1024,128]{1,0:T(8,128)(2,1)S(1)} %add.10), channel_id=1, source_target_pairs={{0,2},{1,3},{2,0},{3,1},{4,6},{5,7},{6,4},{7,5},{8,10},{9,11},{10,... | collective-permute-start | bytes 786440 | tf_op jit(solution)/shard_map/ppermute | solution.py:368
  70.3 23.6 %collective-permute-start.23 = (bf16[1024,128]{1,0:T(8,128)(2,1)S(1)}, bf16[1024,128]{1,0:T(8,128)(2,1)S(1)}, u32[]{:S(2)}, u32[]{:S(2)}) collective-permute-start(bf16[1024,128]{1,0:T(8,128)(2,1)S(1)} %add.8.refs_0_), channel_id=1, source_target_pairs={{0,1},{1,0},{2,4},{3,5},{4,2},{5,3},{6,7},{7,6},{8,9},{9,8},{10,12... | collective-permute-start | bytes 786440 | tf_op jit(solution)/shard_map/ppermute | solution.py:368
  70.4 23.5 %collective-permute-start.21 = (bf16[1024,128]{1,0:T(8,128)(2,1)S(1)}, bf16[1024,128]{1,0:T(8,128)(2,1)S(1)}, u32[]{:S(2)}, u32[]{:S(2)}) collective-permute-start(bf16[1024,128]{1,0:T(8,128)(2,1)S(1)} %add.7.refs_0_), channel_id=1, source_target_pairs={{0,2},{1,3},{2,0},{3,1},{4,6},{5,7},{6,4},{7,5},{8,10},{9,11},{10,... | collective-permute-start | bytes 786440 | tf_op jit(solution)/shard_map/ppermute | solution.py:368
  75.4 1.3 %collective-permute-start.27 = (bf16[128,128]{1,0:T(8,128)(2,1)S(1)}, bf16[128,128]{1,0:T(8,128)(2,1)S(1)}, u32[]{:S(2)}, u32[]{:S(2)}) collective-permute-start(bf16[128,128]{1,0:T(8,128)(2,1)S(1)} %ahead.5), channel_id=1, source_target_pairs={{0,1},{1,0},{2,4},{3,5},{4,2},{5,3},{6,7},{7,6},{8,9},{9,8},{10,12... | collective-permute-start | bytes 98312 | tf_op jit(solution)/shard_map/ppermute | solution.py:368
  75.8 16.5 %copy-start.2 = (s32[8,64]{1,0:T(8,128)S(1)}, s32[8,64]{1,0:T(8,128)}, u32[]{:S(2)}) copy-start(s32[8,64]{1,0:T(8,128)} %listed.5) | copy-start | bytes 6148
  75.8 19.8 %copy-start.1 = (f32[1,128,128]{2,1,0:T(8,128)S(1)}, f32[1,128,128]{2,1,0:T(8,128)}, u32[]{:S(2)}) copy-start(f32[1,128,128]{2,1,0:T(8,128)} %refs_3_.1) | copy-start | bytes 196612
  76.7 11.6 %collective-permute-start.25 = (bf16[128,128]{1,0:T(8,128)(2,1)S(1)}, bf16[128,128]{1,0:T(8,128)(2,1)S(1)}, u32[]{:S(2)}, u32[]{:S(2)}) collective-permute-start(bf16[128,128]{1,0:T(8,128)(2,1)S(1)} %ahead.4), channel_id=1, source_target_pairs={{0,2},{1,3},{2,0},{3,1},{4,6},{5,7},{6,4},{7,5},{8,10},{9,11},{10,... | collective-permute-start | bytes 98312 | tf_op jit(solution)/shard_map/ppermute | solution.py:368
  88.7 5.2 %collective-permute-start.33 = (bf16[128,128]{1,0:T(8,128)(2,1)S(1)}, bf16[128,128]{1,0:T(8,128)(2,1)S(1)}, u32[]{:S(2)}, u32[]{:S(2)}) collective-permute-start(bf16[128,128]{1,0:T(8,128)(2,1)S(1)} %get-tuple-element.37), channel_id=1, source_target_pairs={{0,8},{1,9},{2,10},{3,11},{4,12},{5,13},{6,14},{7,15},{8,0},{9,1},... | collective-permute-start | bytes 98312 | tf_op jit(solution)/shard_map/ppermute | solution.py:368
  90.2 3.9 %collective-permute-start.34 = (bf16[128,128]{1,0:T(8,128)(2,1)S(1)}, bf16[128,128]{1,0:T(8,128)(2,1)S(1)}, u32[]{:S(2)}, u32[]{:S(2)}) collective-permute-start(bf16[128,128]{1,0:T(8,128)(2,1)S(1)} %get-tuple-element.37), channel_id=1, source_target_pairs={{0,16},{1,17},{2,18},{3,19},{4,20},{5,21},{6,22},{7,23},{8,24},{9,... | collective-permute-start | bytes 98312 | tf_op jit(solution)/shard_map/ppermute | solution.py:368
  90.8 4.8 %collective-permute-start.35 = (bf16[128,128]{1,0:T(8,128)(2,1)S(1)}, bf16[128,128]{1,0:T(8,128)(2,1)S(1)}, u32[]{:S(2)}, u32[]{:S(2)}) collective-permute-start(bf16[128,128]{1,0:T(8,128)(2,1)S(1)} %get-tuple-element.37), channel_id=1, source_target_pairs={{0,24},{1,25},{2,26},{3,27},{4,28},{5,29},{6,30},{7,31},{8,16},{9,... | collective-permute-start | bytes 98312 | tf_op jit(solution)/shard_map/ppermute | solution.py:368
